TPU v7x, 512 devices: a whole 4x8x8 slice. The times are simulated.
512 devices in a mesh: seq: 32 (over y, x), head: 16 (over z, core).
Axes of the slice: x: 4, y: 8, z: 8, core: 2. Of those that a mesh axis runs over, the one named last changes fastest.
Arguments:
- queries: bfloat16 [8192, 8192], P('seq', 'head'), may hold values from -1.796875 to 1.796875
- key_rows: bfloat16 [8192, 8192], P('seq', 'head'), may hold values from -1.796875 to 1.796875
- value_rows: bfloat16 [8192, 8192], P('seq', 'head'), may hold values from -6 to 6
- level_table: float32 [64, 7, 64], P(None, None, 'head'), may hold values from 0.25 to 4
- level_index: int32 [8192, 7], P('seq'), may hold values from 0 to 63
- norm_gain: float32 [8192], replicated, may hold values from 0.5 to 1.5
- cotangent: bfloat16 [8192, 8192], P(('seq', 'head')), may hold values from -6 to 6
Outputs:
- normed: bfloat16 [8192, 8192], P(('seq', 'head'))
- grad_query: bfloat16 [8192, 8192], P('seq', 'head')
- grad_key: bfloat16 [8192, 8192], P('seq', 'head')
- grad_value: bfloat16 [8192, 8192], P('seq', 'head')
- grad_table: float32 [64, 7, 64], P(None, None, 'head')
- grad_gain: float32 [8192], replicated
All inputs are finite; a program needn't handle non-finite values.
Results may differ from a plain program's by a relative error of at most 0.014.
Values may be sent and summed in bfloat16 or wider, within the bound.
No kernel may reach another device: no remote copies, remote signals or barrier semaphores. Data moves between devices by JAX's collectives and lax.ppermute only.
A program may use at most 64 MiB of HBM per device.

v0:
```python
import jax
import jax.numpy as jnp
from jax import lax
from jax.sharding import PartitionSpec as P

CH = 128
LEVELS = 7
TABLE = 64


EPSILON = 1e-06
HIGHEST = lax.Precision.HIGHEST


def swapped(value, axis, bit):
    mask = 2**bit
    pairs = [(source, source ^ mask) for source in range(lax.axis_size(axis))]
    return lax.ppermute(value, axis, pairs)


def bit_length_of(values, places):
    result = jnp.zeros_like(values)
    for exponent in range(places):
        result = result + (values >= 1 << exponent).astype(jnp.int32)
    return result


def level_mask(spans):
    row_ids = lax.broadcasted_iota(jnp.int32, (spans, spans), 0)
    col_ids = lax.broadcasted_iota(jnp.int32, (spans, spans), 1)
    lengths = bit_length_of(jnp.bitwise_xor(row_ids, col_ids), 16)
    stacked = [((lengths == 1) & (col_ids < row_ids)).astype(jnp.float32)]
    return jnp.stack(stacked)


def body(queries, key_rows, value_rows, level_table, level_index, norm_gain, cotangent):
    tok_dev = queries.shape[0]
    head_count = level_table.shape[2]
    head_width = queries.shape[1] // head_count
    spans = tok_dev // CH
    local_bits = spans.bit_length() - 1
    seq_bits = lax.axis_size("seq").bit_length() - 1
    cross_count = LEVELS - 1 - local_bits
    shard_id = lax.axis_index("seq")
    query_blocks = queries.reshape(spans, CH, head_count, head_width)
    key_blocks = key_rows.reshape(spans, CH, head_count, head_width)
    value_blocks = value_rows.reshape(spans, CH, head_count, head_width)
    onehot = (level_index[:, :, None] == jnp.arange(TABLE, dtype=jnp.int32)[None, None, :]).astype(
        jnp.float32
    )
    weights = jnp.einsum("tlx,xlh->tlh", onehot, level_table, precision=HIGHEST)
    weights = weights.reshape(spans, CH, LEVELS, head_count)
    span_states = jnp.einsum(
        "icha,ichb->ihab", key_blocks, value_blocks, preferred_element_type=jnp.float32
    )
    masks_local = level_mask(spans)
    intra_states = jnp.einsum("mij,jhab->imhab", masks_local, span_states, precision=HIGHEST)
    shard_total = jnp.sum(span_states, axis=0)
    state_zeros = jnp.zeros((cross_count, head_count, head_width, head_width), jnp.float32)
    shards_in = lax.all_gather(
        shard_total[None].astype(jnp.bfloat16), "seq", axis=0, tiled=True
    ).astype(jnp.float32)
    source = jnp.arange(shards_in.shape[0], dtype=jnp.int32)
    lengths = bit_length_of(jnp.bitwise_xor(source, shard_id), 16)
    slot_of = jnp.minimum(lengths + local_bits, LEVELS - 1) - local_bits - 1
    selector = (slot_of[:, None] == jnp.arange(cross_count, dtype=jnp.int32)[None, :]) & (
        source < shard_id
    )[:, None]
    cross_states = state_zeros + jnp.einsum(
        "sk,shab->khab", selector.astype(jnp.float32), shards_in, precision=HIGHEST
    )
    spread = jnp.broadcast_to(cross_states[None], (spans,) + cross_states.shape)
    level_states = jnp.concatenate([intra_states, spread], axis=1).astype(jnp.bfloat16)
    far_out = jnp.einsum(
        "icha,ilhab->iclhb", query_blocks, level_states, preferred_element_type=jnp.float32
    )
    row_ids = lax.broadcasted_iota(jnp.int32, (CH, CH), 0)
    col_ids = lax.broadcasted_iota(jnp.int32, (CH, CH), 1)
    causal = col_ids <= row_ids
    scores = jnp.einsum(
        "icha,inha->ihcn", query_blocks, key_blocks, preferred_element_type=jnp.float32
    )
    scores = jnp.where(causal, scores, 0.0)
    near_out = jnp.einsum(
        "ihcn,inhb->ichb",
        scores.astype(jnp.bfloat16),
        value_blocks,
        preferred_element_type=jnp.float32,
    )
    level_out = jnp.concatenate([near_out[:, :, None], far_out], axis=2)
    attn = jnp.sum(weights[..., None] * level_out, axis=2).astype(jnp.bfloat16)
    attn_rows = attn.reshape(tok_dev, head_count * head_width)
    token_attn = lax.all_to_all(attn_rows, "head", split_axis=0, concat_axis=1, tiled=True)
    attn_f = token_attn.astype(jnp.float32)
    inv_rms = lax.rsqrt(jnp.mean(attn_f * attn_f, axis=1, keepdims=True) + EPSILON)
    unit_rows = attn_f * inv_rms
    normed = (unit_rows * norm_gain).astype(jnp.bfloat16)
    grad_out = cotangent.astype(jnp.float32)
    scaled = grad_out * norm_gain
    grad_gain = lax.psum(jnp.sum(grad_out * unit_rows, axis=0), ("seq", "head"))
    grad_attn = (
        (scaled - unit_rows * jnp.mean(scaled * unit_rows, axis=1, keepdims=True)) * inv_rms
    ).astype(jnp.bfloat16)
    head_grad = lax.all_to_all(grad_attn, "head", split_axis=1, concat_axis=0, tiled=True)
    grad_blocks = head_grad.reshape(spans, CH, head_count, head_width)
    grad_f = grad_blocks.astype(jnp.float32)
    grad_weight = jnp.sum(level_out * grad_f[:, :, None], axis=4)
    along_values = jnp.einsum(
        "ichb,inhb->ihcn", grad_blocks, value_blocks, preferred_element_type=jnp.float32
    )
    first_weight = jnp.transpose(weights[:, :, 0, :], (0, 2, 1))[..., None]
    grad_scores = jnp.where(causal, along_values * first_weight, 0.0).astype(jnp.bfloat16)
    weighted_scores = jnp.where(causal, scores * first_weight, 0.0).astype(jnp.bfloat16)
    near_dq = jnp.einsum(
        "ihcn,inha->icha", grad_scores, key_blocks, preferred_element_type=jnp.float32
    )
    near_dk = jnp.einsum(
        "ihcn,icha->inha", grad_scores, query_blocks, preferred_element_type=jnp.float32
    )
    near_dv = jnp.einsum(
        "ihcn,ichb->inhb", weighted_scores, grad_blocks, preferred_element_type=jnp.float32
    )
    far_dq = jnp.einsum(
        "ichb,ilhab->iclha", grad_blocks, level_states, preferred_element_type=jnp.float32
    )
    grad_query = near_dq + jnp.sum(weights[:, :, 1:, :, None] * far_dq, axis=2)
    scaled_grad = (weights[:, :, 1:, :, None] * grad_f[:, :, None]).astype(jnp.bfloat16)
    query_grads = jnp.einsum(
        "icha,iclhb->ilhab", query_blocks, scaled_grad, preferred_element_type=jnp.float32
    )
    inner_grad = jnp.einsum(
        "mij,imhab->jhab", masks_local, query_grads[:, :local_bits], precision=HIGHEST
    )
    shard_grads = jnp.sum(query_grads[:, local_bits:], axis=0)
    cross_grad = jnp.zeros((head_count, head_width, head_width), jnp.float32)
    group_grads = shard_grads
    for bit_pos in range(seq_bits):
        partner = swapped(group_grads.astype(jnp.bfloat16), "seq", bit_pos).astype(
            group_grads.dtype
        )
        lower_half = 1.0 - jnp.bitwise_and(jnp.right_shift(shard_id, bit_pos), 1).astype(
            jnp.float32
        )
        level_slot = min(bit_pos, cross_count - 1)
        cross_grad = cross_grad + lower_half * partner[level_slot]
        group_grads = group_grads + partner
    key_state = (inner_grad + cross_grad[None]).astype(jnp.bfloat16)
    grad_key = near_dk + jnp.einsum(
        "jhab,jnhb->jnha", key_state, value_blocks, preferred_element_type=jnp.float32
    )
    grad_value = near_dv + jnp.einsum(
        "jhab,jnha->jnhb", key_state, key_blocks, preferred_element_type=jnp.float32
    )
    table_part = jnp.einsum(
        "tlx,tlh->xlh", onehot, grad_weight.reshape(tok_dev, LEVELS, head_count), precision=HIGHEST
    )
    grad_table = lax.psum(table_part, "seq")
    row_shape = (tok_dev, head_count * head_width)
    return (
        normed,
        grad_query.astype(jnp.bfloat16).reshape(row_shape),
        grad_key.astype(jnp.bfloat16).reshape(row_shape),
        grad_value.astype(jnp.bfloat16).reshape(row_shape),
        grad_table,
        grad_gain,
    )


def solution(mesh):
    placed = (
        P("seq", "head"),
        P("seq", "head"),
        P("seq", "head"),
        P(None, None, "head"),
        P("seq", None),
        P(),
        P(("seq", "head"), None),
    )
    return jax.shard_map(
        body,
        mesh=mesh,
        in_specs=placed,
        out_specs=(
            P(("seq", "head"), None),
            P("seq", "head"),
            P("seq", "head"),
            P("seq", "head"),
            P(None, None, "head"),
            P(),
        ),
        check_vma=False,
    )
```

profile of v0, /device:TPU:64, one launch (start us, length us, event | category | flops | bytes accessed | tf_op | source)
XLA Modules:
  0.0 519.3 jit_solution(9532326248119924726)
XLA Ops:
  7.2 1.1 reshape.150
  8.3 1.0 reshape.151
  9.3 0.9 fusion.135
  10.7 1.3 fusion.16
  12.6 0.8 copy-done.5
  13.8 89.0 %all-gather.3.cloned.1.call-done = bf16[128,128,128]{2,1,0:T(8,128)(2,1)} async-done(((bf16[4,128,128]{2,1,0:T(8,128)(2,1)}), bf16[128,128,128]{2,1,0:T(8,128)(2,1)}) %all-gather.3.cloned.1.call-update) | async-done | bytes 4194320 | tf_op jit(solution)/shard_map/all_gather | solution.py:60
  102.7 4.5 fusion.5
  107.3 0.6 copy.205
  108.2 1.0 copy-done.4
  109.3 0.6 convolution_bitcast_fusion.1
  109.9 1.7 copy-done.1
  111.6 0.5 multiply_reduce_fusion.1
  112.5 17.2 %all_to_all.26 = bf16[16,16,512]{2,1,0:T(8,128)(2,1)S(1)} all-to-all(bf16[16,16,512]{2,1,0:T(8,128)(2,1)S(1)} %convert_element_type.402), channel_id=1, replica_groups=mesh['seq'=32,'head'=16] {'head'}, dimensions={0} | all-to-all | bytes 524288 | tf_op jit(solution)/shard_map/all_to_all | solution.py:93
  129.9 0.4 fusion.22
  130.3 0.9 fusion.21
  131.2 0.7 copy.311
  131.9 5.0 all-to-all-start.1
  136.9 9.9 %all-to-all-done.1 = bf16[16,16,512]{2,0,1:T(8,128)(2,1)S(1)} async-done(((bf16[16,16,512]{2,0,1:T(8,128)(2,1)}), bf16[16,16,512]{2,0,1:T(8,128)(2,1)S(1)}, u32[]{:S(2)}, u32[]{:S(2)}) %all-to-all-start.1) | async-done | bytes 262176 | tf_op jit(solution)/shard_map/all_to_all | solution.py:104
  146.9 0.7 copy-done.10
  147.9 0.6 convolution_bitcast_fusion
  148.9 1.4 copy-done.3
  150.4 2.1 collective-permute-start
  152.6 16.6 %collective-permute-done = bf16[5,4,128,128]{2,3,0,1:T(8,128)(2,1)S(1)} collective-permute-done((bf16[5,4,128,128]{2,3,0,1:T(8,128)(2,1)S(1)}, bf16[5,4,128,128]{2,3,0,1:T(8,128)(2,1)S(1)}, u32[]{:S(2)}, u32[]{:S(2)}) %collective-permute-start) | collective-permute-done | bytes 655392 | tf_op jit(solution)/shard_map/ppermute | solution.py:18
  169.2 1.0 fusion.56
  170.2 3.3 collective-permute-start.1
  173.6 16.3 %collective-permute-done.1 = bf16[5,4,128,128]{2,3,0,1:T(8,128)(2,1)S(1)} collective-permute-done((bf16[5,4,128,128]{2,3,0,1:T(8,128)(2,1)}, bf16[5,4,128,128]{2,3,0,1:T(8,128)(2,1)S(1)}, u32[]{:S(2)}, u32[]{:S(2)}) %collective-permute-start.1) | collective-permute-done | bytes 655392 | tf_op jit(solution)/shard_map/ppermute | solution.py:18
  189.9 1.1 fusion.27
  191.0 3.3 collective-permute-start.2
  194.3 101.9 %psum.15 = f32[8192]{0:T(1024)} all-reduce(f32[8192]{0:T(1024)S(1)} %get-tuple-element.6), channel_id=1, replica_groups=mesh['seq'=32,'head'=16] {'seq','head'}, use_global_device_ids=true, to_apply=%region_9.10 | all-reduce | flops 8192 | bytes 65536 | tf_op jit(solution)/shard_map/psum | solution.py:100
  296.2 3.0 fusion.2
  299.2 2.0 copy.219
  301.2 1.3 fusion.11
  302.5 2.5 fusion.26
  305.0 3.1 collective-permute-start.3
  308.6 0.7 copy.310
  309.3 0.6 multiply_reduce_fusion
  310.0 1.9 slice_bitcast_fusion
  311.9 2.0 copy.226
  313.9 23.5 %collective-permute-done.3 = bf16[5,4,128,128]{2,3,0,1:T(8,128)(2,1)} collective-permute-done((bf16[5,4,128,128]{2,3,0,1:T(8,128)(2,1)}, bf16[5,4,128,128]{2,3,0,1:T(8,128)(2,1)}, u32[]{:S(2)}, u32[]{:S(2)}) %collective-permute-start.3) | collective-permute-done | bytes 655392 | tf_op jit(solution)/shard_map/ppermute | solution.py:18
  337.4 2.6 add_convert_fusion
  340.0 5.1 collective-permute-start.4
  345.5 156.1 %psum.14 = f32[64,7,4]{0,2,1:T(4,128)} all-reduce(f32[64,7,4]{0,2,1:T(4,128)S(1)} %convolution_bitcast_fusion.7), channel_id=1, replica_groups=mesh['seq'=32,'head'=16] {'seq'}, use_global_device_ids=true, to_apply=%region_7.8 | all-reduce | flops 1792 | bytes 14336 | tf_op jit(solution)/shard_map/psum | solution.py:157
  501.6 2.1 fusion.61
  503.7 2.4 fusion.28
  506.3 1.2 convert_element_type.422
  507.5 1.2 convert_element_type.425
  508.8 1.1 fusion.31
  511.6 0.9 copy_bitcast_fusion
  (79 shorter events, 5.9 us)
Async XLA Ops:
  7.2 3.1 copy-start
  7.2 3.1 copy-start.19
  7.2 3.4 copy-start.17
  7.2 95.5 %all-gather.3.cloned.1.call-start = ((), (), s32[]{:S(2)}) async-start(), calls=%async_computation.2 | async-start | bytes 4325376 | tf_op jit(solution)/shard_map/all_gather | solution.py:60
  12.2 96.0 %copy-start.15 = (bf16[2,1,4,128,128]{3,4,1,2,0:T(8,128)(2,1)}, bf16[2,1,4,128,128]{3,4,1,2,0:T(8,128)(2,1)S(1)}, u32[]{:S(2)}) copy-start(bf16[2,1,4,128,128]{3,4,1,2,0:T(8,128)(2,1)S(1)} %copy.206) | copy-start | bytes 786436
  12.6 0.8 copy-start.5
  13.8 96.1 %copy-start.6 = (f32[2,128,1,4,128]{1,4,2,3,0:T(8,128)}, f32[2,128,1,4,128]{1,4,2,3,0:T(8,128)S(1)}, u32[]{:S(2)}) copy-start(f32[2,128,1,4,128]{1,4,2,3,0:T(8,128)S(1)} %convolution_bitcast_fusion.5) | copy-start | bytes 1572868
  108.2 1.0 copy-start.4
  109.9 1.7 copy-start.1
  112.3 17.6 %copy-start.16 = (bf16[16,8192]{1,0:T(8,128)(2,1)S(1)}, bf16[16,8192]{1,0:T(8,128)(2,1)}, u32[]{:S(2)}) copy-start(bf16[16,8192]{1,0:T(8,128)(2,1)} %param.13) | copy-start | bytes 786436
  112.3 17.6 %copy-start.18 = (f32[8192]{0:T(1024)S(1)}, f32[8192]{0:T(1024)}, u32[]{:S(2)}) copy-start(f32[8192]{0:T(1024)} %param.12) | copy-start | bytes 98308
  131.9 14.9 %all-to-all-start.1 = ((bf16[16,16,512]{2,0,1:T(8,128)(2,1)}), bf16[16,16,512]{2,0,1:T(8,128)(2,1)S(1)}, u32[]{:S(2)}, u32[]{:S(2)}) async-start(bf16[16,16,512]{2,0,1:T(8,128)(2,1)} %bitcast.93), calls=%async_computation.1 | async-start | bytes 524288 | tf_op jit(solution)/shard_map/all_to_all | solution.py:104
  146.9 0.7 copy-start.10
  147.9 0.8 copy-start.8
  148.7 1.6 copy-start.3
  150.4 18.8 %collective-permute-start = (bf16[5,4,128,128]{2,3,0,1:T(8,128)(2,1)S(1)}, bf16[5,4,128,128]{2,3,0,1:T(8,128)(2,1)S(1)}, u32[]{:S(2)}, u32[]{:S(2)}) collective-permute-start(bf16[5,4,128,128]{2,3,0,1:T(8,128)(2,1)S(1)} %convert_element_type.415), channel_id=1, source_target_pairs={{0,16},{16,0},{32,48},{48,32},{64,80},{80,64},{96,112},{112,96},{1... | collective-permute-start | bytes 1966088 | tf_op jit(solution)/shard_map/ppermute | solution.py:18
  170.2 19.6 %collective-permute-start.1 = (bf16[5,4,128,128]{2,3,0,1:T(8,128)(2,1)}, bf16[5,4,128,128]{2,3,0,1:T(8,128)(2,1)S(1)}, u32[]{:S(2)}, u32[]{:S(2)}) collective-permute-start(bf16[5,4,128,128]{2,3,0,1:T(8,128)(2,1)} %fusion.56), channel_id=1, source_target_pairs={{0,32},{16,48},{32,0},{48,16},{64,96},{80,112},{96,64},{112,80},{1... | collective-permute-start | bytes 1966088 | tf_op jit(solution)/shard_map/ppermute | solution.py:18
  191.0 111.5 %collective-permute-start.2 = (bf16[5,4,128,128]{2,3,0,1:T(8,128)(2,1)}, bf16[5,4,128,128]{2,3,0,1:T(8,128)(2,1)}, u32[]{:S(2)}, u32[]{:S(2)}) collective-permute-start(bf16[5,4,128,128]{2,3,0,1:T(8,128)(2,1)} %fusion.27), channel_id=1, source_target_pairs={{0,64},{16,80},{32,96},{48,112},{64,0},{80,16},{96,32},{112,48},{1... | collective-permute-start | bytes 1966088 | tf_op jit(solution)/shard_map/ppermute | solution.py:18
  302.5 5.6 %copy-start.13 = (bf16[2,4,128,128]{3,2,1,0:T(8,128)(2,1)}, bf16[2,4,128,128]{3,2,1,0:T(8,128)(2,1)S(1)}, u32[]{:S(2)}) copy-start(bf16[2,4,128,128]{3,2,1,0:T(8,128)(2,1)S(1)} %fusion.11) | copy-start | bytes 786436
  302.5 5.6 %copy-start.12 = (f32[2,128,4,128]{3,1,2,0:T(8,128)S(1)}, f32[2,128,4,128]{3,1,2,0:T(8,128)}, u32[]{:S(2)}) copy-start(f32[2,128,4,128]{3,1,2,0:T(8,128)} %copy.219) | copy-start | bytes 1572868
  302.5 6.8 %copy-start.2 = (f32[2,128,6,4,128]{1,4,2,3,0:T(8,128)S(1)}, f32[2,128,6,4,128]{1,4,2,3,0:T(8,128)}, u32[]{:S(2)}) copy-start(f32[2,128,6,4,128]{1,4,2,3,0:T(8,128)} %copy-done.1) | copy-start | bytes 9437188
  305.0 4.3 copy-start.7
  305.0 4.3 copy-start.9
  305.0 32.4 %collective-permute-start.3 = (bf16[5,4,128,128]{2,3,0,1:T(8,128)(2,1)}, bf16[5,4,128,128]{2,3,0,1:T(8,128)(2,1)}, u32[]{:S(2)}, u32[]{:S(2)}) collective-permute-start(bf16[5,4,128,128]{2,3,0,1:T(8,128)(2,1)} %fusion.26), channel_id=1, source_target_pairs={{0,128},{16,144},{32,160},{48,176},{64,192},{80,208},{96,224},{112... | collective-permute-start | bytes 1966088 | tf_op jit(solution)/shard_map/ppermute | solution.py:18
  340.0 168.8 %collective-permute-start.4 = (bf16[5,4,128,128]{2,3,0,1:T(8,128)(2,1)}, bf16[5,4,128,128]{2,3,0,1:T(8,128)(2,1)}, u32[]{:S(2)}, u32[]{:S(2)}) collective-permute-start(bf16[5,4,128,128]{2,3,0,1:T(8,128)(2,1)} %add_convert_fusion), channel_id=1, source_target_pairs={{0,256},{16,272},{32,288},{48,304},{64,320},{80,336},{96,352},{112... | collective-permute-start | bytes 1966088 | tf_op jit(solution)/shard_map/ppermute | solution.py:18
  508.8 1.5 copy-start.11
  510.0 1.0 copy-start.14
Sparse Core Ops, SparseCore 0:
  11.7 90.9 all-gather.2
where the time goes:
time: 520 us; the launch traced here: 519 us
  blocking collectives  275 us (53%)
  waiting for transfers between devices  155 us (30%)
  starting transfers between devices  22 us (4%)
  local copies, waits for them, and re-layouts  19.3 us (4%)
  matrix products  19 us (4%)
  between operations  14.6 us (3%)
  other arithmetic  13.9 us (3%)
    psum x1, blocking collectives, body(): grad_table = lax.psum(table_part, 'seq')  156 us
    psum x1, blocking collectives, body(): grad_gain = lax.psum(jnp.sum(grad_out * unit_rows, axis=0), ('seq', 'head'))  102 us
    all_gather x1, waiting for transfers between devices, body(): lax.all_gather(shard_total[None].astype(jnp.bfloat16), 'seq', axis=0, til...  89 us
    ppermute x5, waiting for transfers between devices, swapped(): return lax.ppermute(value, axis, pairs)  56.4 us
    all_to_all x1, blocking collectives, body(): lax.all_to_all(attn_rows, 'head', split_axis=0, concat_axis=1, tiled=True)  17.2 us
    ppermute x5, starting transfers between devices, swapped(): return lax.ppermute(value, axis, pairs)  17 us
  transfers between devices with their start and end apart: 7, of which 5 were waited for; matrix products, arithmetic and copies ran while one was open for 4% of the time, Pallas kernels for 0%

commit v1 on v0

v1 whole, which is shorter than its diff:
```python
import jax
import jax.numpy as jnp
from jax import lax
from jax.experimental import pallas as pl
from jax.experimental.pallas import tpu as pltpu
from jax.sharding import PartitionSpec as P

CH = 128
TABLE = 64
EPSILON = 1e-06
HIGHEST = lax.Precision.HIGHEST
F32 = jnp.float32
BF16 = jnp.bfloat16
INTERPRET = False


def call(kernel, name, out_shape, *operands):
    return pl.pallas_call(
        kernel,
        out_shape=out_shape,
        name=name,
        interpret=INTERPRET,
        compiler_params=pltpu.CompilerParams(vmem_limit_bytes=48 * 1024 * 1024),
    )(*operands)


def shaped(shape, dtype):
    return jax.ShapeDtypeStruct(shape, dtype)


def dot_nn(a, b, precision=None):
    return lax.dot_general(a, b, (((1,), (0,)), ((), ())), precision=precision, preferred_element_type=F32)


def dot_nt(a, b):
    return lax.dot_general(a, b, (((1,), (1,)), ((), ())), preferred_element_type=F32)


def dot_tn(a, b, precision=None):
    return lax.dot_general(a, b, (((0,), (0,)), ((), ())), precision=precision, preferred_element_type=F32)


def causal_mask():
    rows = lax.broadcasted_iota(jnp.int32, (CH, CH), 0)
    cols = lax.broadcasted_iota(jnp.int32, (CH, CH), 1)
    return cols <= rows


def span_rows(c):
    return slice(c * CH, (c + 1) * CH)


def to_row(tile):
    return jnp.sum(tile.T, axis=0, keepdims=True)


def to_columns(row):
    return jnp.broadcast_to(row, (CH, CH)).T


def put_slices(ref, value, head, level=None):
    slices, height = ref.shape[0], ref.shape[-2]
    per_head = CH // height
    pieces = value.astype(BF16).reshape(per_head, height, value.shape[1])
    where = slice(head * per_head, (head + 1) * per_head)
    if level is None:
        ref[where] = pieces
    else:
        ref[where, level] = pieces


def get_slices(ref, head, level=None):
    height, width = ref.shape[-2:]
    per_head = CH // height
    where = slice(head * per_head, (head + 1) * per_head)
    pieces = ref[where] if level is None else ref[where, level]
    return pieces.reshape(CH, width)


def state_kernel(key_ref, value_ref, total_ref, first_ref):
    heads = key_ref.shape[1] // CH
    for h in range(heads):
        cols = span_rows(h)
        first = dot_tn(key_ref[0:CH, cols], value_ref[0:CH, cols])
        second = dot_tn(key_ref[CH : 2 * CH, cols], value_ref[CH : 2 * CH, cols])
        first_ref[cols, :] = first.astype(BF16)
        put_slices(total_ref, first + second, h)


def prefix_kernel(in_ref, out_ref):
    shards, levels = out_ref.shape[0], out_ref.shape[1]
    sums = [in_ref[s].astype(F32) for s in range(shards)]
    zero = jnp.zeros(in_ref.shape[1:], BF16)
    for level in range(levels):
        rounded = [s.astype(BF16) for s in sums]
        for t in range(shards):
            group = t >> level
            out_ref[t, level] = rounded[group - 1] if group & 1 else zero
        sums = [sums[2 * i] + sums[2 * i + 1] for i in range(len(sums) // 2)]


def suffix_kernel(in_ref, out_ref):
    shards, levels = in_ref.shape[0], in_ref.shape[1]
    carried = [None]
    for level in range(levels - 1, -1, -1):
        size = 1 << level
        groups = shards >> level
        below = []
        for g in range(groups):
            base = carried[g >> 1]
            if g & 1 == 0:
                total = None
                for s in range((g + 1) * size, (g + 2) * size):
                    piece = in_ref[s, level].astype(F32)
                    total = piece if total is None else total + piece
                base = total if base is None else base + total
            below.append(base)
        carried = below
    zero = jnp.zeros(in_ref.shape[2:], F32)
    for t in range(shards):
        value = zero if carried[t] is None else carried[t]
        out_ref[t] = value.astype(BF16)


def weight_kernel(index_ref, table_ref, weight_ref):
    levels = index_ref.shape[1]
    heads = table_ref.shape[1]
    tokens = index_ref.shape[0]
    entry = lax.broadcasted_iota(jnp.int32, (tokens, TABLE), 1)
    for level in range(levels):
        onehot = (index_ref[:, level : level + 1] == entry).astype(F32)
        picked = dot_nn(onehot, table_ref[level * TABLE : (level + 1) * TABLE, :], HIGHEST)
        weight_ref[:, level * heads : (level + 1) * heads] = picked


def near_kernel(query_ref, key_ref, value_ref, first_ref, weight_ref, out_ref):
    heads = query_ref.shape[1] // CH
    spans = query_ref.shape[0] // CH
    causal = causal_mask()
    for c in range(spans):
        rows = span_rows(c)
        for h in range(heads):
            cols = span_rows(h)
            query = query_ref[rows, cols]
            scores = jnp.where(causal, dot_nt(query, key_ref[rows, cols]), 0.0).astype(BF16)
            near = weight_ref[rows, h : h + 1] * dot_nn(scores, value_ref[rows, cols])
            if c == 1:
                near = near + weight_ref[rows, heads + h : heads + h + 1] * dot_nn(query, first_ref[cols, :])
            out_ref[rows, cols] = near


def far_kernel(near_ref, query_ref, state_ref, weight_ref, cot_ref, gain_ref, attn_ref, stat_ref):
    heads = query_ref.shape[1] // CH
    spans = query_ref.shape[0] // CH
    levels = state_ref.shape[1]
    stats = []
    for c in range(spans):
        rows = span_rows(c)
        squares = jnp.zeros((CH, CH), F32)
        along = jnp.zeros((CH, CH), F32)
        for h in range(heads):
            cols = span_rows(h)
            query = query_ref[rows, cols]
            total = near_ref[rows, cols]
            for level in range(levels):
                spot = (level + 2) * heads + h
                total = total + weight_ref[rows, spot : spot + 1] * dot_nn(query, get_slices(state_ref, h, level))
            attn = total.astype(BF16)
            attn_ref[rows, cols] = attn
            attn_f = attn.astype(F32)
            scaled = cot_ref[rows, cols].astype(F32) * gain_ref[:, cols]
            squares = squares + attn_f * attn_f
            along = along + scaled * attn_f
        stats.append(to_row(squares))
        stats.append(to_row(along))
    block = jnp.concatenate(stats + [jnp.zeros((8 - len(stats), CH), F32)], axis=0)
    for d in range(stat_ref.shape[0]):
        stat_ref[d] = block


def norm_columns(stat_ref, features, c):
    total = stat_ref[0]
    for d in range(1, stat_ref.shape[0]):
        total = total + stat_ref[d]
    inv_rms = lax.rsqrt(total[2 * c : 2 * c + 1, :] / features + EPSILON)
    mean = total[2 * c + 1 : 2 * c + 2, :] * inv_rms / features
    return to_columns(inv_rms), to_columns(mean)


def grad_kernel(attn_ref, stat_ref, cot_ref, gain_ref, query_ref, weight_ref, grad_ref, group_ref):
    heads = query_ref.shape[1] // CH
    spans = query_ref.shape[0] // CH
    levels = group_ref.shape[1]
    features = float(stat_ref.shape[0] * attn_ref.shape[1])
    norms = [norm_columns(stat_ref, features, c) for c in range(spans)]
    for h in range(heads):
        cols = span_rows(h)
        parts = [[] for _ in range(levels)]
        for c in range(spans):
            rows = span_rows(c)
            inv_rms, mean = norms[c]
            unit = attn_ref[rows, cols].astype(F32) * inv_rms
            scaled = cot_ref[rows, cols].astype(F32) * gain_ref[:, cols]
            grad = ((scaled - unit * mean) * inv_rms).astype(BF16)
            grad_ref[rows, cols] = grad
            grad_f = grad.astype(F32)
            for level in range(levels):
                spot = (level + 2) * heads + h
                parts[level].append((weight_ref[rows, spot : spot + 1] * grad_f).astype(BF16))
        query = query_ref[:, cols]
        for level in range(levels):
            put_slices(group_ref, dot_tn(query, jnp.concatenate(parts[level], axis=0)), h, level)


def norm_kernel(attn_ref, stat_ref, cot_ref, gain_ref, normed_ref, gain_part_ref):
    heads = attn_ref.shape[1] // CH
    spans = attn_ref.shape[0] // CH
    features = float(stat_ref.shape[0] * attn_ref.shape[1])
    norms = [norm_columns(stat_ref, features, c) for c in range(spans)]
    pieces = []
    for h in range(heads):
        cols = span_rows(h)
        part = jnp.zeros((1, CH), F32)
        for c in range(spans):
            rows = span_rows(c)
            unit = attn_ref[rows, cols].astype(F32) * norms[c][0]
            normed_ref[rows, cols] = (unit * gain_ref[:, cols]).astype(BF16)
            part = part + jnp.sum(cot_ref[rows, cols].astype(F32) * unit, axis=0, keepdims=True)
        pieces.append(part)
    block = jnp.concatenate(pieces + [jnp.zeros((8 - heads, CH), F32)], axis=0)
    for d in range(gain_part_ref.shape[0]):
        gain_part_ref[d] = block


def back_kernel(
    query_ref, key_ref, value_ref, grad_ref, weight_ref, state_ref, first_ref, index_ref,
    dq_ref, dk_ref, dv_ref, inner_ref, table_ref, gw_ref,
):
    heads = query_ref.shape[1] // CH
    spans = query_ref.shape[0] // CH
    levels = state_ref.shape[1]
    all_levels = levels + 2
    tokens = spans * CH
    causal = causal_mask()
    gw_ref[...] = jnp.zeros(gw_ref.shape, F32)
    for c in range(spans):
        rows = span_rows(c)
        for h in range(heads):
            cols = span_rows(h)
            query = query_ref[rows, cols]
            query_f = query.astype(F32)
            key = key_ref[rows, cols]
            grad = grad_ref[rows, cols]
            first_weight = weight_ref[rows, h : h + 1]
            scores = jnp.where(causal, dot_nt(query, key), 0.0)
            along = jnp.where(causal, dot_nt(grad, value_ref[rows, cols]), 0.0)
            gw_ref[rows, h : h + 1] = jnp.sum(scores.astype(BF16).astype(F32) * along, axis=1, keepdims=True)
            grad_scores = (along * first_weight).astype(BF16)
            weighted = (scores * first_weight).astype(BF16)
            dq = dot_nn(grad_scores, key)
            dk_ref[rows, cols] = dot_tn(grad_scores, query)
            dv_ref[rows, cols] = dot_tn(weighted, grad)
            if c == 1:
                spot = heads + h
                weight = weight_ref[rows, spot : spot + 1]
                far = dot_nt(grad, first_ref[cols, :])
                gw_ref[rows, spot : spot + 1] = jnp.sum(query_f * far, axis=1, keepdims=True)
                dq = dq + weight * far
                inner_ref[cols, :] = dot_tn(query, (weight * grad.astype(F32)).astype(BF16))
            for level in range(levels):
                spot = (level + 2) * heads + h
                far = dot_nt(grad, get_slices(state_ref, h, level))
                gw_ref[rows, spot : spot + 1] = jnp.sum(query_f * far, axis=1, keepdims=True)
                dq = dq + weight_ref[rows, spot : spot + 1] * far
            dq_ref[rows, cols] = dq.astype(BF16)
    grads = gw_ref[...]
    entry = lax.broadcasted_iota(jnp.int32, (tokens, TABLE), 1)
    width = grads.shape[1]
    pick_rows = lax.broadcasted_iota(jnp.int32, (8, width), 0)
    pick_cols = lax.broadcasted_iota(jnp.int32, (8, width), 1)
    blocks = []
    for level in range(all_levels):
        onehot = (index_ref[:, level : level + 1] == entry).astype(F32)
        by_row = dot_tn(grads, onehot, HIGHEST)
        pick = ((pick_cols == pick_rows + level * heads) & (pick_rows < heads)).astype(F32)
        blocks.append(dot_nn(pick, by_row, HIGHEST))
    if all_levels % 2:
        blocks.append(jnp.zeros((8, TABLE), F32))
    for pair in range(len(blocks) // 2):
        joined = jnp.concatenate([blocks[2 * pair], blocks[2 * pair + 1]], axis=1)[:heads]
        for d in range(table_ref.shape[0]):
            table_ref[d, pair * heads : (pair + 1) * heads, :] = joined


def final_kernel(cross_ref, inner_ref, key_ref, value_ref, dk_ref, dv_ref, grad_key_ref, grad_value_ref):
    heads = key_ref.shape[1] // CH
    spans = key_ref.shape[0] // CH
    for h in range(heads):
        cols = span_rows(h)
        cross = get_slices(cross_ref, h)
        for c in range(spans):
            rows = span_rows(c)
            state = cross if c == 1 else (inner_ref[cols, :] + cross.astype(F32)).astype(BF16)
            grad_key = dk_ref[rows, cols] + dot_nt(value_ref[rows, cols], state)
            grad_value = dv_ref[rows, cols] + dot_nn(key_ref[rows, cols], state)
            grad_key_ref[rows, cols] = grad_key.astype(BF16)
            grad_value_ref[rows, cols] = grad_value.astype(BF16)


def exchange(value, axis):
    return lax.all_to_all(value, axis, split_axis=0, concat_axis=0, tiled=True)


def body(queries, key_rows, value_rows, level_table, level_index, norm_gain, cotangent):
    tokens, width = queries.shape
    heads = level_table.shape[2]
    all_levels = level_table.shape[1]
    shards = lax.axis_size("seq")
    columns = lax.axis_size("head")
    levels = shards.bit_length() - 1
    height = heads * CH // shards
    own = tokens // columns

    cot = exchange(jnp.transpose(cotangent.reshape(own, columns, width), (1, 0, 2)), "head").reshape(tokens, width)
    gain = lax.dynamic_slice(norm_gain, (lax.axis_index("head") * width,), (width,)).reshape(1, width)
    table = jnp.transpose(level_table, (1, 0, 2)).reshape(all_levels * TABLE, heads)

    total, first = call(
        state_kernel,
        "span_states",
        (shaped((shards, height, CH), BF16), shaped((heads * CH, CH), BF16)),
        key_rows,
        value_rows,
    )
    slices = exchange(total, "seq")
    weights = call(weight_kernel, "level_weights", shaped((tokens, all_levels * heads), F32), level_index, table)
    near = call(
        near_kernel, "near_attention", shaped((tokens, width), F32), queries, key_rows, value_rows, first, weights
    )
    group_states = call(prefix_kernel, "prefix_states", shaped((shards, levels, height, CH), BF16), slices)
    states = exchange(group_states.reshape(shards, levels * height, CH), "seq").reshape(group_states.shape)
    attn, stat = call(
        far_kernel,
        "far_attention",
        (shaped((tokens, width), BF16), shaped((columns, 8, CH), F32)),
        near,
        queries,
        states,
        weights,
        cot,
        gain,
    )
    stats = exchange(stat, "head")
    grad, groups = call(
        grad_kernel,
        "attention_grad",
        (shaped((tokens, width), BF16), shaped((shards, levels, height, CH), BF16)),
        attn,
        stats,
        cot,
        gain,
        queries,
        weights,
    )
    group_slices = exchange(groups.reshape(shards, levels * height, CH), "seq").reshape(groups.shape)
    normed, gain_part = call(
        norm_kernel,
        "norm_output",
        (shaped((tokens, width), BF16), shaped((shards, 8, CH), F32)),
        attn,
        stats,
        cot,
        gain,
    )
    normed = exchange(normed.reshape(columns, own, width), "head")
    normed = jnp.transpose(normed, (1, 0, 2)).reshape(own, columns * width)
    gain_sum = jnp.sum(exchange(gain_part, "seq"), axis=0)
    gain_all = exchange(jnp.broadcast_to(gain_sum[None], (columns, 8, CH)), "head")
    grad_gain = gain_all[:, :heads].reshape(columns * width)

    pairs = (all_levels + 1) // 2
    grad_query, near_dk, near_dv, inner, table_part, _ = call(
        back_kernel,
        "query_grad",
        (
            shaped((tokens, width), BF16),
            shaped((tokens, width), F32),
            shaped((tokens, width), F32),
            shaped((heads * CH, CH), F32),
            shaped((shards, pairs * heads, 2 * TABLE), F32),
            shaped((tokens, CH), F32),
        ),
        queries,
        key_rows,
        value_rows,
        grad,
        weights,
        states,
        first,
        level_index,
    )
    table_sum = jnp.sum(exchange(table_part, "seq"), axis=0)
    table_sum = table_sum.reshape(pairs, heads, 2, TABLE).transpose(3, 0, 2, 1)
    grad_table = table_sum.reshape(TABLE, 2 * pairs, heads)[:, :all_levels]

    key_slices = call(suffix_kernel, "suffix_states", shaped((shards, height, CH), BF16), group_slices)
    cross = exchange(key_slices, "seq")
    grad_key, grad_value = call(
        final_kernel,
        "key_value_grad",
        (shaped((tokens, width), BF16), shaped((tokens, width), BF16)),
        cross,
        inner,
        key_rows,
        value_rows,
        near_dk,
        near_dv,
    )
    return normed, grad_query, grad_key, grad_value, grad_table, grad_gain


def solution(mesh):
    placed = (
        P("seq", "head"),
        P("seq", "head"),
        P("seq", "head"),
        P(None, None, "head"),
        P("seq", None),
        P(),
        P(("seq", "head"), None),
    )
    return jax.shard_map(
        body,
        mesh=mesh,
        in_specs=placed,
        out_specs=(
            P(("seq", "head"), None),
            P("seq", "head"),
            P("seq", "head"),
            P("seq", "head"),
            P(None, None, "head"),
            P(),
        ),
        check_vma=False,
    )
```

time: 520 us -> 185 us (0.36)
  the two profiles are of different devices: /device:TPU:64 before, /device:TPU:8 now
where the time goes in v1:
time: 185 us; the launch traced here: 184 us
  waiting for transfers between devices  76 us (41%)
  starting transfers between devices  44.3 us (24%)
  blocking collectives  37.7 us (20%)
  Pallas kernels  16.2 us (9%)
  local copies, waits for them, and re-layouts  8.67 us (5%)
    all_to_all x7, waiting for transfers between devices, exchange(): return lax.all_to_all(value, axis, split_axis=0, concat_axis=0, tiled=True)  76 us
    all_to_all x7, starting transfers between devices, exchange(): return lax.all_to_all(value, axis, split_axis=0, concat_axis=0, tiled=True)  44.3 us
    all_to_all x3, blocking collectives, exchange(): return lax.all_to_all(value, axis, split_axis=0, concat_axis=0, tiled=True)  37.7 us
    pallas_call x10, Pallas kernels, call(): pl.pallas_call(kernel, out_shape=out_shape, name=name, interpret=INTERPRE...  16.2 us
    unnamed x32, local copies, waits for them, and re-layouts  5.56 us
  transfers between devices with their start and end apart: 7, of which 7 were waited for; matrix products, arithmetic and copies ran while one was open for 2% of the time, Pallas kernels for 7%

profile of v1, /device:TPU:8, one launch (start us, length us, event | category | flops | bytes accessed | tf_op | source)
XLA Modules:
  0.0 183.7 jit_solution(11565368823992841729)
XLA Ops:
  0.6 0.0 copy-start
  0.6 0.9 copy-done
  1.6 0.9 copy-done.2
  2.5 0.9 span_states.1
  3.5 10.3 %all-to-all-start = ((bf16[32,16,128]{2,1,0:T(8,128)(2,1)}), bf16[32,16,128]{2,1,0:T(8,128)(2,1)S(1)}, u32[]{:S(2)}, u32[]{:S(2)}) async-start(bf16[32,16,128]{2,1,0:T(8,128)(2,1)} %get-tuple-element.22), calls=%async_computation | async-start | bytes 262144 | tf_op jit(solution)/shard_map/all_to_all | solution.py:311
  13.8 0.7 copy.33
  14.5 8.9 %all-to-all-done.in_ref = bf16[32,16,128]{2,1,0:T(8,128)(2,1)S(1)} async-done(((bf16[32,16,128]{2,1,0:T(8,128)(2,1)}), bf16[32,16,128]{2,1,0:T(8,128)(2,1)S(1)}, u32[]{:S(2)}, u32[]{:S(2)}) %all-to-all-start) | async-done | bytes 131104 | tf_op jit(solution)/shard_map/all_to_all | solution.py:311
  23.4 10.4 %all-to-all-start.2 = ((bf16[16,16,512]{2,1,0:T(8,128)(2,1)}), bf16[16,16,512]{2,1,0:T(8,128)(2,1)S(1)}, u32[]{:S(2)}, u32[]{:S(2)}) async-start(bf16[16,16,512]{2,1,0:T(8,128)(2,1)} %bitcast.21), calls=%async_computation.2 | async-start | bytes 524288 | tf_op jit(solution)/shard_map/all_to_all | solution.py:311
  33.8 0.9 prefix_states.1
  34.7 10.2 %all-to-all-done.2 = bf16[16,16,512]{2,1,0:T(8,128)(2,1)S(1)} async-done(((bf16[16,16,512]{2,1,0:T(8,128)(2,1)}), bf16[16,16,512]{2,1,0:T(8,128)(2,1)S(1)}, u32[]{:S(2)}, u32[]{:S(2)}) %all-to-all-start.2) | async-done | bytes 262176 | tf_op jit(solution)/shard_map/all_to_all | solution.py:311
  45.0 4.7 %all-to-all-start.1 = ((bf16[32,80,128]{2,1,0:T(8,128)(2,1)}), bf16[32,80,128]{2,1,0:T(8,128)(2,1)S(1)}, u32[]{:S(2)}, u32[]{:S(2)}) async-start(bf16[32,80,128]{2,1,0:T(8,128)(2,1)} %bitcast.2), calls=%async_computation.1 | async-start | bytes 1310720 | tf_op jit(solution)/shard_map/all_to_all | solution.py:311
  49.7 0.0 copy-start.14
  49.7 0.7 copy-done.14
  50.4 0.1 copy.24.index_ref
  50.6 0.0 copy-start.3
  50.6 0.1 copy.23
  50.7 0.0 copy-start.1
  50.8 0.8 dynamic_slice.3
  51.6 1.0 level_weights.1.weight_ref
  52.6 1.0 near_attention.1.near_ref
  53.7 16.3 %all-to-all-done.1 = bf16[32,80,128]{2,1,0:T(8,128)(2,1)S(1)} async-done(((bf16[32,80,128]{2,1,0:T(8,128)(2,1)}), bf16[32,80,128]{2,1,0:T(8,128)(2,1)S(1)}, u32[]{:S(2)}, u32[]{:S(2)}) %all-to-all-start.1) | async-done | bytes 655392 | tf_op jit(solution)/shard_map/all_to_all | solution.py:311
  69.9 1.0 far_attention.1
  70.9 10.9 %all_to_all.50.stat_ref = f32[16,8,128]{2,1,0:T(8,128)S(1)} all-to-all(f32[16,8,128]{2,1,0:T(8,128)S(1)} %get-tuple-element.24), channel_id=1, replica_groups=mesh['seq'=32,'head'=16] {'head'}, dimensions={0} | all-to-all | bytes 131072 | tf_op jit(solution)/shard_map/all_to_all | solution.py:311
  81.8 0.9 norm_output.1
  82.7 15.8 %all_to_all.51 = f32[32,8,128]{2,1,0:T(8,128)S(1)} all-to-all(f32[32,8,128]{2,1,0:T(8,128)S(1)} %get-tuple-element.35), channel_id=1, replica_groups=mesh['seq'=32,'head'=16] {'seq'}, dimensions={0} | all-to-all | bytes 262144 | tf_op jit(solution)/shard_map/all_to_all | solution.py:311
  98.5 11.1 %all_to_all.52 = f32[16,8,128]{2,1,0:T(8,128)} all-to-all(f32[16,8,128]{2,1,0:T(8,128)S(1)} %broadcast_in_dim.2), channel_id=1, replica_groups=mesh['seq'=32,'head'=16] {'head'}, dimensions={0} | all-to-all | bytes 131072 | tf_op jit(solution)/shard_map/all_to_all | solution.py:311
  109.6 3.5 %all-to-all-start.4 = ((bf16[16,16,512]{2,1,0:T(8,128)(2,1)}), bf16[16,16,512]{2,1,0:T(8,128)(2,1)S(1)}, u32[]{:S(2)}, u32[]{:S(2)}) async-start(bf16[16,16,512]{2,1,0:T(8,128)(2,1)} %bitcast.7), calls=%async_computation.4 | async-start | bytes 524288 | tf_op jit(solution)/shard_map/all_to_all | solution.py:311
  113.1 2.1 %attention_grad.1 = (bf16[256,512]{1,0:T(8,128)(2,1)S(1)}, bf16[32,5,16,128]{3,2,1,0:T(8,128)(2,1)}) custom-call(bf16[256,512]{1,0:T(8,128)(2,1)S(1)} %get-tuple-element.23.attn_ref, f32[16,8,128]{2,1,0:T(8,128)S(1)} %all_to_all.50.stat_ref, bf16[256,512]{1,0:T(8,128)(2,1)S(1)} %bitcast.27, f32[1,512]{1,0:T(1,128)S(1)} %bitcast.32, ...), custom_call_target="tpu_custom_call" | custom-call | tf_op jit(solution)/shard_map/attention_grad/pallas_call | solution.py:18
  115.2 0.7 copy-done.7
  115.9 8.2 %all-to-all-done.4 = bf16[16,16,512]{2,1,0:T(8,128)(2,1)S(1)} async-done(((bf16[16,16,512]{2,1,0:T(8,128)(2,1)}), bf16[16,16,512]{2,1,0:T(8,128)(2,1)S(1)}, u32[]{:S(2)}, u32[]{:S(2)}) %all-to-all-start.4) | async-done | bytes 262176 | tf_op jit(solution)/shard_map/all_to_all | solution.py:311
  124.1 0.7 copy-done.9
  124.8 4.6 %all-to-all-start.5 = ((bf16[32,80,128]{2,1,0:T(8,128)(2,1)}), bf16[32,80,128]{2,1,0:T(8,128)(2,1)S(1)}, u32[]{:S(2)}, u32[]{:S(2)}) async-start(bf16[32,80,128]{2,1,0:T(8,128)(2,1)} %bitcast.9), calls=%async_computation.5 | async-start | bytes 1310720 | tf_op jit(solution)/shard_map/all_to_all | solution.py:311
  129.5 0.0 copy-done.8
  129.5 6.5 %query_grad.1 = (bf16[256,512]{1,0:T(8,128)(2,1)}, f32[256,512]{1,0:T(8,128)S(1)}, f32[256,512]{1,0:T(8,128)S(1)}, f32[512,128]{1,0:T(8,128)S(1)}, f32[32,16,128]{2,1,0:T(8,128)}, /*index=5*/f32[256,128]{1,0:T(8,128)}) custom-call(bf16[256,512]{1,0:T(8,128)(2,1)S(1)} %copy-done.4, bf16[256,512]{1,0:T(8,128)(2,1)S(1)} %copy-done.1, ...), custom_call_target="tpu_custom_call" | custom-call | tf_op jit(solution)/shard_map/query_grad/pallas_call | solution.py:18
  135.9 0.8 copy-done.5
  136.8 12.9 %all-to-all-done.5 = bf16[32,80,128]{2,1,0:T(8,128)(2,1)S(1)} async-done(((bf16[32,80,128]{2,1,0:T(8,128)(2,1)}), bf16[32,80,128]{2,1,0:T(8,128)(2,1)S(1)}, u32[]{:S(2)}, u32[]{:S(2)}) %all-to-all-start.5) | async-done | bytes 655392 | tf_op jit(solution)/shard_map/all_to_all | solution.py:311
  149.6 6.0 %all-to-all-start.7 = ((f32[32,16,128]{2,1,0:T(8,128)}), f32[32,16,128]{2,1,0:T(8,128)S(1)}, u32[]{:S(2)}, u32[]{:S(2)}) async-start(f32[32,16,128]{2,1,0:T(8,128)} %get-tuple-element.34), calls=%async_computation.7 | async-start | bytes 524288 | tf_op jit(solution)/shard_map/all_to_all | solution.py:311
  155.7 0.7 suffix_states.1
  156.4 11.9 %all-to-all-done.7 = f32[32,16,128]{2,1,0:T(8,128)S(1)} async-done(((f32[32,16,128]{2,1,0:T(8,128)}), f32[32,16,128]{2,1,0:T(8,128)S(1)}, u32[]{:S(2)}, u32[]{:S(2)}) %all-to-all-start.7) | async-done | bytes 262176 | tf_op jit(solution)/shard_map/all_to_all | solution.py:311
  168.3 4.6 %all-to-all-start.6 = ((bf16[32,16,128]{2,1,0:T(8,128)(2,1)}), bf16[32,16,128]{2,1,0:T(8,128)(2,1)S(1)}, u32[]{:S(2)}, u32[]{:S(2)}) async-start(bf16[32,16,128]{2,1,0:T(8,128)(2,1)} %suffix_states.1), calls=%async_computation.6 | async-start | bytes 262144 | tf_op jit(solution)/shard_map/all_to_all | solution.py:311
  173.0 0.0 copy-done.12
  173.0 0.0 copy-start.6
  173.0 0.6 slice.9
  173.6 0.7 copy.31
  174.4 0.1 reshape.62
  174.5 0.6 copy.29
  175.1 7.5 %all-to-all-done.6.cross_ref = bf16[32,16,128]{2,1,0:T(8,128)(2,1)S(1)} async-done(((bf16[32,16,128]{2,1,0:T(8,128)(2,1)}), bf16[32,16,128]{2,1,0:T(8,128)(2,1)S(1)}, u32[]{:S(2)}, u32[]{:S(2)}) %all-to-all-start.6) | async-done | bytes 131104 | tf_op jit(solution)/shard_map/all_to_all | solution.py:311
  182.6 1.1 key_value_grad.1
  (21 shorter events, 0.1 us)
Async XLA Ops:
  0.6 1.0 copy-start
  1.6 0.9 copy-start.2
  3.5 10.3 %copy-start.11 = (bf16[16,8192]{1,0:T(8,128)(2,1)S(1)}, bf16[16,8192]{1,0:T(8,128)(2,1)}, u32[]{:S(2)}) copy-start(bf16[16,8192]{1,0:T(8,128)(2,1)} %param.13) | copy-start | bytes 786436
  3.5 20.0 %all-to-all-start = ((bf16[32,16,128]{2,1,0:T(8,128)(2,1)}), bf16[32,16,128]{2,1,0:T(8,128)(2,1)S(1)}, u32[]{:S(2)}, u32[]{:S(2)}) async-start(bf16[32,16,128]{2,1,0:T(8,128)(2,1)} %get-tuple-element.22), calls=%async_computation | async-start | bytes 262144 | tf_op jit(solution)/shard_map/all_to_all | solution.py:311
  23.4 21.6 %all-to-all-start.2 = ((bf16[16,16,512]{2,1,0:T(8,128)(2,1)}), bf16[16,16,512]{2,1,0:T(8,128)(2,1)S(1)}, u32[]{:S(2)}, u32[]{:S(2)}) async-start(bf16[16,16,512]{2,1,0:T(8,128)(2,1)} %bitcast.21), calls=%async_computation.2 | async-start | bytes 524288 | tf_op jit(solution)/shard_map/all_to_all | solution.py:311
  45.0 5.6 %copy-start.13 = (f32[64,7,4]{0,2,1:T(4,128)S(1)}, f32[64,7,4]{0,2,1:T(4,128)}, u32[]{:S(2)}) copy-start(f32[64,7,4]{0,2,1:T(4,128)} %param.10) | copy-start | bytes 21508
  45.0 24.9 %all-to-all-start.1 = ((bf16[32,80,128]{2,1,0:T(8,128)(2,1)}), bf16[32,80,128]{2,1,0:T(8,128)(2,1)S(1)}, u32[]{:S(2)}, u32[]{:S(2)}) async-start(bf16[32,80,128]{2,1,0:T(8,128)(2,1)} %bitcast.2), calls=%async_computation.1 | async-start | bytes 1310720 | tf_op jit(solution)/shard_map/all_to_all | solution.py:311
  49.7 0.7 copy-start.14
  50.4 2.2 %copy-start.4 = (bf16[256,512]{1,0:T(8,128)(2,1)S(1)}, bf16[256,512]{1,0:T(8,128)(2,1)}, u32[]{:S(2)}) copy-start(bf16[256,512]{1,0:T(8,128)(2,1)} %query_ref.7) | copy-start | bytes 786436
  50.6 2.0 %copy-start.3 = (bf16[256,512]{1,0:T(8,128)(2,1)S(1)}, bf16[256,512]{1,0:T(8,128)(2,1)}, u32[]{:S(2)}) copy-start(bf16[256,512]{1,0:T(8,128)(2,1)} %value_ref.7) | copy-start | bytes 786436
  50.7 1.9 %copy-start.1 = (bf16[256,512]{1,0:T(8,128)(2,1)S(1)}, bf16[256,512]{1,0:T(8,128)(2,1)}, u32[]{:S(2)}) copy-start(bf16[256,512]{1,0:T(8,128)(2,1)} %key_ref.7) | copy-start | bytes 786436
  109.6 14.5 %all-to-all-start.4 = ((bf16[16,16,512]{2,1,0:T(8,128)(2,1)}), bf16[16,16,512]{2,1,0:T(8,128)(2,1)S(1)}, u32[]{:S(2)}, u32[]{:S(2)}) async-start(bf16[16,16,512]{2,1,0:T(8,128)(2,1)} %bitcast.7), calls=%async_computation.4 | async-start | bytes 524288 | tf_op jit(solution)/shard_map/all_to_all | solution.py:311
  115.2 0.7 copy-start.7
  124.1 0.7 copy-start.9
  124.1 5.3 %copy-start.8 = (bf16[256,512]{1,0:T(8,128)(2,1)S(1)}, bf16[256,512]{1,0:T(8,128)(2,1)}, u32[]{:S(2)}) copy-start(bf16[256,512]{1,0:T(8,128)(2,1)} %copy-done.7) | copy-start | bytes 786436
  124.8 24.8 %all-to-all-start.5 = ((bf16[32,80,128]{2,1,0:T(8,128)(2,1)}), bf16[32,80,128]{2,1,0:T(8,128)(2,1)S(1)}, u32[]{:S(2)}, u32[]{:S(2)}) async-start(bf16[32,80,128]{2,1,0:T(8,128)(2,1)} %bitcast.9), calls=%async_computation.5 | async-start | bytes 1310720 | tf_op jit(solution)/shard_map/all_to_all | solution.py:311
  135.9 0.8 copy-start.5
  149.6 18.7 %all-to-all-start.7 = ((f32[32,16,128]{2,1,0:T(8,128)}), f32[32,16,128]{2,1,0:T(8,128)S(1)}, u32[]{:S(2)}, u32[]{:S(2)}) async-start(f32[32,16,128]{2,1,0:T(8,128)} %get-tuple-element.34), calls=%async_computation.7 | async-start | bytes 524288 | tf_op jit(solution)/shard_map/all_to_all | solution.py:311
  155.7 17.3 %copy-start.12 = (f32[16,8,128]{2,1,0:T(8,128)S(1)}, f32[16,8,128]{2,1,0:T(8,128)}, u32[]{:S(2)}) copy-start(f32[16,8,128]{2,1,0:T(8,128)} %all_to_all.52) | copy-start | bytes 196612
  156.4 17.2 %copy-start.10 = (bf16[16,16,512]{2,1,0:T(8,128)(2,1)S(1)}, bf16[16,16,512]{2,1,0:T(8,128)(2,1)}, u32[]{:S(2)}) copy-start(bf16[16,16,512]{2,1,0:T(8,128)(2,1)} %copy-done.9) | copy-start | bytes 786436
  168.3 14.3 %all-to-all-start.6 = ((bf16[32,16,128]{2,1,0:T(8,128)(2,1)}), bf16[32,16,128]{2,1,0:T(8,128)(2,1)S(1)}, u32[]{:S(2)}, u32[]{:S(2)}) async-start(bf16[32,16,128]{2,1,0:T(8,128)(2,1)} %suffix_states.1), calls=%async_computation.6 | async-start | bytes 262144 | tf_op jit(solution)/shard_map/all_to_all | solution.py:311
  173.0 9.6 %copy-start.6 = (f32[256,512]{1,0:T(8,128)S(1)}, f32[256,512]{1,0:T(8,128)}, u32[]{:S(2)}) copy-start(f32[256,512]{1,0:T(8,128)} %copy-done.5) | copy-start | bytes 1572868

commit v2 on v1

v2 whole, which is shorter than its diff:
```python
import jax
import jax.numpy as jnp
from jax import lax
from jax.experimental import pallas as pl
from jax.experimental.pallas import tpu as pltpu
from jax.sharding import PartitionSpec as P

CH = 128
TABLE = 64
EPSILON = 1e-06
HIGHEST = lax.Precision.HIGHEST
F32 = jnp.float32
BF16 = jnp.bfloat16
INTERPRET = False


def call(kernel, out_shape, *operands):
    whole = pl.BlockSpec(memory_space=pltpu.VMEM)
    scalar = pl.BlockSpec(memory_space=pltpu.SMEM)
    return pl.pallas_call(
        kernel,
        out_shape=out_shape,
        in_specs=[scalar if operand.ndim == 1 else whole for operand in operands],
        interpret=INTERPRET,
        compiler_params=pltpu.CompilerParams(vmem_limit_bytes=48 * 1024 * 1024),
    )(*operands)


def shaped(shape, dtype):
    return jax.ShapeDtypeStruct(shape, dtype)


def dot_nn(a, b, precision=None):
    return lax.dot_general(a, b, (((1,), (0,)), ((), ())), precision=precision, preferred_element_type=F32)


def dot_nt(a, b):
    return lax.dot_general(a, b, (((1,), (1,)), ((), ())), preferred_element_type=F32)


def dot_tn(a, b, precision=None):
    return lax.dot_general(a, b, (((0,), (0,)), ((), ())), precision=precision, preferred_element_type=F32)


def causal_mask():
    rows = lax.broadcasted_iota(jnp.int32, (CH, CH), 0)
    cols = lax.broadcasted_iota(jnp.int32, (CH, CH), 1)
    return cols <= rows


def span_rows(c):
    return slice(c * CH, (c + 1) * CH)


def to_row(tile):
    return jnp.sum(tile.T, axis=0, keepdims=True)


def to_columns(row):
    return jnp.broadcast_to(row, (CH, CH)).T


def put_slices(ref, value, head, height, level=0):
    per_head = CH // height
    pieces = value.astype(BF16).reshape(per_head, height, value.shape[1])
    ref[head * per_head : (head + 1) * per_head, level * height : (level + 1) * height, :] = pieces


def get_slices(ref, head, height, level=0):
    per_head = CH // height
    pieces = ref[head * per_head : (head + 1) * per_head, level * height : (level + 1) * height, :]
    return pieces.reshape(CH, ref.shape[2])


def height_of(heads, ref):
    return heads * CH // ref.shape[0]


def split_pair(value):
    high = value.astype(BF16)
    return high, (value - high.astype(F32)).astype(BF16)


def state_kernel(key_ref, value_ref, total_ref, first_ref):
    heads = key_ref.shape[1] // CH
    for h in range(heads):
        cols = span_rows(h)
        first = dot_tn(key_ref[0:CH, cols], value_ref[0:CH, cols])
        second = dot_tn(key_ref[CH : 2 * CH, cols], value_ref[CH : 2 * CH, cols])
        first_ref[cols, :] = first.astype(BF16)
        put_slices(total_ref, first + second, h, total_ref.shape[1])


def prefix_kernel(in_ref, out_ref):
    shards, height = in_ref.shape[0], in_ref.shape[1]
    levels = out_ref.shape[1] // height
    sums = [in_ref[s].astype(F32) for s in range(shards)]
    zero = jnp.zeros(in_ref.shape[1:], BF16)
    for level in range(levels):
        rounded = [s.astype(BF16) for s in sums]
        for t in range(shards):
            group = t >> level
            out_ref[t, level * height : (level + 1) * height, :] = rounded[group - 1] if group & 1 else zero
        sums = [sums[2 * i] + sums[2 * i + 1] for i in range(len(sums) // 2)]


def suffix_kernel(place_ref, in_ref, table_ref, out_ref, gain_ref):
    shards = in_ref.shape[0]
    height = out_ref.shape[1] - table_ref.shape[0]
    levels = shards.bit_length() - 1
    rows = (in_ref.shape[1] - levels * height) // 2
    start = levels * height
    gain = in_ref[0, start : start + 2 * rows, :].astype(F32)
    for s in range(1, shards):
        gain = gain + in_ref[s, start : start + 2 * rows, :].astype(F32)
    gain = gain[:rows] + gain[rows:]
    for spot in range(gain_ref.shape[0] // rows):
        gain_ref[spot * rows : (spot + 1) * rows, :] = jnp.where(place_ref[0] == spot, gain, 0.0)
    carried = [None]
    for level in range(levels - 1, -1, -1):
        size = 1 << level
        groups = shards >> level
        below = []
        for g in range(groups):
            base = carried[g >> 1]
            if g & 1 == 0:
                total = None
                for s in range((g + 1) * size, (g + 2) * size):
                    piece = in_ref[s, level * height : (level + 1) * height, :].astype(F32)
                    total = piece if total is None else total + piece
                base = total if base is None else base + total
            below.append(base)
        carried = below
    zero = jnp.zeros((height, CH), F32)
    table = table_ref[...]
    for t in range(shards):
        value = zero if carried[t] is None else carried[t]
        out_ref[t, 0:height, :] = value.astype(BF16)
        out_ref[t, height:, :] = table


def onehot_of(index_ref, level):
    tokens = index_ref.shape[1]
    entry = lax.broadcasted_iota(jnp.int32, (TABLE, tokens), 0)
    return (index_ref[level : level + 1, :] == entry).astype(F32)


def weight_kernel(index_ref, table_ref, weight_ref):
    levels, tokens = index_ref.shape
    heads = table_ref.shape[1]
    rows = [dot_nn(table_ref[level], onehot_of(index_ref, level), HIGHEST) for level in range(levels)]
    rows.append(jnp.zeros((CH - levels * heads, tokens), F32))
    weight_ref[...] = jnp.concatenate(rows, axis=0).T


def near_kernel(query_ref, key_ref, value_ref, first_ref, weight_ref, out_ref):
    heads = query_ref.shape[1] // CH
    spans = query_ref.shape[0] // CH
    causal = causal_mask()
    for c in range(spans):
        rows = span_rows(c)
        for h in range(heads):
            cols = span_rows(h)
            query = query_ref[rows, cols]
            scores = jnp.where(causal, dot_nt(query, key_ref[rows, cols]), 0.0).astype(BF16)
            near = weight_ref[rows, h : h + 1] * dot_nn(scores, value_ref[rows, cols])
            if c == 1:
                near = near + weight_ref[rows, heads + h : heads + h + 1] * dot_nn(query, first_ref[cols, :])
            out_ref[rows, cols] = near


def spread_kernel(place_ref, in_ref, out_ref):
    width = out_ref.shape[2]
    for column in range(out_ref.shape[0]):
        out_ref[column ^ place_ref[0]] = in_ref[:, column * width : (column + 1) * width]


def collect_kernel(place_ref, in_ref, out_ref):
    width = in_ref.shape[2]
    for column in range(in_ref.shape[0]):
        out_ref[:, column * width : (column + 1) * width] = in_ref[column ^ place_ref[0]]


def span_block(place_ref, ref, c, cols):
    own = ref.shape[1]
    count = CH // own
    pieces = [ref[(c * count + i) ^ place_ref[0], :, cols] for i in range(count)]
    return jnp.concatenate(pieces, axis=0)


def far_kernel(place_ref, near_ref, query_ref, state_ref, weight_ref, cot_ref, gain_ref, attn_ref, stat_ref):
    heads = query_ref.shape[1] // CH
    spans = query_ref.shape[0] // CH
    height = height_of(heads, state_ref)
    levels = state_ref.shape[1] // height
    stats = []
    for c in range(spans):
        rows = span_rows(c)
        squares = jnp.zeros((CH, CH), F32)
        along = jnp.zeros((CH, CH), F32)
        for h in range(heads):
            cols = span_rows(h)
            query = query_ref[rows, cols]
            total = near_ref[rows, cols]
            for level in range(levels):
                spot = (level + 2) * heads + h
                total = total + weight_ref[rows, spot : spot + 1] * dot_nn(query, get_slices(state_ref, h, height, level))
            attn = total.astype(BF16)
            attn_ref[rows, cols] = attn
            attn_f = attn.astype(F32)
            scaled = span_block(place_ref, cot_ref, c, cols).astype(F32) * gain_ref[:, cols]
            squares = squares + attn_f * attn_f
            along = along + scaled * attn_f
        stats.append(to_row(squares))
        stats.append(to_row(along))
    block = jnp.concatenate(stats + [jnp.zeros((8 - len(stats), CH), F32)], axis=0)
    for d in range(stat_ref.shape[0]):
        stat_ref[d] = block


def norm_columns(stat_ref, features, c):
    total = stat_ref[0]
    for d in range(1, stat_ref.shape[0]):
        total = total + stat_ref[d]
    inv_rms = lax.rsqrt(total[2 * c : 2 * c + 1, :] / features + EPSILON)
    mean = total[2 * c + 1 : 2 * c + 2, :] * inv_rms / features
    return to_columns(inv_rms), to_columns(mean)


def grad_kernel(place_ref, attn_ref, stat_ref, cot_ref, gain_ref, query_ref, weight_ref, grad_ref, group_ref):
    heads = query_ref.shape[1] // CH
    spans = query_ref.shape[0] // CH
    height = height_of(heads, group_ref)
    levels = group_ref.shape[1] // height
    start = levels * height
    features = float(stat_ref.shape[0] * attn_ref.shape[1])
    norms = [norm_columns(stat_ref, features, c) for c in range(spans)]
    gain_parts = []
    for h in range(heads):
        cols = span_rows(h)
        parts = [[] for _ in range(levels)]
        gain_part = jnp.zeros((1, CH), F32)
        for c in range(spans):
            rows = span_rows(c)
            inv_rms, mean = norms[c]
            unit = attn_ref[rows, cols].astype(F32) * inv_rms
            cot = span_block(place_ref, cot_ref, c, cols).astype(F32)
            gain_part = gain_part + jnp.sum(cot * unit, axis=0, keepdims=True)
            scaled = cot * gain_ref[:, cols]
            grad = ((scaled - unit * mean) * inv_rms).astype(BF16)
            grad_ref[rows, cols] = grad
            grad_f = grad.astype(F32)
            for level in range(levels):
                spot = (level + 2) * heads + h
                parts[level].append((weight_ref[rows, spot : spot + 1] * grad_f).astype(BF16))
        query = query_ref[:, cols]
        for level in range(levels):
            put_slices(group_ref, dot_tn(query, jnp.concatenate(parts[level], axis=0)), h, height, level)
        gain_parts.append(gain_part)
    high, low = split_pair(jnp.concatenate(gain_parts, axis=0))
    block = jnp.concatenate([high, low], axis=0)
    for d in range(group_ref.shape[0]):
        group_ref[d, start:, :] = block


def norm_kernel(place_ref, attn_ref, stat_ref, gain_ref, normed_ref):
    heads = attn_ref.shape[1] // CH
    spans = attn_ref.shape[0] // CH
    features = float(stat_ref.shape[0] * attn_ref.shape[1])
    own = normed_ref.shape[1]
    for c in range(spans):
        rows = span_rows(c)
        inv_rms, _ = norm_columns(stat_ref, features, c)
        for h in range(heads):
            cols = span_rows(h)
            unit = attn_ref[rows, cols].astype(F32) * inv_rms
            normed = (unit * gain_ref[:, cols]).astype(BF16)
            for i in range(CH // own):
                normed_ref[(c * (CH // own) + i) ^ place_ref[0], :, cols] = normed[i * own : (i + 1) * own]


def back_kernel(
    query_ref, key_ref, value_ref, grad_ref, weight_ref, state_ref, first_ref, index_ref,
    dq_ref, dk_ref, dv_ref, inner_ref, table_ref, gw_ref,
):
    heads = query_ref.shape[1] // CH
    spans = query_ref.shape[0] // CH
    height = height_of(heads, state_ref)
    levels = state_ref.shape[1] // height
    all_levels = levels + 2
    causal = causal_mask()
    gw_ref[...] = jnp.zeros(gw_ref.shape, F32)
    for c in range(spans):
        rows = span_rows(c)
        for h in range(heads):
            cols = span_rows(h)
            query = query_ref[rows, cols]
            query_f = query.astype(F32)
            key = key_ref[rows, cols]
            grad = grad_ref[rows, cols]
            first_weight = weight_ref[rows, h : h + 1]
            scores = jnp.where(causal, dot_nt(query, key), 0.0)
            along = jnp.where(causal, dot_nt(grad, value_ref[rows, cols]), 0.0)
            gw_ref[rows, h : h + 1] = jnp.sum(scores.astype(BF16).astype(F32) * along, axis=1, keepdims=True)
            grad_scores = (along * first_weight).astype(BF16)
            weighted = (scores * first_weight).astype(BF16)
            dq = dot_nn(grad_scores, key)
            dk_ref[rows, cols] = dot_tn(grad_scores, query)
            dv_ref[rows, cols] = dot_tn(weighted, grad)
            if c == 1:
                spot = heads + h
                weight = weight_ref[rows, spot : spot + 1]
                far = dot_nt(grad, first_ref[cols, :])
                gw_ref[rows, spot : spot + 1] = jnp.sum(query_f * far, axis=1, keepdims=True)
                dq = dq + weight * far
                inner_ref[cols, :] = dot_tn(query, (weight * grad.astype(F32)).astype(BF16))
            for level in range(levels):
                spot = (level + 2) * heads + h
                far = dot_nt(grad, get_slices(state_ref, h, height, level))
                gw_ref[rows, spot : spot + 1] = jnp.sum(query_f * far, axis=1, keepdims=True)
                dq = dq + weight_ref[rows, spot : spot + 1] * far
            dq_ref[rows, cols] = dq.astype(BF16)
    grads = gw_ref[...].T
    blocks = []
    for level in range(all_levels):
        by_row = lax.dot_general(
            grads, onehot_of(index_ref, level), (((1,), (1,)), ((), ())), precision=HIGHEST, preferred_element_type=F32
        )
        blocks.append(by_row[level * heads : (level + 1) * heads])
    if all_levels % 2:
        blocks.append(jnp.zeros((heads, TABLE), F32))
    joined = [
        jnp.concatenate([blocks[2 * pair], blocks[2 * pair + 1]], axis=1) for pair in range(len(blocks) // 2)
    ]
    high, low = split_pair(jnp.concatenate(joined, axis=0))
    table_ref[...] = jnp.concatenate([high, low], axis=0)


def final_kernel(
    cross_ref, inner_ref, key_ref, value_ref, dk_ref, dv_ref, grad_key_ref, grad_value_ref, table_ref
):
    heads = key_ref.shape[1] // CH
    spans = key_ref.shape[0] // CH
    height = height_of(heads, cross_ref)
    half = (cross_ref.shape[1] - height) // 2
    total = cross_ref[0, height:, :].astype(F32)
    for s in range(1, cross_ref.shape[0]):
        total = total + cross_ref[s, height:, :].astype(F32)
    total = total[:half] + total[half:]
    for level in range(table_ref.shape[0]):
        top, left = (level // 2) * heads, (level % 2) * TABLE
        table_ref[level] = total[top : top + heads, left : left + TABLE]
    for h in range(heads):
        cols = span_rows(h)
        cross = get_slices(cross_ref, h, height)
        for c in range(spans):
            rows = span_rows(c)
            state = cross if c == 1 else (inner_ref[cols, :] + cross.astype(F32)).astype(BF16)
            grad_key = dk_ref[rows, cols] + dot_nt(value_ref[rows, cols], state)
            grad_value = dv_ref[rows, cols] + dot_nn(key_ref[rows, cols], state)
            grad_key_ref[rows, cols] = grad_key.astype(BF16)
            grad_value_ref[rows, cols] = grad_value.astype(BF16)


def exchange(value, axis):
    return lax.all_to_all(value, axis, split_axis=0, concat_axis=0, tiled=True)


def swapped(value, axis, bit):
    pairs = [(source, source ^ (1 << bit)) for source in range(lax.axis_size(axis))]
    return lax.ppermute(value, axis, pairs)


def gathered(slots):
    arrays = []
    for array, _ in slots:
        if not any(array is other for other in arrays):
            arrays.append(array)
    places = [(next(i for i, other in enumerate(arrays) if other is array), row) for array, row in slots]

    def pack_kernel(*refs):
        for spot, (source, row) in enumerate(places):
            refs[-1][spot] = refs[source][row]

    return call(pack_kernel, shaped((len(slots),) + arrays[0].shape[1:], arrays[0].dtype), *arrays)


def cube_exchange(value, axis):
    count = value.shape[0]
    slots = [(value, row) for row in range(count)]
    for bit in range(count.bit_length() - 2, -1, -1):
        moving = [row for row in range(count) if row >> bit & 1]
        received = swapped(gathered([slots[row] for row in moving]), axis, bit)
        for spot, row in enumerate(moving):
            slots[row] = (received, spot)
    return gathered(slots)


def body(queries, key_rows, value_rows, level_table, level_index, norm_gain, cotangent):
    tokens, width = queries.shape
    heads = level_table.shape[2]
    all_levels = level_table.shape[1]
    shards = lax.axis_size("seq")
    columns = lax.axis_size("head")
    levels = shards.bit_length() - 1
    height = heads * CH // shards
    own = tokens // columns
    pairs = (all_levels + 1) // 2
    place = lax.axis_index("head")
    spot = place.reshape(1)

    total, first = call(
        state_kernel, (shaped((shards, height, CH), BF16), shaped((heads * CH, CH), BF16)), key_rows, value_rows
    )
    slices = exchange(total, "seq")
    cot = call(spread_kernel, shaped((columns, own, width), BF16), spot, cotangent)
    cot = cube_exchange(cot, "head")
    gain = lax.dynamic_slice(norm_gain, (place * width,), (width,)).reshape(1, width)
    table = jnp.transpose(level_table, (1, 2, 0))
    index = jnp.transpose(level_index)
    weights = call(weight_kernel, shaped((tokens, CH), F32), index, table)
    near = call(near_kernel, shaped((tokens, width), F32), queries, key_rows, value_rows, first, weights)
    group_states = call(prefix_kernel, shaped((shards, levels * height, CH), BF16), slices)
    states = exchange(group_states, "seq")
    attn, stat = call(
        far_kernel,
        (shaped((tokens, width), BF16), shaped((columns, 8, CH), F32)),
        spot,
        near,
        queries,
        states,
        weights,
        cot,
        gain,
    )
    stats = exchange(stat, "head")
    grad, groups = call(
        grad_kernel,
        (shaped((tokens, width), BF16), shaped((shards, levels * height + 2 * heads, CH), BF16)),
        spot,
        attn,
        stats,
        cot,
        gain,
        queries,
        weights,
    )
    group_slices = exchange(groups, "seq")
    normed = call(norm_kernel, shaped((columns, own, width), BF16), spot, attn, stats, gain)
    normed = cube_exchange(normed, "head")
    normed = call(collect_kernel, shaped((own, columns * width), BF16), spot, normed)
    grad_query, near_dk, near_dv, inner, table_part, _ = call(
        back_kernel,
        (
            shaped((tokens, width), BF16),
            shaped((tokens, width), F32),
            shaped((tokens, width), F32),
            shaped((heads * CH, CH), F32),
            shaped((2 * pairs * heads, 2 * TABLE), BF16),
            shaped((tokens, CH), F32),
        ),
        queries,
        key_rows,
        value_rows,
        grad,
        weights,
        states,
        first,
        index,
    )
    key_slices, gain_sum = call(
        suffix_kernel,
        (
            shaped((shards, height + 2 * pairs * heads, CH), BF16),
            shaped((columns * heads, CH), F32),
        ),
        spot,
        group_slices,
        table_part,
    )
    cross = exchange(key_slices, "seq")
    for bit in range(columns.bit_length() - 1):
        gain_sum = gain_sum + swapped(gain_sum, "head", bit)
    grad_key, grad_value, table_sum = call(
        final_kernel,
        (
            shaped((tokens, width), BF16),
            shaped((tokens, width), BF16),
            shaped((all_levels, heads, TABLE), F32),
        ),
        cross,
        inner,
        key_rows,
        value_rows,
        near_dk,
        near_dv,
    )
    grad_table = jnp.transpose(table_sum, (2, 0, 1))
    return normed, grad_query, grad_key, grad_value, grad_table, gain_sum.reshape(columns * width)


def solution(mesh):
    placed = (
        P("seq", "head"),
        P("seq", "head"),
        P("seq", "head"),
        P(None, None, "head"),
        P("seq", None),
        P(),
        P(("seq", "head"), None),
    )
    return jax.shard_map(
        body,
        mesh=mesh,
        in_specs=placed,
        out_specs=(
            P(("seq", "head"), None),
            P("seq", "head"),
            P("seq", "head"),
            P("seq", "head"),
            P(None, None, "head"),
            P(),
        ),
        check_vma=False,
    )
```

time: 185 us -> 177 us (0.957)
  the two profiles are of different devices: /device:TPU:8 before, /device:TPU:2 now
where the time goes in v2:
time: 177 us; the launch traced here: 176 us
  starting transfers between devices  59.8 us (34%)
  waiting for transfers between devices  59.4 us (34%)
  blocking collectives  35.6 us (20%)
  Pallas kernels  13.6 us (8%)
  local copies, waits for them, and re-layouts  5.51 us (3%)
    ppermute x12, waiting for transfers between devices, swapped(): return lax.ppermute(value, axis, pairs)  44.8 us
    ppermute x12, starting transfers between devices, swapped(): return lax.ppermute(value, axis, pairs)  38.8 us
    all_to_all x2, blocking collectives, exchange(): return lax.all_to_all(value, axis, split_axis=0, concat_axis=0, tiled=True)  35.6 us
    all_to_all x3, starting transfers between devices, exchange(): return lax.all_to_all(value, axis, split_axis=0, concat_axis=0, tiled=True)  21 us
    all_to_all x3, waiting for transfers between devices, exchange(): return lax.all_to_all(value, axis, split_axis=0, concat_axis=0, tiled=True)  14.6 us
    pallas_call x22, Pallas kernels, call(): pl.pallas_call(kernel, out_shape=out_shape, in_specs=[scalar if operand.n...  13.6 us
    unnamed x28, local copies, waits for them, and re-layouts  4.74 us
  transfers between devices with their start and end apart: 15, of which 10 were waited for; matrix products, arithmetic and copies ran while one was open for 1% of the time, Pallas kernels for 4%

profile of v2, /device:TPU:2, one launch (start us, length us, event | category | flops | bytes accessed | tf_op | source)
XLA Modules:
  0.0 175.6 jit_solution(10968267239970428008)
XLA Ops:
  0.6 0.0 copy-start.1
  0.6 0.9 copy-done.1
  1.6 0.9 copy-done.3
  2.5 0.3 shard_map.118
  2.8 18.9 %all_to_all.25.in_ref = bf16[32,16,128]{2,1,0:T(8,128)(2,1)S(1)} all-to-all(bf16[32,16,128]{2,1,0:T(8,128)(2,1)S(1)} %get-tuple-element.23), channel_id=1, replica_groups=mesh['seq'=32,'head'=16] {'seq'}, dimensions={0} | all-to-all | bytes 262144 | tf_op jit(solution)/shard_map/all_to_all | solution.py:366
  21.7 0.9 shard_map.121
  22.6 5.6 %all-to-all-start.1 = ((bf16[32,80,128]{2,1,0:T(8,128)(2,1)}), bf16[32,80,128]{2,1,0:T(8,128)(2,1)S(1)}, u32[]{:S(2)}, u32[]{:S(2)}) async-start(bf16[32,80,128]{2,1,0:T(8,128)(2,1)} %shard_map.121), calls=%async_computation.1 | async-start | bytes 1310720 | tf_op jit(solution)/shard_map/all_to_all | solution.py:366
  28.3 10.9 %collective-permute-start = (bf16[8,16,512]{2,1,0:T(8,128)(2,1)S(1)}, bf16[8,16,512]{2,1,0:T(8,128)(2,1)S(1)}, u32[]{:S(2)}, u32[]{:S(2)}) collective-permute-start(bf16[8,16,512]{2,1,0:T(8,128)(2,1)S(1)} %shard_map.123), channel_id=1, source_target_pairs={{0,8},{1,9},{2,10},{3,11},{4,12},{5,13},{6,14},{7,15},{8,0},{9,1},... | collective-permute-start | bytes 393224 | tf_op jit(solution)/shard_map/ppermute | solution.py:371
  39.2 4.0 %collective-permute-done.refs_1_.refs_2_.refs_3_.refs_4_ = bf16[8,16,512]{2,1,0:T(8,128)(2,1)S(1)} collective-permute-done((bf16[8,16,512]{2,1,0:T(8,128)(2,1)S(1)}, bf16[8,16,512]{2,1,0:T(8,128)(2,1)S(1)}, u32[]{:S(2)}, u32[]{:S(2)}) %collective-permute-start) | collective-permute-done | bytes 131104 | tf_op jit(solution)/shard_map/ppermute | solution.py:371
  43.2 4.9 %collective-permute-start.1 = (bf16[8,16,512]{2,1,0:T(8,128)(2,1)S(1)}, bf16[8,16,512]{2,1,0:T(8,128)(2,1)S(1)}, u32[]{:S(2)}, u32[]{:S(2)}) collective-permute-start(bf16[8,16,512]{2,1,0:T(8,128)(2,1)S(1)} %shard_map.124), channel_id=1, source_target_pairs={{0,4},{1,5},{2,6},{3,7},{4,0},{5,1},{6,2},{7,3},{8,12},{9,13},{10,... | collective-permute-start | bytes 393224 | tf_op jit(solution)/shard_map/ppermute | solution.py:371
  48.2 2.9 %collective-permute-done.1.refs_1_.refs_2_.refs_3_ = bf16[8,16,512]{2,1,0:T(8,128)(2,1)S(1)} collective-permute-done((bf16[8,16,512]{2,1,0:T(8,128)(2,1)S(1)}, bf16[8,16,512]{2,1,0:T(8,128)(2,1)S(1)}, u32[]{:S(2)}, u32[]{:S(2)}) %collective-permute-start.1) | collective-permute-done | bytes 131104 | tf_op jit(solution)/shard_map/ppermute | solution.py:371
  51.1 3.9 %collective-permute-start.2 = (bf16[8,16,512]{2,1,0:T(8,128)(2,1)S(1)}, bf16[8,16,512]{2,1,0:T(8,128)(2,1)S(1)}, u32[]{:S(2)}, u32[]{:S(2)}) collective-permute-start(bf16[8,16,512]{2,1,0:T(8,128)(2,1)S(1)} %shard_map.125), channel_id=1, source_target_pairs={{0,2},{1,3},{2,0},{3,1},{4,6},{5,7},{6,4},{7,5},{8,10},{9,11},{10,... | collective-permute-start | bytes 393224 | tf_op jit(solution)/shard_map/ppermute | solution.py:371
  55.1 2.9 %collective-permute-done.2.refs_1_.refs_2_ = bf16[8,16,512]{2,1,0:T(8,128)(2,1)S(1)} collective-permute-done((bf16[8,16,512]{2,1,0:T(8,128)(2,1)S(1)}, bf16[8,16,512]{2,1,0:T(8,128)(2,1)S(1)}, u32[]{:S(2)}, u32[]{:S(2)}) %collective-permute-start.2) | collective-permute-done | bytes 131104 | tf_op jit(solution)/shard_map/ppermute | solution.py:371
  58.0 2.1 %collective-permute-start.3 = (bf16[8,16,512]{2,1,0:T(8,128)(2,1)S(1)}, bf16[8,16,512]{2,1,0:T(8,128)(2,1)S(1)}, u32[]{:S(2)}, u32[]{:S(2)}) collective-permute-start(bf16[8,16,512]{2,1,0:T(8,128)(2,1)S(1)} %shard_map.126), channel_id=1, source_target_pairs={{0,1},{1,0},{2,3},{3,2},{4,5},{5,4},{6,7},{7,6},{8,9},{9,8},{10,11... | collective-permute-start | bytes 393224 | tf_op jit(solution)/shard_map/ppermute | solution.py:371
  60.1 0.8 dynamic_slice.3
  60.9 0.4 shard_map.119.weight_ref
  61.3 1.0 shard_map.120.near_ref
  62.4 1.0 shard_map.128
  63.4 16.7 %all_to_all.26.stat_ref = f32[16,8,128]{2,1,0:T(8,128)S(1)} all-to-all(f32[16,8,128]{2,1,0:T(8,128)S(1)} %get-tuple-element.25), channel_id=1, replica_groups=mesh['seq'=32,'head'=16] {'head'}, dimensions={0} | all-to-all | bytes 131072 | tf_op jit(solution)/shard_map/all_to_all | solution.py:366
  80.1 2.2 %shard_map.136 = (bf16[256,512]{1,0:T(8,128)(2,1)S(1)}, bf16[32,88,128]{2,1,0:T(8,128)(2,1)}) custom-call(s32[1]{0:T(128)} %bitcast.place_ref, bf16[256,512]{1,0:T(8,128)(2,1)S(1)} %get-tuple-element.24.attn_ref, f32[16,8,128]{2,1,0:T(8,128)S(1)} %all_to_all.26.stat_ref, bf16[16,16,512]{2,1,0:T(8,128)(2,1)S(1)} %shard_map.127.cot_ref, f32[1,512]{1,0:T(1,128)S(1)} %bitcast.8, ...), custom_call_target="tpu_custom_call" | custom-call | tf_op jit(solution)/shard_map/pallas_call | solution.py:20
  82.3 9.9 %all-to-all-start.3 = ((bf16[32,88,128]{2,1,0:T(8,128)(2,1)}), bf16[32,88,128]{2,1,0:T(8,128)(2,1)S(1)}, u32[]{:S(2)}, u32[]{:S(2)}) async-start(bf16[32,88,128]{2,1,0:T(8,128)(2,1)} %get-tuple-element.28), calls=%async_computation.3 | async-start | bytes 1441792 | tf_op jit(solution)/shard_map/all_to_all | solution.py:366
  92.2 4.8 %shard_map.137 = (bf16[256,512]{1,0:T(8,128)(2,1)}, f32[256,512]{1,0:T(8,128)S(1)}, f32[256,512]{1,0:T(8,128)S(1)}, f32[512,128]{1,0:T(8,128)S(1)}, bf16[32,128]{1,0:T(8,128)(2,1)S(1)}, /*index=5*/f32[256,128]{1,0:T(8,128)}) custom-call(bf16[256,512]{1,0:T(8,128)(2,1)S(1)} %copy-done, bf16[256,512]{1,0:T(8,128)(2,1)S(1)} %copy-done.2, ...), custom_call_target="tpu_custom_call" | custom-call | tf_op jit(solution)/shard_map/pallas_call | solution.py:20
  97.0 0.8 copy-done.5
  97.8 0.7 copy-done.7
  98.5 0.6 copy-done.12
  99.1 14.6 %all-to-all-done.3.in_ref = bf16[32,88,128]{2,1,0:T(8,128)(2,1)S(1)} async-done(((bf16[32,88,128]{2,1,0:T(8,128)(2,1)}), bf16[32,88,128]{2,1,0:T(8,128)(2,1)S(1)}, u32[]{:S(2)}, u32[]{:S(2)}) %all-to-all-start.3) | async-done | bytes 720928 | tf_op jit(solution)/shard_map/all_to_all | solution.py:366
  113.8 0.7 copy-done.13
  114.5 0.8 shard_map.138
  115.3 5.6 %all-to-all-start.4 = ((bf16[32,48,128]{2,1,0:T(8,128)(2,1)}), bf16[32,48,128]{2,1,0:T(8,128)(2,1)S(1)}, u32[]{:S(2)}, u32[]{:S(2)}) async-start(bf16[32,48,128]{2,1,0:T(8,128)(2,1)} %get-tuple-element.30), calls=%async_computation.4 | async-start | bytes 786432 | tf_op jit(solution)/shard_map/all_to_all | solution.py:366
  120.8 0.2 shard_map.129.refs_0_
  121.0 2.8 %collective-permute-start.4 = (bf16[8,16,512]{2,1,0:T(8,128)(2,1)S(1)}, bf16[8,16,512]{2,1,0:T(8,128)(2,1)S(1)}, u32[]{:S(2)}, u32[]{:S(2)}) collective-permute-start(bf16[8,16,512]{2,1,0:T(8,128)(2,1)S(1)} %shard_map.130), channel_id=1, source_target_pairs={{0,8},{1,9},{2,10},{3,11},{4,12},{5,13},{6,14},{7,15},{8,0},{9,1},... | collective-permute-start | bytes 393224 | tf_op jit(solution)/shard_map/ppermute | solution.py:371
  123.8 9.7 %collective-permute-done.4.refs_1_.refs_2_.refs_3_.refs_4_ = bf16[8,16,512]{2,1,0:T(8,128)(2,1)S(1)} collective-permute-done((bf16[8,16,512]{2,1,0:T(8,128)(2,1)S(1)}, bf16[8,16,512]{2,1,0:T(8,128)(2,1)S(1)}, u32[]{:S(2)}, u32[]{:S(2)}) %collective-permute-start.4) | collective-permute-done | bytes 131104 | tf_op jit(solution)/shard_map/ppermute | solution.py:371
  133.5 2.1 %collective-permute-start.5 = (bf16[8,16,512]{2,1,0:T(8,128)(2,1)S(1)}, bf16[8,16,512]{2,1,0:T(8,128)(2,1)S(1)}, u32[]{:S(2)}, u32[]{:S(2)}) collective-permute-start(bf16[8,16,512]{2,1,0:T(8,128)(2,1)S(1)} %shard_map.131), channel_id=1, source_target_pairs={{0,4},{1,5},{2,6},{3,7},{4,0},{5,1},{6,2},{7,3},{8,12},{9,13},{10,... | collective-permute-start | bytes 393224 | tf_op jit(solution)/shard_map/ppermute | solution.py:371
  135.6 7.1 %collective-permute-done.5.refs_1_.refs_2_.refs_3_ = bf16[8,16,512]{2,1,0:T(8,128)(2,1)S(1)} collective-permute-done((bf16[8,16,512]{2,1,0:T(8,128)(2,1)S(1)}, bf16[8,16,512]{2,1,0:T(8,128)(2,1)S(1)}, u32[]{:S(2)}, u32[]{:S(2)}) %collective-permute-start.5) | collective-permute-done | bytes 131104 | tf_op jit(solution)/shard_map/ppermute | solution.py:371
  142.7 1.9 %collective-permute-start.6 = (bf16[8,16,512]{2,1,0:T(8,128)(2,1)S(1)}, bf16[8,16,512]{2,1,0:T(8,128)(2,1)S(1)}, u32[]{:S(2)}, u32[]{:S(2)}) collective-permute-start(bf16[8,16,512]{2,1,0:T(8,128)(2,1)S(1)} %shard_map.132), channel_id=1, source_target_pairs={{0,2},{1,3},{2,0},{3,1},{4,6},{5,7},{6,4},{7,5},{8,10},{9,11},{10,... | collective-permute-start | bytes 393224 | tf_op jit(solution)/shard_map/ppermute | solution.py:371
  144.7 1.9 %collective-permute-start.8 = (f32[64,128]{1,0:T(8,128)S(1)}, f32[64,128]{1,0:T(8,128)S(1)}, u32[]{:S(2)}, u32[]{:S(2)}) collective-permute-start(f32[64,128]{1,0:T(8,128)S(1)} %get-tuple-element.37), channel_id=1, source_target_pairs={{0,1},{1,0},{2,3},{3,2},{4,5},{5,4},{6,7},{7,6},{8,9},{9,8},{10,11... | collective-permute-start | bytes 98312 | tf_op jit(solution)/shard_map/ppermute | solution.py:371
  146.6 3.0 %collective-permute-done.6.refs_1_.refs_2_ = bf16[8,16,512]{2,1,0:T(8,128)(2,1)S(1)} collective-permute-done((bf16[8,16,512]{2,1,0:T(8,128)(2,1)S(1)}, bf16[8,16,512]{2,1,0:T(8,128)(2,1)S(1)}, u32[]{:S(2)}, u32[]{:S(2)}) %collective-permute-start.6) | collective-permute-done | bytes 131104 | tf_op jit(solution)/shard_map/ppermute | solution.py:371
  149.6 1.9 %collective-permute-start.7 = (bf16[8,16,512]{2,1,0:T(8,128)(2,1)S(1)}, bf16[8,16,512]{2,1,0:T(8,128)(2,1)S(1)}, u32[]{:S(2)}, u32[]{:S(2)}) collective-permute-start(bf16[8,16,512]{2,1,0:T(8,128)(2,1)S(1)} %shard_map.133), channel_id=1, source_target_pairs={{0,1},{1,0},{2,3},{3,2},{4,5},{5,4},{6,7},{7,6},{8,9},{9,8},{10,11... | collective-permute-start | bytes 393224 | tf_op jit(solution)/shard_map/ppermute | solution.py:371
  151.6 1.9 %collective-permute-start.9 = (f32[64,128]{1,0:T(8,128)S(1)}, f32[64,128]{1,0:T(8,128)S(1)}, u32[]{:S(2)}, u32[]{:S(2)}) collective-permute-start(f32[64,128]{1,0:T(8,128)S(1)} %add.16), channel_id=1, source_target_pairs={{0,2},{1,3},{2,0},{3,1},{4,6},{5,7},{6,4},{7,5},{8,10},{9,11},{10,... | collective-permute-start | bytes 98312 | tf_op jit(solution)/shard_map/ppermute | solution.py:371
  153.5 3.9 %collective-permute-done.9 = f32[64,128]{1,0:T(8,128)S(1)} collective-permute-done((f32[64,128]{1,0:T(8,128)S(1)}, f32[64,128]{1,0:T(8,128)S(1)}, u32[]{:S(2)}, u32[]{:S(2)}) %collective-permute-start.9) | collective-permute-done | bytes 32800 | tf_op jit(solution)/shard_map/ppermute | solution.py:371
  157.4 1.9 %collective-permute-start.10 = (f32[64,128]{1,0:T(8,128)S(1)}, f32[64,128]{1,0:T(8,128)S(1)}, u32[]{:S(2)}, u32[]{:S(2)}) collective-permute-start(f32[64,128]{1,0:T(8,128)S(1)} %add.17), channel_id=1, source_target_pairs={{0,4},{1,5},{2,6},{3,7},{4,0},{5,1},{6,2},{7,3},{8,12},{9,13},{10,... | collective-permute-start | bytes 98312 | tf_op jit(solution)/shard_map/ppermute | solution.py:371
  159.3 4.8 %collective-permute-done.10 = f32[64,128]{1,0:T(8,128)S(1)} collective-permute-done((f32[64,128]{1,0:T(8,128)S(1)}, f32[64,128]{1,0:T(8,128)S(1)}, u32[]{:S(2)}, u32[]{:S(2)}) %collective-permute-start.10) | collective-permute-done | bytes 32800 | tf_op jit(solution)/shard_map/ppermute | solution.py:371
  164.1 2.5 %collective-permute-start.11 = (f32[64,128]{1,0:T(8,128)S(1)}, f32[64,128]{1,0:T(8,128)S(1)}, u32[]{:S(2)}, u32[]{:S(2)}) collective-permute-start(f32[64,128]{1,0:T(8,128)S(1)} %add.18), channel_id=1, source_target_pairs={{0,8},{1,9},{2,10},{3,11},{4,12},{5,13},{6,14},{7,15},{8,0},{9,1},... | collective-permute-start | bytes 98312 | tf_op jit(solution)/shard_map/ppermute | solution.py:371
  166.6 0.0 copy-start.8
  166.6 0.7 shard_map.135
  167.4 6.4 %collective-permute-done.11 = f32[64,128]{1,0:T(8,128)S(1)} collective-permute-done((f32[64,128]{1,0:T(8,128)S(1)}, f32[64,128]{1,0:T(8,128)S(1)}, u32[]{:S(2)}, u32[]{:S(2)}) %collective-permute-start.11) | collective-permute-done | bytes 32800 | tf_op jit(solution)/shard_map/ppermute | solution.py:371
  173.8 0.6 add_bitcast_fusion
  174.4 1.2 shard_map.139
  (39 shorter events, 0.2 us)
Async XLA Ops:
  0.6 1.0 copy-start.1
  1.6 0.9 copy-start.3
  22.6 5.6 %copy-start.9 = (bf16[16,8192]{1,0:T(8,128)(2,1)S(1)}, bf16[16,8192]{1,0:T(8,128)(2,1)}, u32[]{:S(2)}) copy-start(bf16[16,8192]{1,0:T(8,128)(2,1)} %in_ref.1) | copy-start | bytes 786436
  22.6 39.8 %all-to-all-start.1 = ((bf16[32,80,128]{2,1,0:T(8,128)(2,1)}), bf16[32,80,128]{2,1,0:T(8,128)(2,1)S(1)}, u32[]{:S(2)}, u32[]{:S(2)}) async-start(bf16[32,80,128]{2,1,0:T(8,128)(2,1)} %shard_map.121), calls=%async_computation.1 | async-start | bytes 1310720 | tf_op jit(solution)/shard_map/all_to_all | solution.py:366
  28.3 15.0 %collective-permute-start = (bf16[8,16,512]{2,1,0:T(8,128)(2,1)S(1)}, bf16[8,16,512]{2,1,0:T(8,128)(2,1)S(1)}, u32[]{:S(2)}, u32[]{:S(2)}) collective-permute-start(bf16[8,16,512]{2,1,0:T(8,128)(2,1)S(1)} %shard_map.123), channel_id=1, source_target_pairs={{0,8},{1,9},{2,10},{3,11},{4,12},{5,13},{6,14},{7,15},{8,0},{9,1},... | collective-permute-start | bytes 393224 | tf_op jit(solution)/shard_map/ppermute | solution.py:371
  43.2 7.9 %collective-permute-start.1 = (bf16[8,16,512]{2,1,0:T(8,128)(2,1)S(1)}, bf16[8,16,512]{2,1,0:T(8,128)(2,1)S(1)}, u32[]{:S(2)}, u32[]{:S(2)}) collective-permute-start(bf16[8,16,512]{2,1,0:T(8,128)(2,1)S(1)} %shard_map.124), channel_id=1, source_target_pairs={{0,4},{1,5},{2,6},{3,7},{4,0},{5,1},{6,2},{7,3},{8,12},{9,13},{10,... | collective-permute-start | bytes 393224 | tf_op jit(solution)/shard_map/ppermute | solution.py:371
  51.1 9.8 %copy-start.11 = (f32[64,7,4]{0,2,1:T(4,128)S(1)}, f32[64,7,4]{0,2,1:T(4,128)}, u32[]{:S(2)}) copy-start(f32[64,7,4]{0,2,1:T(4,128)} %param.10) | copy-start | bytes 21508
  51.1 6.9 %collective-permute-start.2 = (bf16[8,16,512]{2,1,0:T(8,128)(2,1)S(1)}, bf16[8,16,512]{2,1,0:T(8,128)(2,1)S(1)}, u32[]{:S(2)}, u32[]{:S(2)}) collective-permute-start(bf16[8,16,512]{2,1,0:T(8,128)(2,1)S(1)} %shard_map.125), channel_id=1, source_target_pairs={{0,2},{1,3},{2,0},{3,1},{4,6},{5,7},{6,4},{7,5},{8,10},{9,11},{10,... | collective-permute-start | bytes 393224 | tf_op jit(solution)/shard_map/ppermute | solution.py:371
  58.0 3.3 %copy-start = (bf16[256,512]{1,0:T(8,128)(2,1)S(1)}, bf16[256,512]{1,0:T(8,128)(2,1)}, u32[]{:S(2)}) copy-start(bf16[256,512]{1,0:T(8,128)(2,1)} %query_ref.7) | copy-start | bytes 786436
  58.0 3.3 %copy-start.2 = (bf16[256,512]{1,0:T(8,128)(2,1)S(1)}, bf16[256,512]{1,0:T(8,128)(2,1)}, u32[]{:S(2)}) copy-start(bf16[256,512]{1,0:T(8,128)(2,1)} %key_ref.7) | copy-start | bytes 786436
  58.0 3.3 %copy-start.4 = (bf16[256,512]{1,0:T(8,128)(2,1)S(1)}, bf16[256,512]{1,0:T(8,128)(2,1)}, u32[]{:S(2)}) copy-start(bf16[256,512]{1,0:T(8,128)(2,1)} %value_ref.7) | copy-start | bytes 786436
  58.0 2.8 %copy-start.10 = (s32[256,7]{0,1:T(8,128)S(1)}, s32[256,7]{0,1:T(8,128)}, u32[]{:S(2)}) copy-start(s32[256,7]{0,1:T(8,128)} %param.11) | copy-start | bytes 21508
  58.0 4.3 %collective-permute-start.3 = (bf16[8,16,512]{2,1,0:T(8,128)(2,1)S(1)}, bf16[8,16,512]{2,1,0:T(8,128)(2,1)S(1)}, u32[]{:S(2)}, u32[]{:S(2)}) collective-permute-start(bf16[8,16,512]{2,1,0:T(8,128)(2,1)S(1)} %shard_map.126), channel_id=1, source_target_pairs={{0,1},{1,0},{2,3},{3,2},{4,5},{5,4},{6,7},{7,6},{8,9},{9,8},{10,11... | collective-permute-start | bytes 393224 | tf_op jit(solution)/shard_map/ppermute | solution.py:371
  82.3 31.5 %all-to-all-start.3 = ((bf16[32,88,128]{2,1,0:T(8,128)(2,1)}), bf16[32,88,128]{2,1,0:T(8,128)(2,1)S(1)}, u32[]{:S(2)}, u32[]{:S(2)}) async-start(bf16[32,88,128]{2,1,0:T(8,128)(2,1)} %get-tuple-element.28), calls=%async_computation.3 | async-start | bytes 1441792 | tf_op jit(solution)/shard_map/all_to_all | solution.py:366
  97.0 0.8 copy-start.5
  97.8 0.7 copy-start.7
  98.5 0.6 copy-start.12
  113.8 0.7 copy-start.13
  115.3 59.1 %all-to-all-start.4 = ((bf16[32,48,128]{2,1,0:T(8,128)(2,1)}), bf16[32,48,128]{2,1,0:T(8,128)(2,1)S(1)}, u32[]{:S(2)}, u32[]{:S(2)}) async-start(bf16[32,48,128]{2,1,0:T(8,128)(2,1)} %get-tuple-element.30), calls=%async_computation.4 | async-start | bytes 786432 | tf_op jit(solution)/shard_map/all_to_all | solution.py:366
  121.0 12.5 %collective-permute-start.4 = (bf16[8,16,512]{2,1,0:T(8,128)(2,1)S(1)}, bf16[8,16,512]{2,1,0:T(8,128)(2,1)S(1)}, u32[]{:S(2)}, u32[]{:S(2)}) collective-permute-start(bf16[8,16,512]{2,1,0:T(8,128)(2,1)S(1)} %shard_map.130), channel_id=1, source_target_pairs={{0,8},{1,9},{2,10},{3,11},{4,12},{5,13},{6,14},{7,15},{8,0},{9,1},... | collective-permute-start | bytes 393224 | tf_op jit(solution)/shard_map/ppermute | solution.py:371
  133.5 9.2 %collective-permute-start.5 = (bf16[8,16,512]{2,1,0:T(8,128)(2,1)S(1)}, bf16[8,16,512]{2,1,0:T(8,128)(2,1)S(1)}, u32[]{:S(2)}, u32[]{:S(2)}) collective-permute-start(bf16[8,16,512]{2,1,0:T(8,128)(2,1)S(1)} %shard_map.131), channel_id=1, source_target_pairs={{0,4},{1,5},{2,6},{3,7},{4,0},{5,1},{6,2},{7,3},{8,12},{9,13},{10,... | collective-permute-start | bytes 393224 | tf_op jit(solution)/shard_map/ppermute | solution.py:371
  142.7 6.9 %collective-permute-start.6 = (bf16[8,16,512]{2,1,0:T(8,128)(2,1)S(1)}, bf16[8,16,512]{2,1,0:T(8,128)(2,1)S(1)}, u32[]{:S(2)}, u32[]{:S(2)}) collective-permute-start(bf16[8,16,512]{2,1,0:T(8,128)(2,1)S(1)} %shard_map.132), channel_id=1, source_target_pairs={{0,2},{1,3},{2,0},{3,1},{4,6},{5,7},{6,4},{7,5},{8,10},{9,11},{10,... | collective-permute-start | bytes 393224 | tf_op jit(solution)/shard_map/ppermute | solution.py:371
  144.7 6.9 %collective-permute-start.8 = (f32[64,128]{1,0:T(8,128)S(1)}, f32[64,128]{1,0:T(8,128)S(1)}, u32[]{:S(2)}, u32[]{:S(2)}) collective-permute-start(f32[64,128]{1,0:T(8,128)S(1)} %get-tuple-element.37), channel_id=1, source_target_pairs={{0,1},{1,0},{2,3},{3,2},{4,5},{5,4},{6,7},{7,6},{8,9},{9,8},{10,11... | collective-permute-start | bytes 98312 | tf_op jit(solution)/shard_map/ppermute | solution.py:371
  149.6 17.0 %collective-permute-start.7 = (bf16[8,16,512]{2,1,0:T(8,128)(2,1)S(1)}, bf16[8,16,512]{2,1,0:T(8,128)(2,1)S(1)}, u32[]{:S(2)}, u32[]{:S(2)}) collective-permute-start(bf16[8,16,512]{2,1,0:T(8,128)(2,1)S(1)} %shard_map.133), channel_id=1, source_target_pairs={{0,1},{1,0},{2,3},{3,2},{4,5},{5,4},{6,7},{7,6},{8,9},{9,8},{10,11... | collective-permute-start | bytes 393224 | tf_op jit(solution)/shard_map/ppermute | solution.py:371
  151.6 5.8 %collective-permute-start.9 = (f32[64,128]{1,0:T(8,128)S(1)}, f32[64,128]{1,0:T(8,128)S(1)}, u32[]{:S(2)}, u32[]{:S(2)}) collective-permute-start(f32[64,128]{1,0:T(8,128)S(1)} %add.16), channel_id=1, source_target_pairs={{0,2},{1,3},{2,0},{3,1},{4,6},{5,7},{6,4},{7,5},{8,10},{9,11},{10,... | collective-permute-start | bytes 98312 | tf_op jit(solution)/shard_map/ppermute | solution.py:371
  157.4 6.7 %collective-permute-start.10 = (f32[64,128]{1,0:T(8,128)S(1)}, f32[64,128]{1,0:T(8,128)S(1)}, u32[]{:S(2)}, u32[]{:S(2)}) collective-permute-start(f32[64,128]{1,0:T(8,128)S(1)} %add.17), channel_id=1, source_target_pairs={{0,4},{1,5},{2,6},{3,7},{4,0},{5,1},{6,2},{7,3},{8,12},{9,13},{10,... | collective-permute-start | bytes 98312 | tf_op jit(solution)/shard_map/ppermute | solution.py:371
  164.1 9.7 %collective-permute-start.11 = (f32[64,128]{1,0:T(8,128)S(1)}, f32[64,128]{1,0:T(8,128)S(1)}, u32[]{:S(2)}, u32[]{:S(2)}) collective-permute-start(f32[64,128]{1,0:T(8,128)S(1)} %add.18), channel_id=1, source_target_pairs={{0,8},{1,9},{2,10},{3,11},{4,12},{5,13},{6,14},{7,15},{8,0},{9,1},... | collective-permute-start | bytes 98312 | tf_op jit(solution)/shard_map/ppermute | solution.py:371
  166.6 7.8 %copy-start.8 = (f32[512,128]{1,0:T(8,128)S(1)}, f32[512,128]{1,0:T(8,128)}, u32[]{:S(2)}) copy-start(f32[512,128]{1,0:T(8,128)} %copy-done.7) | copy-start | bytes 786436
  166.6 7.8 %copy-start.6 = (f32[256,512]{1,0:T(8,128)S(1)}, f32[256,512]{1,0:T(8,128)}, u32[]{:S(2)}) copy-start(f32[256,512]{1,0:T(8,128)} %copy-done.5) | copy-start | bytes 1572868

commit v3 on v2

v3 whole, which is shorter than its diff:
```python
import jax
import jax.numpy as jnp
from jax import lax
from jax.experimental import pallas as pl
from jax.experimental.pallas import tpu as pltpu
from jax.sharding import PartitionSpec as P

CH = 128
TABLE = 64
EPSILON = 1e-06
HIGHEST = lax.Precision.HIGHEST
F32 = jnp.float32
BF16 = jnp.bfloat16
INTERPRET = False


def call(kernel, out_shape, *operands):
    whole = pl.BlockSpec(memory_space=pltpu.VMEM)
    scalar = pl.BlockSpec(memory_space=pltpu.SMEM)
    return pl.pallas_call(
        kernel,
        out_shape=out_shape,
        in_specs=[scalar if operand.ndim == 1 else whole for operand in operands],
        interpret=INTERPRET,
        compiler_params=pltpu.CompilerParams(vmem_limit_bytes=48 * 1024 * 1024),
    )(*operands)


def shaped(shape, dtype):
    return jax.ShapeDtypeStruct(shape, dtype)


def dot_nn(a, b, precision=None):
    return lax.dot_general(a, b, (((1,), (0,)), ((), ())), precision=precision, preferred_element_type=F32)


def dot_nt(a, b):
    return lax.dot_general(a, b, (((1,), (1,)), ((), ())), preferred_element_type=F32)


def dot_tn(a, b, precision=None):
    return lax.dot_general(a, b, (((0,), (0,)), ((), ())), precision=precision, preferred_element_type=F32)


def causal_mask():
    rows = lax.broadcasted_iota(jnp.int32, (CH, CH), 0)
    cols = lax.broadcasted_iota(jnp.int32, (CH, CH), 1)
    return cols <= rows


def span_rows(c):
    return slice(c * CH, (c + 1) * CH)


def put_slices(ref, value, head, height, level=0):
    per_head = CH // height
    pieces = value.astype(BF16).reshape(per_head, height, value.shape[1])
    ref[head * per_head : (head + 1) * per_head, level * height : (level + 1) * height, :] = pieces


def get_slices(ref, head, height, level=0):
    per_head = CH // height
    pieces = ref[head * per_head : (head + 1) * per_head, level * height : (level + 1) * height, :]
    return pieces.reshape(CH, ref.shape[2])


def height_of(heads, ref):
    return heads * CH // ref.shape[0]


def split_pair(value):
    high = value.astype(BF16)
    return high, (value - high.astype(F32)).astype(BF16)


def state_kernel(key_ref, value_ref, total_ref, first_ref):
    heads = key_ref.shape[1] // CH
    for h in range(heads):
        cols = span_rows(h)
        first = dot_tn(key_ref[0:CH, cols], value_ref[0:CH, cols])
        second = dot_tn(key_ref[CH : 2 * CH, cols], value_ref[CH : 2 * CH, cols])
        first_ref[cols, :] = first.astype(BF16)
        put_slices(total_ref, first + second, h, total_ref.shape[1])


def prefix_kernel(in_ref, out_ref):
    shards, height = in_ref.shape[0], in_ref.shape[1]
    levels = out_ref.shape[1] // height
    sums = [in_ref[s].astype(F32) for s in range(shards)]
    zero = jnp.zeros(in_ref.shape[1:], BF16)
    for level in range(levels):
        rounded = [s.astype(BF16) for s in sums]
        for t in range(shards):
            group = t >> level
            out_ref[t, level * height : (level + 1) * height, :] = rounded[group - 1] if group & 1 else zero
        sums = [sums[2 * i] + sums[2 * i + 1] for i in range(len(sums) // 2)]


def suffix_kernel(in_ref, table_ref, out_ref):
    shards = in_ref.shape[0]
    levels = shards.bit_length() - 1
    height = in_ref.shape[1] // (8 * levels) * 8
    start = levels * height
    table_rows = table_ref.shape[0]
    rows = out_ref.shape[1] - height - table_rows
    gain = in_ref[0, start:, :].astype(F32)
    for s in range(1, shards):
        gain = gain + in_ref[s, start:, :].astype(F32)
    gain = (gain[:rows] + gain[rows : 2 * rows]).astype(BF16)
    tail = jnp.concatenate([table_ref[...], gain], axis=0)
    carried = [None]
    for level in range(levels - 1, -1, -1):
        size = 1 << level
        groups = shards >> level
        below = []
        for g in range(groups):
            base = carried[g >> 1]
            if g & 1 == 0:
                total = None
                for s in range((g + 1) * size, (g + 2) * size):
                    piece = in_ref[s, level * height : (level + 1) * height, :].astype(F32)
                    total = piece if total is None else total + piece
                base = total if base is None else base + total
            below.append(base)
        carried = below
    zero = jnp.zeros((height, CH), F32)
    for t in range(shards):
        value = zero if carried[t] is None else carried[t]
        out_ref[t, 0:height, :] = value.astype(BF16)
        out_ref[t, height:, :] = tail


def onehot_of(index_ref, level):
    tokens = index_ref.shape[1]
    entry = lax.broadcasted_iota(jnp.int32, (TABLE, tokens), 0)
    return (index_ref[level : level + 1, :] == entry).astype(F32)


def weight_kernel(index_ref, table_ref, weight_ref):
    levels, tokens = index_ref.shape
    heads = table_ref.shape[1]
    rows = [dot_nn(table_ref[level], onehot_of(index_ref, level), HIGHEST) for level in range(levels)]
    rows.append(jnp.zeros((CH - levels * heads, tokens), F32))
    weight_ref[...] = jnp.concatenate(rows, axis=0).T


def near_kernel(query_ref, key_ref, value_ref, first_ref, weight_ref, out_ref):
    heads = query_ref.shape[1] // CH
    spans = query_ref.shape[0] // CH
    causal = causal_mask()
    for c in range(spans):
        rows = span_rows(c)
        for h in range(heads):
            cols = span_rows(h)
            query = query_ref[rows, cols]
            scores = jnp.where(causal, dot_nt(query, key_ref[rows, cols]), 0.0).astype(BF16)
            near = weight_ref[rows, h : h + 1] * dot_nn(scores, value_ref[rows, cols])
            if c == 1:
                near = near + weight_ref[rows, heads + h : heads + h + 1] * dot_nn(query, first_ref[cols, :])
            out_ref[rows, cols] = near


def far_kernel(near_ref, query_ref, state_ref, weight_ref, attn_ref):
    heads = query_ref.shape[1] // CH
    spans = query_ref.shape[0] // CH
    height = height_of(heads, state_ref)
    levels = state_ref.shape[1] // height
    for c in range(spans):
        rows = span_rows(c)
        for h in range(heads):
            cols = span_rows(h)
            query = query_ref[rows, cols]
            total = near_ref[rows, cols]
            for level in range(levels):
                spot = (level + 2) * heads + h
                total = total + weight_ref[rows, spot : spot + 1] * dot_nn(query, get_slices(state_ref, h, height, level))
            attn_ref[rows, cols] = total.astype(BF16)


def norm_kernel(attn_ref, cot_ref, gain_ref, normed_ref, grad_ref):
    columns, own, width = attn_ref.shape
    features = float(columns * width)
    squares = jnp.zeros((own, width), F32)
    along = jnp.zeros((own, width), F32)
    for d in range(columns):
        cols = slice(d * width, (d + 1) * width)
        attn = attn_ref[d].astype(F32)
        squares = squares + attn * attn
        along = along + cot_ref[:, cols].astype(F32) * gain_ref[:, cols] * attn
    inv_rms = lax.rsqrt(jnp.sum(squares, axis=1, keepdims=True) / features + EPSILON)
    mean = jnp.sum(along, axis=1, keepdims=True) * inv_rms / features
    parts = []
    for d in range(columns):
        cols = slice(d * width, (d + 1) * width)
        cot = cot_ref[:, cols].astype(F32)
        unit = attn_ref[d].astype(F32) * inv_rms
        normed_ref[:, cols] = (unit * gain_ref[:, cols]).astype(BF16)
        grad_ref[d, 0:own, :] = ((cot * gain_ref[:, cols] - unit * mean) * inv_rms).astype(BF16)
        parts.append(jnp.sum(cot * unit, axis=0, keepdims=True))
    block = jnp.concatenate(parts, axis=0).astype(BF16)
    for d in range(columns):
        grad_ref[d, own:, :] = block


def grad_kernel(head_ref, query_ref, weight_ref, grad_ref, group_ref):
    columns = head_ref.shape[0]
    own = head_ref.shape[1] - columns
    heads = query_ref.shape[1] // CH
    shards = group_ref.shape[0]
    height = height_of(heads, group_ref)
    levels = group_ref.shape[1] // height
    start = levels * height
    for d in range(columns):
        grad_ref[d * own : (d + 1) * own, :] = head_ref[d, 0:own, :]
    for h in range(heads):
        cols = span_rows(h)
        grad_f = grad_ref[:, cols].astype(F32)
        query = query_ref[:, cols]
        for level in range(levels):
            spot = (level + 2) * heads + h
            scaled = (weight_ref[:, spot : spot + 1] * grad_f).astype(BF16)
            put_slices(group_ref, dot_tn(query, scaled), h, height, level)
    gain = head_ref[0, own:, :].astype(F32)
    for d in range(1, columns):
        gain = gain + head_ref[d, own:, :].astype(F32)
    rows = columns * heads // shards
    extra = group_ref.shape[1] - start
    for s in range(shards):
        spots = range(s * rows, (s + 1) * rows)
        picked = [gain[i // heads : i // heads + 1, span_rows(i % heads)] for i in spots]
        high, low = split_pair(jnp.concatenate(picked, axis=0))
        fill = jnp.zeros((extra - 2 * rows, CH), BF16)
        group_ref[s, start:, :] = jnp.concatenate([high, low, fill], axis=0)


def back_kernel(
    query_ref, key_ref, value_ref, grad_ref, weight_ref, state_ref, first_ref, index_ref,
    dq_ref, dk_ref, dv_ref, inner_ref, table_ref, gw_ref,
):
    heads = query_ref.shape[1] // CH
    spans = query_ref.shape[0] // CH
    height = height_of(heads, state_ref)
    levels = state_ref.shape[1] // height
    all_levels = levels + 2
    causal = causal_mask()
    gw_ref[...] = jnp.zeros(gw_ref.shape, F32)
    for c in range(spans):
        rows = span_rows(c)
        for h in range(heads):
            cols = span_rows(h)
            query = query_ref[rows, cols]
            query_f = query.astype(F32)
            key = key_ref[rows, cols]
            grad = grad_ref[rows, cols]
            first_weight = weight_ref[rows, h : h + 1]
            scores = jnp.where(causal, dot_nt(query, key), 0.0)
            along = jnp.where(causal, dot_nt(grad, value_ref[rows, cols]), 0.0)
            gw_ref[rows, h : h + 1] = jnp.sum(scores.astype(BF16).astype(F32) * along, axis=1, keepdims=True)
            grad_scores = (along * first_weight).astype(BF16)
            weighted = (scores * first_weight).astype(BF16)
            dq = dot_nn(grad_scores, key)
            dk_ref[rows, cols] = dot_tn(grad_scores, query)
            dv_ref[rows, cols] = dot_tn(weighted, grad)
            if c == 1:
                spot = heads + h
                weight = weight_ref[rows, spot : spot + 1]
                far = dot_nt(grad, first_ref[cols, :])
                gw_ref[rows, spot : spot + 1] = jnp.sum(query_f * far, axis=1, keepdims=True)
                dq = dq + weight * far
                inner_ref[cols, :] = dot_tn(query, (weight * grad.astype(F32)).astype(BF16))
            for level in range(levels):
                spot = (level + 2) * heads + h
                far = dot_nt(grad, get_slices(state_ref, h, height, level))
                gw_ref[rows, spot : spot + 1] = jnp.sum(query_f * far, axis=1, keepdims=True)
                dq = dq + weight_ref[rows, spot : spot + 1] * far
            dq_ref[rows, cols] = dq.astype(BF16)
    grads = gw_ref[...].T
    blocks = []
    for level in range(all_levels):
        by_row = lax.dot_general(
            grads, onehot_of(index_ref, level), (((1,), (1,)), ((), ())), precision=HIGHEST, preferred_element_type=F32
        )
        blocks.append(by_row[level * heads : (level + 1) * heads])
    joined = [jnp.concatenate(blocks[2 * pair : 2 * pair + 2], axis=1) for pair in range(all_levels // 2)]
    for h in range(0, heads if all_levels % 2 else 0, 2):
        joined.append(jnp.concatenate([blocks[-1][h : h + 1], blocks[-1][h + 1 : h + 2]], axis=1))
    table_ref[...] = jnp.concatenate(joined, axis=0).astype(BF16)


def final_kernel(
    cross_ref, inner_ref, key_ref, value_ref, dk_ref, dv_ref, grad_key_ref, grad_value_ref, table_ref, gain_ref
):
    heads = key_ref.shape[1] // CH
    spans = key_ref.shape[0] // CH
    shards = cross_ref.shape[0]
    height = height_of(heads, cross_ref)
    rows = gain_ref.shape[0] // shards
    table_end = cross_ref.shape[1] - height - rows
    total = None
    for s in range(shards):
        tail = cross_ref[s, height:, :].astype(F32)
        total = tail if total is None else total + tail
        gain_ref[s * rows : (s + 1) * rows, :] = tail[table_end:]
    all_levels = table_ref.shape[0]
    for level in range(all_levels):
        if level == all_levels - 1 and all_levels % 2:
            base = (level // 2) * heads
            for h in range(heads):
                spot, left = base + h // 2, (h % 2) * TABLE
                table_ref[level, h : h + 1, :] = total[spot : spot + 1, left : left + TABLE]
        else:
            top, left = (level // 2) * heads, (level % 2) * TABLE
            table_ref[level] = total[top : top + heads, left : left + TABLE]
    for h in range(heads):
        cols = span_rows(h)
        cross = get_slices(cross_ref, h, height)
        for c in range(spans):
            rows = span_rows(c)
            state = cross if c == 1 else (inner_ref[cols, :] + cross.astype(F32)).astype(BF16)
            grad_key = dk_ref[rows, cols] + dot_nt(value_ref[rows, cols], state)
            grad_value = dv_ref[rows, cols] + dot_nn(key_ref[rows, cols], state)
            grad_key_ref[rows, cols] = grad_key.astype(BF16)
            grad_value_ref[rows, cols] = grad_value.astype(BF16)


def exchange(value, axis):
    return lax.all_to_all(value, axis, split_axis=0, concat_axis=0, tiled=True)


def body(queries, key_rows, value_rows, level_table, level_index, norm_gain, cotangent):
    tokens, width = queries.shape
    heads = level_table.shape[2]
    all_levels = level_table.shape[1]
    shards = lax.axis_size("seq")
    columns = lax.axis_size("head")
    levels = shards.bit_length() - 1
    height = heads * CH // shards
    own = tokens // columns
    table_rows = all_levels * heads * TABLE // CH
    gain_rows = columns * heads // shards

    total, first = call(
        state_kernel, (shaped((shards, height, CH), BF16), shaped((heads * CH, CH), BF16)), key_rows, value_rows
    )
    slices = exchange(total, "seq")
    gain = norm_gain.reshape(1, columns * width)
    table = jnp.transpose(level_table, (1, 2, 0))
    index = jnp.transpose(level_index)
    weights = call(weight_kernel, shaped((tokens, CH), F32), index, table)
    near = call(near_kernel, shaped((tokens, width), F32), queries, key_rows, value_rows, first, weights)
    group_states = call(prefix_kernel, shaped((shards, levels * height, CH), BF16), slices)
    states = exchange(group_states, "seq")
    attn = call(far_kernel, shaped((tokens, width), BF16), near, queries, states, weights)
    token_attn = exchange(attn.reshape(columns, own, width), "head")
    normed, token_grad = call(
        norm_kernel,
        (shaped((own, columns * width), BF16), shaped((columns, own + columns, width), BF16)),
        token_attn,
        cotangent,
        gain,
    )
    head_grad = exchange(token_grad, "head")
    grad, groups = call(
        grad_kernel,
        (shaped((tokens, width), BF16), shaped((shards, levels * height + 8, CH), BF16)),
        head_grad,
        queries,
        weights,
    )
    group_slices = exchange(groups, "seq")
    grad_query, near_dk, near_dv, inner, table_part, _ = call(
        back_kernel,
        (
            shaped((tokens, width), BF16),
            shaped((tokens, width), F32),
            shaped((tokens, width), F32),
            shaped((heads * CH, CH), F32),
            shaped((table_rows, CH), BF16),
            shaped((tokens, CH), F32),
        ),
        queries,
        key_rows,
        value_rows,
        grad,
        weights,
        states,
        first,
        index,
    )
    key_slices = call(
        suffix_kernel, shaped((shards, height + table_rows + gain_rows, CH), BF16), group_slices, table_part
    )
    cross = exchange(key_slices, "seq")
    grad_key, grad_value, table_sum, gain_sum = call(
        final_kernel,
        (
            shaped((tokens, width), BF16),
            shaped((tokens, width), BF16),
            shaped((all_levels, heads, TABLE), F32),
            shaped((columns * heads, CH), F32),
        ),
        cross,
        inner,
        key_rows,
        value_rows,
        near_dk,
        near_dv,
    )
    grad_table = jnp.transpose(table_sum, (2, 0, 1))
    return normed, grad_query, grad_key, grad_value, grad_table, gain_sum.reshape(columns * width)


def solution(mesh):
    placed = (
        P("seq", "head"),
        P("seq", "head"),
        P("seq", "head"),
        P(None, None, "head"),
        P("seq", None),
        P(),
        P(("seq", "head"), None),
    )
    return jax.shard_map(
        body,
        mesh=mesh,
        in_specs=placed,
        out_specs=(
            P(("seq", "head"), None),
            P("seq", "head"),
            P("seq", "head"),
            P("seq", "head"),
            P(None, None, "head"),
            P(),
        ),
        check_vma=False,
    )
```

time: 177 us -> 140 us (0.79)
  the two profiles are of different devices: /device:TPU:2 before, /device:TPU:1 now
where the time goes in v3:
time: 140 us; the launch traced here: 139 us
  blocking collectives  82.3 us (59%)
  waiting for transfers between devices  30.6 us (22%)
  Pallas kernels  12.5 us (9%)
  starting transfers between devices  8.66 us (6%)
  local copies, waits for them, and re-layouts  4.28 us (3%)
    all_to_all x4, blocking collectives, exchange(): return lax.all_to_all(value, axis, split_axis=0, concat_axis=0, tiled=True)  82.3 us
    all_to_all x2, waiting for transfers between devices, exchange(): return lax.all_to_all(value, axis, split_axis=0, concat_axis=0, tiled=True)  30.6 us
    pallas_call x10, Pallas kernels, call(): pl.pallas_call(kernel, out_shape=out_shape, in_specs=[scalar if operand.n...  12.5 us
    all_to_all x2, starting transfers between devices, exchange(): return lax.all_to_all(value, axis, split_axis=0, concat_axis=0, tiled=True)  8.66 us
    unnamed x26, local copies, waits for them, and re-layouts  4.28 us
  transfers between devices with their start and end apart: 2, of which 2 were waited for; matrix products, arithmetic and copies ran while one was open for 0% of the time, Pallas kernels for 4%

profile of v3, /device:TPU:1, one launch (start us, length us, event | category | flops | bytes accessed | tf_op | source)
XLA Modules:
  0.0 139.1 jit_solution(895394021050506171)
XLA Ops:
  0.6 0.0 copy-start.1
  0.6 0.9 copy-done.1
  1.6 0.0 copy-start.3
  1.6 0.9 copy-done.3
  2.5 0.3 shard_map.118
  2.8 19.6 %all_to_all.30.in_ref = bf16[32,16,128]{2,1,0:T(8,128)(2,1)S(1)} all-to-all(bf16[32,16,128]{2,1,0:T(8,128)(2,1)S(1)} %get-tuple-element.22), channel_id=1, replica_groups=mesh['seq'=32,'head'=16] {'seq'}, dimensions={0} | all-to-all | bytes 262144 | tf_op jit(solution)/shard_map/all_to_all | solution.py:327
  22.4 0.9 shard_map.121
  23.4 0.0 copy-start.10
  23.4 0.0 copy-start.12
  23.4 0.0 copy-start
  23.4 0.0 copy-start.2
  23.4 0.0 copy-start.4
  23.4 4.0 %all-to-all-start.1 = ((bf16[32,80,128]{2,1,0:T(8,128)(2,1)}), bf16[32,80,128]{2,1,0:T(8,128)(2,1)S(1)}, u32[]{:S(2)}, u32[]{:S(2)}) async-start(bf16[32,80,128]{2,1,0:T(8,128)(2,1)} %shard_map.121), calls=%async_computation.1 | async-start | bytes 1310720 | tf_op jit(solution)/shard_map/all_to_all | solution.py:327
  27.4 0.0 copy-done.10
  27.5 0.0 copy-done.12
  27.5 0.4 shard_map.119.weight_ref
  27.9 0.0 copy-done
  27.9 0.0 copy-done.2
  27.9 0.0 copy-done.4
  27.9 1.0 shard_map.120.near_ref
  29.0 16.2 %all-to-all-done.1.state_ref = bf16[32,80,128]{2,1,0:T(8,128)(2,1)S(1)} async-done(((bf16[32,80,128]{2,1,0:T(8,128)(2,1)}), bf16[32,80,128]{2,1,0:T(8,128)(2,1)S(1)}, u32[]{:S(2)}, u32[]{:S(2)}) %all-to-all-start.1) | async-done | bytes 655392 | tf_op jit(solution)/shard_map/all_to_all | solution.py:327
  45.2 0.9 shard_map.122
  46.0 0.0 copy-start.7
  46.0 0.0 copy-start.11
  46.0 25.4 %all_to_all.31.attn_ref = bf16[16,16,512]{2,1,0:T(8,128)(2,1)S(1)} all-to-all(bf16[16,16,512]{2,1,0:T(8,128)(2,1)S(1)} %bitcast.6), channel_id=1, replica_groups=mesh['seq'=32,'head'=16] {'head'}, dimensions={0} | all-to-all | bytes 524288 | tf_op jit(solution)/shard_map/all_to_all | solution.py:327
  71.4 0.0 copy-done.7
  71.4 0.0 copy-done.11
  71.4 1.1 shard_map.123
  72.5 20.0 %all_to_all.32.head_ref = bf16[16,32,512]{2,1,0:T(8,128)(2,1)S(1)} all-to-all(bf16[16,32,512]{2,1,0:T(8,128)(2,1)S(1)} %get-tuple-element.24), channel_id=1, replica_groups=mesh['seq'=32,'head'=16] {'head'}, dimensions={0} | all-to-all | bytes 1048576 | tf_op jit(solution)/shard_map/all_to_all | solution.py:327
  92.5 2.0 %shard_map.124 = (bf16[256,512]{1,0:T(8,128)(2,1)S(1)}, bf16[32,88,128]{2,1,0:T(8,128)(2,1)}) custom-call(bf16[16,32,512]{2,1,0:T(8,128)(2,1)S(1)} %all_to_all.32.head_ref, bf16[256,512]{1,0:T(8,128)(2,1)S(1)} %copy-done, f32[256,128]{1,0:T(8,128)S(1)} %shard_map.119.weight_ref), custom_call_target="tpu_custom_call" | custom-call | tf_op jit(solution)/shard_map/pallas_call | solution.py:20
  94.5 0.0 copy-start.5
  94.5 0.7 copy-done.5
  95.2 4.6 %all-to-all-start.4 = ((bf16[32,88,128]{2,1,0:T(8,128)(2,1)}), bf16[32,88,128]{2,1,0:T(8,128)(2,1)S(1)}, u32[]{:S(2)}, u32[]{:S(2)}) async-start(bf16[32,88,128]{2,1,0:T(8,128)(2,1)} %get-tuple-element.27), calls=%async_computation.4 | async-start | bytes 1441792 | tf_op jit(solution)/shard_map/all_to_all | solution.py:327
  99.8 0.0 copy-start.6
  99.8 0.9 copy-done.6
  100.7 4.7 %shard_map.125 = (bf16[256,512]{1,0:T(8,128)(2,1)}, f32[256,512]{1,0:T(8,128)S(1)}, f32[256,512]{1,0:T(8,128)S(1)}, f32[512,128]{1,0:T(8,128)S(1)}, bf16[14,128]{1,0:T(8,128)(2,1)S(1)}, /*index=5*/f32[256,128]{1,0:T(8,128)}) custom-call(bf16[256,512]{1,0:T(8,128)(2,1)S(1)} %copy-done, bf16[256,512]{1,0:T(8,128)(2,1)S(1)} %copy-done.2, ...), custom_call_target="tpu_custom_call" | custom-call | tf_op jit(solution)/shard_map/pallas_call | solution.py:20
  105.5 0.0 copy-start.8
  105.5 0.7 copy-done.8
  106.2 14.4 %all-to-all-done.4.in_ref = bf16[32,88,128]{2,1,0:T(8,128)(2,1)S(1)} async-done(((bf16[32,88,128]{2,1,0:T(8,128)(2,1)}), bf16[32,88,128]{2,1,0:T(8,128)(2,1)S(1)}, u32[]{:S(2)}, u32[]{:S(2)}) %all-to-all-start.4) | async-done | bytes 720928 | tf_op jit(solution)/shard_map/all_to_all | solution.py:327
  120.5 0.1 shard_map.126
  120.6 0.0 copy-start.9
  120.6 17.3 %all_to_all.33.cross_ref = bf16[32,32,128]{2,1,0:T(8,128)(2,1)S(1)} all-to-all(bf16[32,32,128]{2,1,0:T(8,128)(2,1)S(1)} %shard_map.126), channel_id=1, replica_groups=mesh['seq'=32,'head'=16] {'seq'}, dimensions={0} | all-to-all | bytes 524288 | tf_op jit(solution)/shard_map/all_to_all | solution.py:327
  137.9 0.0 copy-done.9
  137.9 1.2 shard_map.127
Async XLA Ops:
  0.6 1.0 copy-start.1
  1.6 0.9 copy-start.3
  23.4 4.1 %copy-start.10 = (s32[256,7]{0,1:T(8,128)S(1)}, s32[256,7]{0,1:T(8,128)}, u32[]{:S(2)}) copy-start(s32[256,7]{0,1:T(8,128)} %param.11) | copy-start | bytes 21508
  23.4 4.1 %copy-start.12 = (f32[64,7,4]{0,2,1:T(4,128)S(1)}, f32[64,7,4]{0,2,1:T(4,128)}, u32[]{:S(2)}) copy-start(f32[64,7,4]{0,2,1:T(4,128)} %param.10) | copy-start | bytes 21508
  23.4 4.5 %copy-start = (bf16[256,512]{1,0:T(8,128)(2,1)S(1)}, bf16[256,512]{1,0:T(8,128)(2,1)}, u32[]{:S(2)}) copy-start(bf16[256,512]{1,0:T(8,128)(2,1)} %query_ref.7) | copy-start | bytes 786436
  23.4 4.5 %copy-start.2 = (bf16[256,512]{1,0:T(8,128)(2,1)S(1)}, bf16[256,512]{1,0:T(8,128)(2,1)}, u32[]{:S(2)}) copy-start(bf16[256,512]{1,0:T(8,128)(2,1)} %key_ref.7) | copy-start | bytes 786436
  23.4 4.5 %copy-start.4 = (bf16[256,512]{1,0:T(8,128)(2,1)S(1)}, bf16[256,512]{1,0:T(8,128)(2,1)}, u32[]{:S(2)}) copy-start(bf16[256,512]{1,0:T(8,128)(2,1)} %value_ref.7) | copy-start | bytes 786436
  23.4 21.8 %all-to-all-start.1 = ((bf16[32,80,128]{2,1,0:T(8,128)(2,1)}), bf16[32,80,128]{2,1,0:T(8,128)(2,1)S(1)}, u32[]{:S(2)}, u32[]{:S(2)}) async-start(bf16[32,80,128]{2,1,0:T(8,128)(2,1)} %shard_map.121), calls=%async_computation.1 | async-start | bytes 1310720 | tf_op jit(solution)/shard_map/all_to_all | solution.py:327
  46.0 25.4 %copy-start.7 = (bf16[16,8192]{1,0:T(8,128)(2,1)S(1)}, bf16[16,8192]{1,0:T(8,128)(2,1)}, u32[]{:S(2)}) copy-start(bf16[16,8192]{1,0:T(8,128)(2,1)} %cot_ref.1) | copy-start | bytes 786436
  46.0 25.4 %copy-start.11 = (f32[8192]{0:T(1024)S(1)}, f32[8192]{0:T(1024)}, u32[]{:S(2)}) copy-start(f32[8192]{0:T(1024)} %param.12) | copy-start | bytes 98308
  94.5 0.7 copy-start.5
  95.2 25.4 %all-to-all-start.4 = ((bf16[32,88,128]{2,1,0:T(8,128)(2,1)}), bf16[32,88,128]{2,1,0:T(8,128)(2,1)S(1)}, u32[]{:S(2)}, u32[]{:S(2)}) async-start(bf16[32,88,128]{2,1,0:T(8,128)(2,1)} %get-tuple-element.27), calls=%async_computation.4 | async-start | bytes 1441792 | tf_op jit(solution)/shard_map/all_to_all | solution.py:327
  99.8 1.0 copy-start.6
  105.5 0.7 copy-start.8
  120.6 17.3 %copy-start.9 = (f32[512,128]{1,0:T(8,128)S(1)}, f32[512,128]{1,0:T(8,128)}, u32[]{:S(2)}) copy-start(f32[512,128]{1,0:T(8,128)} %copy-done.8) | copy-start | bytes 786436

commit v4 on v3

--- a/solution.py
+++ b/solution.py
@@ -12,6 +12,7 @@
 F32 = jnp.float32
 BF16 = jnp.bfloat16
 INTERPRET = False
+ROW_BITS = 2
 
 
 def call(kernel, out_shape, *operands):
@@ -22,7 +23,7 @@
         out_shape=out_shape,
         in_specs=[scalar if operand.ndim == 1 else whole for operand in operands],
         interpret=INTERPRET,
-        compiler_params=pltpu.CompilerParams(vmem_limit_bytes=48 * 1024 * 1024),
+        compiler_params=pltpu.CompilerParams(vmem_limit_bytes=16 * 1024 * 1024),
     )(*operands)
 
 
@@ -73,7 +74,13 @@
     return high, (value - high.astype(F32)).astype(BF16)
 
 
-def state_kernel(key_ref, value_ref, total_ref, first_ref):
+def state_kernel(key_hbm, value_hbm, total_ref, first_ref, key_ref, value_ref, sems):
+    key_copy = pltpu.make_async_copy(key_hbm, key_ref, sems.at[0])
+    value_copy = pltpu.make_async_copy(value_hbm, value_ref, sems.at[1])
+    key_copy.start()
+    value_copy.start()
+    key_copy.wait()
+    value_copy.wait()
     heads = key_ref.shape[1] // CH
     for h in range(heads):
         cols = span_rows(h)
@@ -83,23 +90,56 @@
         put_slices(total_ref, first + second, h, total_ref.shape[1])
 
 
+def span_states(key_rows, value_rows, shards):
+    tokens, width = key_rows.shape
+    return pl.pallas_call(
+        state_kernel,
+        out_shape=(shaped((shards, width // shards, CH), BF16), shaped((width, CH), BF16)),
+        in_specs=[pl.BlockSpec(memory_space=pltpu.MemorySpace.HBM)] * 2,
+        scratch_shapes=[
+            pltpu.VMEM((tokens, width), BF16),
+            pltpu.VMEM((tokens, width), BF16),
+            pltpu.SemaphoreType.DMA((2,)),
+        ],
+        name="span_states",
+        interpret=INTERPRET,
+        compiler_params=pltpu.CompilerParams(vmem_limit_bytes=16 * 1024 * 1024),
+    )(key_rows, value_rows)
+
+
+def low_state_kernel(place_ref, one_ref, two_ref, three_ref, state_ref):
+    row = place_ref[0] & ((1 << ROW_BITS) - 1)
+    one = one_ref[...].astype(F32)
+    two = two_ref[...].astype(F32)
+    three = three_ref[...].astype(F32)
+    state_ref[0] = jnp.where((row & 1) == 1, one, 0.0).astype(BF16)
+    pair = jnp.where(row == 2, two + one, jnp.where(row == 3, three + two, 0.0))
+    state_ref[1] = pair.astype(BF16)
+
+
+def low_grad_kernel(one_ref, two_ref, three_ref, sum_ref):
+    sum_ref[...] = one_ref[...].astype(F32) + two_ref[...].astype(F32) + three_ref[...].astype(F32)
+
+
 def prefix_kernel(in_ref, out_ref):
     shards, height = in_ref.shape[0], in_ref.shape[1]
     levels = out_ref.shape[1] // height
     sums = [in_ref[s].astype(F32) for s in range(shards)]
+    for _ in range(ROW_BITS):
+        sums = [sums[2 * i] + sums[2 * i + 1] for i in range(len(sums) // 2)]
     zero = jnp.zeros(in_ref.shape[1:], BF16)
     for level in range(levels):
         rounded = [s.astype(BF16) for s in sums]
         for t in range(shards):
-            group = t >> level
+            group = t >> (level + ROW_BITS)
             out_ref[t, level * height : (level + 1) * height, :] = rounded[group - 1] if group & 1 else zero
         sums = [sums[2 * i] + sums[2 * i + 1] for i in range(len(sums) // 2)]
 
 
 def suffix_kernel(in_ref, table_ref, out_ref):
     shards = in_ref.shape[0]
-    levels = shards.bit_length() - 1
-    height = in_ref.shape[1] // (8 * levels) * 8
+    levels = shards.bit_length() - 1 - ROW_BITS
+    height = (in_ref.shape[1] - 8) // levels
     start = levels * height
     table_rows = table_ref.shape[0]
     rows = out_ref.shape[1] - height - table_rows
@@ -110,8 +150,8 @@
     tail = jnp.concatenate([table_ref[...], gain], axis=0)
     carried = [None]
     for level in range(levels - 1, -1, -1):
-        size = 1 << level
-        groups = shards >> level
+        size = 1 << (level + ROW_BITS)
+        groups = shards >> (level + ROW_BITS)
         below = []
         for g in range(groups):
             base = carried[g >> 1]
@@ -125,7 +165,7 @@
         carried = below
     zero = jnp.zeros((height, CH), F32)
     for t in range(shards):
-        value = zero if carried[t] is None else carried[t]
+        value = zero if carried[t >> ROW_BITS] is None else carried[t >> ROW_BITS]
         out_ref[t, 0:height, :] = value.astype(BF16)
         out_ref[t, height:, :] = tail
 
@@ -144,7 +184,7 @@
     weight_ref[...] = jnp.concatenate(rows, axis=0).T
 
 
-def near_kernel(query_ref, key_ref, value_ref, first_ref, weight_ref, out_ref):
+def near_kernel(query_ref, key_ref, value_ref, first_ref, low_ref, weight_ref, out_ref):
     heads = query_ref.shape[1] // CH
     spans = query_ref.shape[0] // CH
     causal = causal_mask()
@@ -157,6 +197,9 @@
             near = weight_ref[rows, h : h + 1] * dot_nn(scores, value_ref[rows, cols])
             if c == 1:
                 near = near + weight_ref[rows, heads + h : heads + h + 1] * dot_nn(query, first_ref[cols, :])
+            for level in range(ROW_BITS):
+                spot = (level + 2) * heads + h
+                near = near + weight_ref[rows, spot : spot + 1] * dot_nn(query, low_ref[level, cols, :])
             out_ref[rows, cols] = near
 
 
@@ -172,7 +215,7 @@
             query = query_ref[rows, cols]
             total = near_ref[rows, cols]
             for level in range(levels):
-                spot = (level + 2) * heads + h
+                spot = (level + 2 + ROW_BITS) * heads + h
                 total = total + weight_ref[rows, spot : spot + 1] * dot_nn(query, get_slices(state_ref, h, height, level))
             attn_ref[rows, cols] = total.astype(BF16)
 
@@ -202,7 +245,7 @@
         grad_ref[d, own:, :] = block
 
 
-def grad_kernel(head_ref, query_ref, weight_ref, grad_ref, group_ref):
+def grad_kernel(place_ref, head_ref, query_ref, weight_ref, grad_ref, group_ref, one_ref, two_ref):
     columns = head_ref.shape[0]
     own = head_ref.shape[1] - columns
     heads = query_ref.shape[1] // CH
@@ -216,10 +259,16 @@
         cols = span_rows(h)
         grad_f = grad_ref[:, cols].astype(F32)
         query = query_ref[:, cols]
-        for level in range(levels):
+        low = []
+        for level in range(levels + ROW_BITS):
             spot = (level + 2) * heads + h
-            scaled = (weight_ref[:, spot : spot + 1] * grad_f).astype(BF16)
-            put_slices(group_ref, dot_tn(query, scaled), h, height, level)
+            product = dot_tn(query, (weight_ref[:, spot : spot + 1] * grad_f).astype(BF16))
+            if level < ROW_BITS:
+                low.append(product)
+            else:
+                put_slices(group_ref, product, h, height, level - ROW_BITS)
+        one_ref[cols, :] = jnp.where((place_ref[0] & 1) == 1, low[0], low[1]).astype(BF16)
+        two_ref[cols, :] = low[1].astype(BF16)
     gain = head_ref[0, own:, :].astype(F32)
     for d in range(1, columns):
         gain = gain + head_ref[d, own:, :].astype(F32)
@@ -234,13 +283,13 @@
 
 
 def back_kernel(
-    query_ref, key_ref, value_ref, grad_ref, weight_ref, state_ref, first_ref, index_ref,
+    query_ref, key_ref, value_ref, grad_ref, weight_ref, state_ref, low_ref, first_ref, index_ref,
     dq_ref, dk_ref, dv_ref, inner_ref, table_ref, gw_ref,
 ):
     heads = query_ref.shape[1] // CH
     spans = query_ref.shape[0] // CH
     height = height_of(heads, state_ref)
-    levels = state_ref.shape[1] // height
+    levels = state_ref.shape[1] // height + ROW_BITS
     all_levels = levels + 2
     causal = causal_mask()
     gw_ref[...] = jnp.zeros(gw_ref.shape, F32)
@@ -270,7 +319,11 @@
                 inner_ref[cols, :] = dot_tn(query, (weight * grad.astype(F32)).astype(BF16))
             for level in range(levels):
                 spot = (level + 2) * heads + h
-                far = dot_nt(grad, get_slices(state_ref, h, height, level))
+                if level < ROW_BITS:
+                    state = low_ref[level, cols, :]
+                else:
+                    state = get_slices(state_ref, h, height, level - ROW_BITS)
+                far = dot_nt(grad, state)
                 gw_ref[rows, spot : spot + 1] = jnp.sum(query_f * far, axis=1, keepdims=True)
                 dq = dq + weight_ref[rows, spot : spot + 1] * far
             dq_ref[rows, cols] = dq.astype(BF16)
@@ -288,7 +341,7 @@
 
 
 def final_kernel(
-    cross_ref, inner_ref, key_ref, value_ref, dk_ref, dv_ref, grad_key_ref, grad_value_ref, table_ref, gain_ref
+    cross_ref, low_ref, inner_ref, key_ref, value_ref, dk_ref, dv_ref, grad_key_ref, grad_value_ref, table_ref, gain_ref
 ):
     heads = key_ref.shape[1] // CH
     spans = key_ref.shape[0] // CH
@@ -313,10 +366,10 @@
             table_ref[level] = total[top : top + heads, left : left + TABLE]
     for h in range(heads):
         cols = span_rows(h)
-        cross = get_slices(cross_ref, h, height)
+        cross = get_slices(cross_ref, h, height).astype(F32) + low_ref[cols, :]
         for c in range(spans):
             rows = span_rows(c)
-            state = cross if c == 1 else (inner_ref[cols, :] + cross.astype(F32)).astype(BF16)
+            state = (cross if c == 1 else inner_ref[cols, :] + cross).astype(BF16)
             grad_key = dk_ref[rows, cols] + dot_nt(value_ref[rows, cols], state)
             grad_value = dv_ref[rows, cols] + dot_nn(key_ref[rows, cols], state)
             grad_key_ref[rows, cols] = grad_key.astype(BF16)
@@ -325,6 +378,13 @@
 
 def exchange(value, axis):
     return lax.all_to_all(value, axis, split_axis=0, concat_axis=0, tiled=True)
+
+
+def row_shift(value, step):
+    row = 1 << ROW_BITS
+    shards = lax.axis_size("seq")
+    pairs = [(s, s + step) for s in range(shards) if 0 <= s % row + step < row]
+    return lax.ppermute(value, "seq", pairs)
 
 
 def body(queries, key_rows, value_rows, level_table, level_index, norm_gain, cotangent):
@@ -333,21 +393,24 @@
     all_levels = level_table.shape[1]
     shards = lax.axis_size("seq")
     columns = lax.axis_size("head")
-    levels = shards.bit_length() - 1
+    levels = shards.bit_length() - 1 - ROW_BITS
     height = heads * CH // shards
     own = tokens // columns
     table_rows = all_levels * heads * TABLE // CH
     gain_rows = columns * heads // shards
 
-    total, first = call(
-        state_kernel, (shaped((shards, height, CH), BF16), shaped((heads * CH, CH), BF16)), key_rows, value_rows
-    )
+    spot = lax.axis_index("seq").reshape(1)
+
+    total, first = span_states(key_rows, value_rows, shards)
     slices = exchange(total, "seq")
+    flat = total.reshape(width, CH)
+    shifts = [row_shift(flat, step) for step in (1, 2, 3)]
+    low = call(low_state_kernel, shaped((ROW_BITS, width, CH), BF16), spot, *shifts)
     gain = norm_gain.reshape(1, columns * width)
     table = jnp.transpose(level_table, (1, 2, 0))
     index = jnp.transpose(level_index)
     weights = call(weight_kernel, shaped((tokens, CH), F32), index, table)
-    near = call(near_kernel, shaped((tokens, width), F32), queries, key_rows, value_rows, first, weights)
+    near = call(near_kernel, shaped((tokens, width), F32), queries, key_rows, value_rows, first, low, weights)
     group_states = call(prefix_kernel, shaped((shards, levels * height, CH), BF16), slices)
     states = exchange(group_states, "seq")
     attn = call(far_kernel, shaped((tokens, width), BF16), near, queries, states, weights)
@@ -360,14 +423,22 @@
         gain,
     )
     head_grad = exchange(token_grad, "head")
-    grad, groups = call(
+    grad, groups, low_one, low_two = call(
         grad_kernel,
-        (shaped((tokens, width), BF16), shaped((shards, levels * height + 8, CH), BF16)),
+        (
+            shaped((tokens, width), BF16),
+            shaped((shards, levels * height + 8, CH), BF16),
+            shaped((width, CH), BF16),
+            shaped((width, CH), BF16),
+        ),
+        spot,
         head_grad,
         queries,
         weights,
     )
     group_slices = exchange(groups, "seq")
+    shifts = [row_shift(low_one if step == 1 else low_two, -step) for step in (1, 2, 3)]
+    low_sum = call(low_grad_kernel, shaped((width, CH), F32), *shifts)
     grad_query, near_dk, near_dv, inner, table_part, _ = call(
         back_kernel,
         (
@@ -384,6 +455,7 @@
         grad,
         weights,
         states,
+        low,
         first,
         index,
     )
@@ -400,6 +472,7 @@
             shaped((columns * heads, CH), F32),
         ),
         cross,
+        low_sum,
         inner,
         key_rows,
         value_rows,

time: 140 us -> 137 us (0.979)
  starting transfers between devices: 8.66 us -> 29.6 us
  blocking collectives: 82.3 us -> 63.8 us
  waiting for transfers between devices: 30.6 us -> 24.2 us
    all_to_all x2 -> x3, waiting for transfers between devices: 30.6 us -> 10.4 us  [exchange(): return lax.all_to_all(value, axis, split_axis=0, concat_axis=0, tiled=True)]
    all_to_all x4 -> x3, blocking collectives: 82.3 us -> 63.8 us  [exchange(): return lax.all_to_all(value, axis, split_axis=0, concat_axis=0, tiled=True)]
    ppermute x0 -> x6, waiting for transfers between devices: none -> 13.8 us  [row_shift(): return lax.ppermute(value, 'seq', pairs)]
    ppermute x0 -> x6, starting transfers between devices: none -> 11.9 us  [row_shift(): return lax.ppermute(value, 'seq', pairs)]
    all_to_all x2 -> x3, starting transfers between devices: 8.66 us -> 17.7 us  [exchange(): return lax.all_to_all(value, axis, split_axis=0, concat_axis=0, tiled=True)]
    unnamed x26 -> x30, local copies, waits for them, and re-layouts: 4.28 us -> 5.2 us
    pallas_call x10 -> x11, Pallas kernels: 12.5 us -> 12.7 us  [call(): pl.pallas_call(kernel, out_shape=out_shape, in_specs=[scalar if operand.n...]
  transfers between devices with their start and end apart: 2 -> 9, of which waited for: 2 -> 5; matrix products, arithmetic and copies ran while one was open for 0% -> 0% of each run, Pallas kernels for 4% -> 5%
where the time goes in v4:
time: 137 us
  blocking collectives  63.8 us (47%)
  starting transfers between devices  29.6 us (22%)
  waiting for transfers between devices  24.2 us (18%)
  Pallas kernels  13 us (9%)
  local copies, waits for them, and re-layouts  5.2 us (4%)
    all_to_all x3, blocking collectives, exchange(): return lax.all_to_all(value, axis, split_axis=0, concat_axis=0, tiled=True)  63.8 us
    all_to_all x3, starting transfers between devices, exchange(): return lax.all_to_all(value, axis, split_axis=0, concat_axis=0, tiled=True)  17.7 us
    ppermute x6, waiting for transfers between devices, row_shift(): return lax.ppermute(value, 'seq', pairs)  13.8 us
    pallas_call x11, Pallas kernels, call(): pl.pallas_call(kernel, out_shape=out_shape, in_specs=[scalar if operand.n...  12.7 us
    ppermute x6, starting transfers between devices, row_shift(): return lax.ppermute(value, 'seq', pairs)  11.9 us
    all_to_all x3, waiting for transfers between devices, exchange(): return lax.all_to_all(value, axis, split_axis=0, concat_axis=0, tiled=True)  10.4 us
    unnamed x30, local copies, waits for them, and re-layouts  5.2 us
  transfers between devices with their start and end apart: 9, of which 5 were waited for; matrix products, arithmetic and copies ran while one was open for 0% of the time, Pallas kernels for 5%

profile of v4, /device:TPU:1, one launch (start us, length us, event | category | flops | bytes accessed | tf_op | source)
XLA Modules:
  0.0 136.7 jit_solution(2874288499721029447)
XLA Ops:
  0.6 0.0 copy-start
  0.6 0.9 copy-done
  1.6 0.9 copy-done.2
  2.5 0.3 span_states.1
  2.9 19.6 %all_to_all.30.in_ref = bf16[32,16,128]{2,1,0:T(8,128)(2,1)S(1)} all-to-all(bf16[32,16,128]{2,1,0:T(8,128)(2,1)S(1)} %get-tuple-element.24), channel_id=1, replica_groups=mesh['seq'=32,'head'=16] {'seq'}, dimensions={0} | all-to-all | bytes 262144 | tf_op jit(solution)/shard_map/all_to_all | solution.py:380
  22.5 0.8 shard_map.121
  23.3 4.0 %all-to-all-start.1 = ((bf16[32,48,128]{2,1,0:T(8,128)(2,1)}), bf16[32,48,128]{2,1,0:T(8,128)(2,1)S(1)}, u32[]{:S(2)}, u32[]{:S(2)}) async-start(bf16[32,48,128]{2,1,0:T(8,128)(2,1)} %shard_map.121), calls=%async_computation.1 | async-start | bytes 786432 | tf_op jit(solution)/shard_map/all_to_all | solution.py:380
  27.3 0.0 copy-start.8
  27.3 4.3 %collective-permute-start.2 = (bf16[512,128]{1,0:T(8,128)(2,1)S(1)}, bf16[512,128]{1,0:T(8,128)(2,1)S(1)}, u32[]{:S(2)}, u32[]{:S(2)}) collective-permute-start(bf16[512,128]{1,0:T(8,128)(2,1)S(1)} %bitcast.9), channel_id=1, source_target_pairs={{0,48},{64,112},{128,176},{192,240},{256,304},{320,368},{384,432},... | collective-permute-start | bytes 393224 | tf_op jit(solution)/shard_map/ppermute | solution.py:387
  31.6 1.3 collective-permute-start.1
  32.9 2.5 %collective-permute-start = (bf16[512,128]{1,0:T(8,128)(2,1)S(1)}, bf16[512,128]{1,0:T(8,128)(2,1)S(1)}, u32[]{:S(2)}, u32[]{:S(2)}) collective-permute-start(bf16[512,128]{1,0:T(8,128)(2,1)S(1)} %bitcast.11), channel_id=1, source_target_pairs={{0,16},{16,32},{32,48},{64,80},{80,96},{96,112},{128,144},{144,160... | collective-permute-start | bytes 393224 | tf_op jit(solution)/shard_map/ppermute | solution.py:387
  35.4 0.0 copy-done.10
  35.4 0.0 copy-done.8
  35.4 0.0 copy-start.4
  35.4 0.4 shard_map.119.weight_ref
  35.9 3.5 %collective-permute-done.2.three_ref = bf16[512,128]{1,0:T(8,128)(2,1)S(1)} collective-permute-done((bf16[512,128]{1,0:T(8,128)(2,1)S(1)}, bf16[512,128]{1,0:T(8,128)(2,1)S(1)}, u32[]{:S(2)}, u32[]{:S(2)}) %collective-permute-start.2) | collective-permute-done | bytes 131104 | tf_op jit(solution)/shard_map/ppermute | solution.py:387
  39.3 0.0 collective-permute-done.1.two_ref
  39.3 0.1 collective-permute-done.one_ref
  39.4 0.1 shard_map.118.low_ref
  39.5 0.8 copy-done.1
  40.4 0.1 copy-done.3
  40.4 1.2 shard_map.120.near_ref
  41.6 0.0 all-to-all-done.1.state_ref
  41.7 0.5 shard_map.122
  42.2 0.0 copy-start.7
  42.2 0.0 copy-start.9
  42.2 24.2 %all_to_all.31.attn_ref = bf16[16,16,512]{2,1,0:T(8,128)(2,1)S(1)} all-to-all(bf16[16,16,512]{2,1,0:T(8,128)(2,1)S(1)} %bitcast.8), channel_id=1, replica_groups=mesh['seq'=32,'head'=16] {'head'}, dimensions={0} | all-to-all | bytes 524288 | tf_op jit(solution)/shard_map/all_to_all | solution.py:380
  66.4 1.1 shard_map.123
  67.5 20.0 %all_to_all.32.head_ref = bf16[16,32,512]{2,1,0:T(8,128)(2,1)S(1)} all-to-all(bf16[16,32,512]{2,1,0:T(8,128)(2,1)S(1)} %get-tuple-element.26), channel_id=1, replica_groups=mesh['seq'=32,'head'=16] {'head'}, dimensions={0} | all-to-all | bytes 1048576 | tf_op jit(solution)/shard_map/all_to_all | solution.py:380
  87.5 1.9 %shard_map.124 = (bf16[256,512]{1,0:T(8,128)(2,1)S(1)}, bf16[32,56,128]{2,1,0:T(8,128)(2,1)}, bf16[512,128]{1,0:T(8,128)(2,1)S(1)}, bf16[512,128]{1,0:T(8,128)(2,1)S(1)}) custom-call(s32[1]{0:T(128)} %bitcast.place_ref, bf16[16,32,512]{2,1,0:T(8,128)(2,1)S(1)} %all_to_all.32.head_ref, bf16[256,512]{1,0:T(8,128)(2,1)S(1)} %copy-done.4, ...), custom_call_target="tpu_custom_call" | custom-call | tf_op jit(solution)/shard_map/pallas_call | solution.py:21
  89.4 0.7 copy-done.5
  90.1 0.6 copy-done.11
  90.7 0.0 copy-done.13
  90.8 9.1 %all-to-all-start.4 = ((bf16[32,56,128]{2,1,0:T(8,128)(2,1)}), bf16[32,56,128]{2,1,0:T(8,128)(2,1)S(1)}, u32[]{:S(2)}, u32[]{:S(2)}) async-start(bf16[32,56,128]{2,1,0:T(8,128)(2,1)} %get-tuple-element.29), calls=%async_computation.4 | async-start | bytes 917504 | tf_op jit(solution)/shard_map/all_to_all | solution.py:380
  99.8 0.0 copy-start.6
  99.8 0.9 copy-done.6
  100.8 4.7 %shard_map.125 = (bf16[256,512]{1,0:T(8,128)(2,1)}, f32[256,512]{1,0:T(8,128)S(1)}, f32[256,512]{1,0:T(8,128)S(1)}, f32[512,128]{1,0:T(8,128)S(1)}, bf16[14,128]{1,0:T(8,128)(2,1)S(1)}, /*index=5*/f32[256,128]{1,0:T(8,128)}) custom-call(bf16[256,512]{1,0:T(8,128)(2,1)S(1)} %copy-done.4, bf16[256,512]{1,0:T(8,128)(2,1)S(1)} %copy-done.1, ...), custom_call_target="tpu_custom_call" | custom-call | tf_op jit(solution)/shard_map/pallas_call | solution.py:21
  105.5 10.4 %all-to-all-done.4.in_ref = bf16[32,56,128]{2,1,0:T(8,128)(2,1)S(1)} async-done(((bf16[32,56,128]{2,1,0:T(8,128)(2,1)}), bf16[32,56,128]{2,1,0:T(8,128)(2,1)S(1)}, u32[]{:S(2)}, u32[]{:S(2)}) %all-to-all-start.4) | async-done | bytes 458784 | tf_op jit(solution)/shard_map/all_to_all | solution.py:380
  115.9 0.8 shard_map.126
  116.6 4.6 %all-to-all-start.5 = ((bf16[32,32,128]{2,1,0:T(8,128)(2,1)}), bf16[32,32,128]{2,1,0:T(8,128)(2,1)S(1)}, u32[]{:S(2)}, u32[]{:S(2)}) async-start(bf16[32,32,128]{2,1,0:T(8,128)(2,1)} %shard_map.126), calls=%async_computation.5 | async-start | bytes 524288 | tf_op jit(solution)/shard_map/all_to_all | solution.py:380
  121.3 1.3 collective-permute-start.3
  122.6 1.3 collective-permute-start.5
  123.9 1.3 collective-permute-start.4
  125.2 4.3 %collective-permute-done.3.one_ref = bf16[512,128]{1,0:T(8,128)(2,1)S(1)} collective-permute-done((bf16[512,128]{1,0:T(8,128)(2,1)S(1)}, bf16[512,128]{1,0:T(8,128)(2,1)S(1)}, u32[]{:S(2)}, u32[]{:S(2)}) %collective-permute-start.3) | collective-permute-done | bytes 131104 | tf_op jit(solution)/shard_map/ppermute | solution.py:387
  129.5 6.0 %collective-permute-done.5.three_ref = bf16[512,128]{1,0:T(8,128)(2,1)S(1)} collective-permute-done((bf16[512,128]{1,0:T(8,128)(2,1)S(1)}, bf16[512,128]{1,0:T(8,128)(2,1)S(1)}, u32[]{:S(2)}, u32[]{:S(2)}) %collective-permute-start.5) | collective-permute-done | bytes 131104 | tf_op jit(solution)/shard_map/ppermute | solution.py:387
  135.4 0.0 collective-permute-done.4.two_ref
  135.5 0.0 all-to-all-done.5.cross_ref
  135.5 1.2 shard_map.128
  (15 shorter events, 0.1 us)
Async XLA Ops:
  0.6 1.0 copy-start
  1.6 0.9 copy-start.2
  23.3 12.1 %copy-start.10 = (f32[64,7,4]{0,2,1:T(4,128)S(1)}, f32[64,7,4]{0,2,1:T(4,128)}, u32[]{:S(2)}) copy-start(f32[64,7,4]{0,2,1:T(4,128)} %param.10) | copy-start | bytes 21508
  23.3 18.3 %all-to-all-start.1 = ((bf16[32,48,128]{2,1,0:T(8,128)(2,1)}), bf16[32,48,128]{2,1,0:T(8,128)(2,1)S(1)}, u32[]{:S(2)}, u32[]{:S(2)}) async-start(bf16[32,48,128]{2,1,0:T(8,128)(2,1)} %shard_map.121), calls=%async_computation.1 | async-start | bytes 786432 | tf_op jit(solution)/shard_map/all_to_all | solution.py:380
  27.3 8.1 %copy-start.8 = (s32[256,7]{0,1:T(8,128)S(1)}, s32[256,7]{0,1:T(8,128)}, u32[]{:S(2)}) copy-start(s32[256,7]{0,1:T(8,128)} %param.11) | copy-start | bytes 21508
  27.3 12.0 %collective-permute-start.2 = (bf16[512,128]{1,0:T(8,128)(2,1)S(1)}, bf16[512,128]{1,0:T(8,128)(2,1)S(1)}, u32[]{:S(2)}, u32[]{:S(2)}) collective-permute-start(bf16[512,128]{1,0:T(8,128)(2,1)S(1)} %bitcast.9), channel_id=1, source_target_pairs={{0,48},{64,112},{128,176},{192,240},{256,304},{320,368},{384,432},... | collective-permute-start | bytes 393224 | tf_op jit(solution)/shard_map/ppermute | solution.py:387
  31.6 7.7 %collective-permute-start.1 = (bf16[512,128]{1,0:T(8,128)(2,1)S(1)}, bf16[512,128]{1,0:T(8,128)(2,1)S(1)}, u32[]{:S(2)}, u32[]{:S(2)}) collective-permute-start(bf16[512,128]{1,0:T(8,128)(2,1)S(1)} %bitcast.10), channel_id=1, source_target_pairs={{0,32},{16,48},{64,96},{80,112},{128,160},{144,176},{192,224},{208... | collective-permute-start | bytes 393224 | tf_op jit(solution)/shard_map/ppermute | solution.py:387
  32.9 6.5 %collective-permute-start = (bf16[512,128]{1,0:T(8,128)(2,1)S(1)}, bf16[512,128]{1,0:T(8,128)(2,1)S(1)}, u32[]{:S(2)}, u32[]{:S(2)}) collective-permute-start(bf16[512,128]{1,0:T(8,128)(2,1)S(1)} %bitcast.11), channel_id=1, source_target_pairs={{0,16},{16,32},{32,48},{64,80},{80,96},{96,112},{128,144},{144,160... | collective-permute-start | bytes 393224 | tf_op jit(solution)/shard_map/ppermute | solution.py:387
  35.4 4.1 %copy-start.4 = (bf16[256,512]{1,0:T(8,128)(2,1)S(1)}, bf16[256,512]{1,0:T(8,128)(2,1)}, u32[]{:S(2)}) copy-start(bf16[256,512]{1,0:T(8,128)(2,1)} %query_ref.7) | copy-start | bytes 786436
  39.4 0.9 copy-start.1
  39.4 1.0 copy-start.3
  42.2 24.2 %copy-start.7 = (bf16[16,8192]{1,0:T(8,128)(2,1)S(1)}, bf16[16,8192]{1,0:T(8,128)(2,1)}, u32[]{:S(2)}) copy-start(bf16[16,8192]{1,0:T(8,128)(2,1)} %cot_ref.1) | copy-start | bytes 786436
  42.2 24.2 %copy-start.9 = (f32[8192]{0:T(1024)S(1)}, f32[8192]{0:T(1024)}, u32[]{:S(2)}) copy-start(f32[8192]{0:T(1024)} %param.12) | copy-start | bytes 98308
  89.4 0.7 copy-start.5
  90.1 0.7 copy-start.11
  90.1 0.7 copy-start.13
  90.8 25.1 %all-to-all-start.4 = ((bf16[32,56,128]{2,1,0:T(8,128)(2,1)}), bf16[32,56,128]{2,1,0:T(8,128)(2,1)S(1)}, u32[]{:S(2)}, u32[]{:S(2)}) async-start(bf16[32,56,128]{2,1,0:T(8,128)(2,1)} %get-tuple-element.29), calls=%async_computation.4 | async-start | bytes 917504 | tf_op jit(solution)/shard_map/all_to_all | solution.py:380
  99.8 1.0 copy-start.6
  116.6 4.7 %copy-start.14 = (bf16[512,128]{1,0:T(8,128)(2,1)S(1)}, bf16[512,128]{1,0:T(8,128)(2,1)}, u32[]{:S(2)}) copy-start(bf16[512,128]{1,0:T(8,128)(2,1)} %copy-done.13) | copy-start | bytes 393220
  116.6 6.0 %copy-start.12 = (bf16[512,128]{1,0:T(8,128)(2,1)S(1)}, bf16[512,128]{1,0:T(8,128)(2,1)}, u32[]{:S(2)}) copy-start(bf16[512,128]{1,0:T(8,128)(2,1)} %copy-done.11) | copy-start | bytes 393220
  116.6 18.9 %all-to-all-start.5 = ((bf16[32,32,128]{2,1,0:T(8,128)(2,1)}), bf16[32,32,128]{2,1,0:T(8,128)(2,1)S(1)}, u32[]{:S(2)}, u32[]{:S(2)}) async-start(bf16[32,32,128]{2,1,0:T(8,128)(2,1)} %shard_map.126), calls=%async_computation.5 | async-start | bytes 524288 | tf_op jit(solution)/shard_map/all_to_all | solution.py:380
  121.3 8.2 %collective-permute-start.3 = (bf16[512,128]{1,0:T(8,128)(2,1)S(1)}, bf16[512,128]{1,0:T(8,128)(2,1)S(1)}, u32[]{:S(2)}, u32[]{:S(2)}) collective-permute-start(bf16[512,128]{1,0:T(8,128)(2,1)S(1)} %copy-done.14), channel_id=1, source_target_pairs={{16,0},{32,16},{48,32},{80,64},{96,80},{112,96},{144,128},{160,144... | collective-permute-start | bytes 393224 | tf_op jit(solution)/shard_map/ppermute | solution.py:387
  122.6 12.8 %collective-permute-start.5 = (bf16[512,128]{1,0:T(8,128)(2,1)S(1)}, bf16[512,128]{1,0:T(8,128)(2,1)S(1)}, u32[]{:S(2)}, u32[]{:S(2)}) collective-permute-start(bf16[512,128]{1,0:T(8,128)(2,1)S(1)} %copy-done.12), channel_id=1, source_target_pairs={{48,0},{112,64},{176,128},{240,192},{304,256},{368,320},{432,384},... | collective-permute-start | bytes 393224 | tf_op jit(solution)/shard_map/ppermute | solution.py:387
  123.9 11.5 %collective-permute-start.4 = (bf16[512,128]{1,0:T(8,128)(2,1)S(1)}, bf16[512,128]{1,0:T(8,128)(2,1)S(1)}, u32[]{:S(2)}, u32[]{:S(2)}) collective-permute-start(bf16[512,128]{1,0:T(8,128)(2,1)S(1)} %copy-done.12), channel_id=1, source_target_pairs={{32,0},{48,16},{96,64},{112,80},{160,128},{176,144},{224,192},{240... | collective-permute-start | bytes 393224 | tf_op jit(solution)/shard_map/ppermute | solution.py:387

commit v5 on v4

--- a/solution.py
+++ b/solution.py
@@ -15,13 +15,26 @@
 ROW_BITS = 2
 
 
-def call(kernel, out_shape, *operands):
+def in_hbm(value):
+    return pltpu.with_memory_space_constraint(value, pltpu.MemorySpace.HBM)
+
+
+def call(kernel, out_shape, *operands, hbm=(), hbm_out=(), scratch=()):
     whole = pl.BlockSpec(memory_space=pltpu.VMEM)
     scalar = pl.BlockSpec(memory_space=pltpu.SMEM)
+    apart = pl.BlockSpec(memory_space=pltpu.MemorySpace.HBM)
+    if isinstance(out_shape, tuple):
+        out_specs = tuple(apart if i in hbm_out else whole for i in range(len(out_shape)))
+    else:
+        out_specs = whole
     return pl.pallas_call(
         kernel,
         out_shape=out_shape,
-        in_specs=[scalar if operand.ndim == 1 else whole for operand in operands],
+        in_specs=[
+            apart if i in hbm else scalar if operand.ndim == 1 else whole for i, operand in enumerate(operands)
+        ],
+        out_specs=out_specs,
+        scratch_shapes=scratch,
         interpret=INTERPRET,
         compiler_params=pltpu.CompilerParams(vmem_limit_bytes=16 * 1024 * 1024),
     )(*operands)
@@ -104,7 +117,7 @@
         name="span_states",
         interpret=INTERPRET,
         compiler_params=pltpu.CompilerParams(vmem_limit_bytes=16 * 1024 * 1024),
-    )(key_rows, value_rows)
+    )(in_hbm(key_rows), in_hbm(value_rows))
 
 
 def low_state_kernel(place_ref, one_ref, two_ref, three_ref, state_ref):
@@ -245,7 +258,7 @@
         grad_ref[d, own:, :] = block
 
 
-def grad_kernel(place_ref, head_ref, query_ref, weight_ref, grad_ref, group_ref, one_ref, two_ref):
+def grad_kernel(place_ref, head_ref, query_ref, weight_ref, grad_hbm, group_ref, one_ref, two_ref, grad_ref, sem):
     columns = head_ref.shape[0]
     own = head_ref.shape[1] - columns
     heads = query_ref.shape[1] // CH
@@ -255,6 +268,8 @@
     start = levels * height
     for d in range(columns):
         grad_ref[d * own : (d + 1) * own, :] = head_ref[d, 0:own, :]
+    grad_copy = pltpu.make_async_copy(grad_ref, grad_hbm, sem)
+    grad_copy.start()
     for h in range(heads):
         cols = span_rows(h)
         grad_f = grad_ref[:, cols].astype(F32)
@@ -280,12 +295,16 @@
         high, low = split_pair(jnp.concatenate(picked, axis=0))
         fill = jnp.zeros((extra - 2 * rows, CH), BF16)
         group_ref[s, start:, :] = jnp.concatenate([high, low, fill], axis=0)
+    grad_copy.wait()
 
 
 def back_kernel(
-    query_ref, key_ref, value_ref, grad_ref, weight_ref, state_ref, low_ref, first_ref, index_ref,
-    dq_ref, dk_ref, dv_ref, inner_ref, table_ref, gw_ref,
+    query_ref, key_ref, value_ref, grad_hbm, weight_ref, state_ref, low_ref, first_ref, index_ref,
+    dq_ref, dk_ref, dv_ref, inner_ref, table_ref, gw_ref, grad_ref, sem,
 ):
+    grad_copy = pltpu.make_async_copy(grad_hbm, grad_ref, sem)
+    grad_copy.start()
+    grad_copy.wait()
     heads = query_ref.shape[1] // CH
     spans = query_ref.shape[0] // CH
     height = height_of(heads, state_ref)
@@ -426,7 +445,7 @@
     grad, groups, low_one, low_two = call(
         grad_kernel,
         (
-            shaped((tokens, width), BF16),
+            pltpu.MemorySpace.HBM((tokens, width), BF16),
             shaped((shards, levels * height + 8, CH), BF16),
             shaped((width, CH), BF16),
             shaped((width, CH), BF16),
@@ -435,11 +454,13 @@
         head_grad,
         queries,
         weights,
+        hbm_out=(0,),
+        scratch=(pltpu.VMEM((tokens, width), BF16), pltpu.SemaphoreType.DMA),
     )
     group_slices = exchange(groups, "seq")
     shifts = [row_shift(low_one if step == 1 else low_two, -step) for step in (1, 2, 3)]
     low_sum = call(low_grad_kernel, shaped((width, CH), F32), *shifts)
-    grad_query, near_dk, near_dv, inner, table_part, _ = call(
+    grad_query, near_dk, near_dv, inner, table_part = call(
         back_kernel,
         (
             shaped((tokens, width), BF16),
@@ -447,17 +468,18 @@
             shaped((tokens, width), F32),
             shaped((heads * CH, CH), F32),
             shaped((table_rows, CH), BF16),
-            shaped((tokens, CH), F32),
         ),
         queries,
         key_rows,
         value_rows,
-        grad,
+        in_hbm(grad),
         weights,
         states,
         low,
         first,
         index,
+        hbm=(3,),
+        scratch=(pltpu.VMEM((tokens, CH), F32), pltpu.VMEM((tokens, width), BF16), pltpu.SemaphoreType.DMA),
     )
     key_slices = call(
         suffix_kernel, shaped((shards, height + table_rows + gain_rows, CH), BF16), group_slices, table_part

time: 137 us -> 136 us (level)
  local copies, waits for them, and re-layouts: 5.2 us -> 1.64 us
  Pallas kernels: 13 us -> 15.1 us
    unnamed x30 -> x22, local copies, waits for them, and re-layouts: 5.2 us -> 1.64 us
where the time goes in v5:
time: 136 us; the launch traced here: 135 us
  blocking collectives  63.7 us (47%)
  starting transfers between devices  29.6 us (22%)
  waiting for transfers between devices  24.2 us (18%)
  Pallas kernels  15.1 us (11%)
  local copies, waits for them, and re-layouts  1.64 us (1%)
    all_to_all x3, blocking collectives, exchange(): return lax.all_to_all(value, axis, split_axis=0, concat_axis=0, tiled=True)  63.7 us
    all_to_all x3, starting transfers between devices, exchange(): return lax.all_to_all(value, axis, split_axis=0, concat_axis=0, tiled=True)  17.7 us
    ppermute x6, waiting for transfers between devices, row_shift(): return lax.ppermute(value, 'seq', pairs)  13.8 us
    pallas_call x11, Pallas kernels, call(): pl.pallas_call(kernel, out_shape=out_shape, in_specs=[apart if i in hbm e...  13.8 us
    ppermute x6, starting transfers between devices, row_shift(): return lax.ppermute(value, 'seq', pairs)  11.9 us
    all_to_all x3, waiting for transfers between devices, exchange(): return lax.all_to_all(value, axis, split_axis=0, concat_axis=0, tiled=True)  10.4 us
  transfers between devices with their start and end apart: 9, of which 5 were waited for; matrix products, arithmetic and copies ran while one was open for 0% of the time, Pallas kernels for 5%

profile of v5, /device:TPU:1, one launch (start us, length us, event | category | flops | bytes accessed | tf_op | source)
XLA Modules:
  0.0 135.1 jit_solution(11380537866547771602)
XLA Ops:
  0.6 1.3 span_states.1
  1.9 19.6 %all_to_all.30.in_ref = bf16[32,16,128]{2,1,0:T(8,128)(2,1)S(1)} all-to-all(bf16[32,16,128]{2,1,0:T(8,128)(2,1)S(1)} %get-tuple-element.24), channel_id=1, replica_groups=mesh['seq'=32,'head'=16] {'seq'}, dimensions={0} | all-to-all | bytes 262144 | tf_op jit(solution)/shard_map/all_to_all | solution.py:399
  21.6 0.8 shard_map.121
  22.4 4.0 %all-to-all-start.1 = ((bf16[32,48,128]{2,1,0:T(8,128)(2,1)}), bf16[32,48,128]{2,1,0:T(8,128)(2,1)S(1)}, u32[]{:S(2)}, u32[]{:S(2)}) async-start(bf16[32,48,128]{2,1,0:T(8,128)(2,1)} %shard_map.121), calls=%async_computation.1 | async-start | bytes 786432 | tf_op jit(solution)/shard_map/all_to_all | solution.py:399
  26.4 0.0 copy-start.4
  26.4 4.3 %collective-permute-start.2 = (bf16[512,128]{1,0:T(8,128)(2,1)S(1)}, bf16[512,128]{1,0:T(8,128)(2,1)S(1)}, u32[]{:S(2)}, u32[]{:S(2)}) collective-permute-start(bf16[512,128]{1,0:T(8,128)(2,1)S(1)} %bitcast.9), channel_id=1, source_target_pairs={{0,48},{64,112},{128,176},{192,240},{256,304},{320,368},{384,432},... | collective-permute-start | bytes 393224 | tf_op jit(solution)/shard_map/ppermute | solution.py:406
  30.7 1.3 collective-permute-start.1
  32.0 2.5 %collective-permute-start = (bf16[512,128]{1,0:T(8,128)(2,1)S(1)}, bf16[512,128]{1,0:T(8,128)(2,1)S(1)}, u32[]{:S(2)}, u32[]{:S(2)}) collective-permute-start(bf16[512,128]{1,0:T(8,128)(2,1)S(1)} %bitcast.11), channel_id=1, source_target_pairs={{0,16},{16,32},{32,48},{64,80},{80,96},{96,112},{128,144},{144,160... | collective-permute-start | bytes 393224 | tf_op jit(solution)/shard_map/ppermute | solution.py:406
  34.5 0.0 copy-done.6
  34.5 0.0 copy-done.4
  34.5 0.0 copy-start.2
  34.5 0.4 shard_map.119.weight_ref
  34.9 3.5 %collective-permute-done.2.three_ref = bf16[512,128]{1,0:T(8,128)(2,1)S(1)} collective-permute-done((bf16[512,128]{1,0:T(8,128)(2,1)S(1)}, bf16[512,128]{1,0:T(8,128)(2,1)S(1)}, u32[]{:S(2)}, u32[]{:S(2)}) %collective-permute-start.2) | collective-permute-done | bytes 131104 | tf_op jit(solution)/shard_map/ppermute | solution.py:406
  38.4 0.0 collective-permute-done.1.two_ref
  38.4 0.1 collective-permute-done.one_ref
  38.5 0.1 shard_map.118.low_ref
  38.6 0.0 copy-done.2
  38.6 0.8 copy-done
  39.4 0.1 copy-done.1
  39.5 1.2 shard_map.120.near_ref
  40.7 0.0 all-to-all-done.1.state_ref
  40.7 0.6 shard_map.122
  41.3 0.0 copy-start.3
  41.3 0.0 copy-start.5
  41.3 24.1 %all_to_all.31.attn_ref = bf16[16,16,512]{2,1,0:T(8,128)(2,1)S(1)} all-to-all(bf16[16,16,512]{2,1,0:T(8,128)(2,1)S(1)} %bitcast.8), channel_id=1, replica_groups=mesh['seq'=32,'head'=16] {'head'}, dimensions={0} | all-to-all | bytes 524288 | tf_op jit(solution)/shard_map/all_to_all | solution.py:399
  65.5 0.0 copy-done.3
  65.5 0.0 copy-done.5
  65.5 1.1 shard_map.123
  66.6 20.0 %all_to_all.32.head_ref = bf16[16,32,512]{2,1,0:T(8,128)(2,1)S(1)} all-to-all(bf16[16,32,512]{2,1,0:T(8,128)(2,1)S(1)} %get-tuple-element.26), channel_id=1, replica_groups=mesh['seq'=32,'head'=16] {'head'}, dimensions={0} | all-to-all | bytes 1048576 | tf_op jit(solution)/shard_map/all_to_all | solution.py:399
  86.6 2.0 %shard_map.124 = (bf16[256,512]{1,0:T(8,128)(2,1)}, bf16[32,56,128]{2,1,0:T(8,128)(2,1)}, bf16[512,128]{1,0:T(8,128)(2,1)S(1)}, bf16[512,128]{1,0:T(8,128)(2,1)S(1)}) custom-call(s32[1]{0:T(128)} %bitcast.place_ref, bf16[16,32,512]{2,1,0:T(8,128)(2,1)S(1)} %all_to_all.32.head_ref, bf16[256,512]{1,0:T(8,128)(2,1)S(1)} %copy-done.2, ...), custom_call_target="tpu_custom_call" | custom-call | tf_op jit(solution)/shard_map/pallas_call | solution.py:30
  88.5 0.0 copy-start.7
  88.5 0.0 copy-start.9
  88.5 0.6 copy-done.7
  89.2 0.0 copy-done.9
  89.2 9.1 %all-to-all-start.4 = ((bf16[32,56,128]{2,1,0:T(8,128)(2,1)}), bf16[32,56,128]{2,1,0:T(8,128)(2,1)S(1)}, u32[]{:S(2)}, u32[]{:S(2)}) async-start(bf16[32,56,128]{2,1,0:T(8,128)(2,1)} %get-tuple-element.29), calls=%async_computation.4 | async-start | bytes 917504 | tf_op jit(solution)/shard_map/all_to_all | solution.py:399
  98.3 5.7 %shard_map.125 = (bf16[256,512]{1,0:T(8,128)(2,1)}, f32[256,512]{1,0:T(8,128)S(1)}, f32[256,512]{1,0:T(8,128)S(1)}, f32[512,128]{1,0:T(8,128)S(1)}, bf16[14,128]{1,0:T(8,128)(2,1)S(1)}) custom-call(bf16[256,512]{1,0:T(8,128)(2,1)S(1)} %copy-done.2, bf16[256,512]{1,0:T(8,128)(2,1)S(1)} %copy-done, bf16[256,512]{1,0:T(8,128)(2,1)S(1)} %copy-done.1, ...), custom_call_target="tpu_custom_call" | custom-call | tf_op jit(solution)/shard_map/pallas_call | solution.py:30
  104.0 10.4 %all-to-all-done.4.in_ref = bf16[32,56,128]{2,1,0:T(8,128)(2,1)S(1)} async-done(((bf16[32,56,128]{2,1,0:T(8,128)(2,1)}), bf16[32,56,128]{2,1,0:T(8,128)(2,1)S(1)}, u32[]{:S(2)}, u32[]{:S(2)}) %all-to-all-start.4) | async-done | bytes 458784 | tf_op jit(solution)/shard_map/all_to_all | solution.py:399
  114.3 0.8 shard_map.126
  115.1 4.6 %all-to-all-start.5 = ((bf16[32,32,128]{2,1,0:T(8,128)(2,1)}), bf16[32,32,128]{2,1,0:T(8,128)(2,1)S(1)}, u32[]{:S(2)}, u32[]{:S(2)}) async-start(bf16[32,32,128]{2,1,0:T(8,128)(2,1)} %shard_map.126), calls=%async_computation.5 | async-start | bytes 524288 | tf_op jit(solution)/shard_map/all_to_all | solution.py:399
  119.8 0.0 copy-done.10
  119.8 1.3 collective-permute-start.3
  121.1 1.3 collective-permute-start.5
  122.4 1.3 collective-permute-start.4
  123.7 4.3 %collective-permute-done.3.one_ref = bf16[512,128]{1,0:T(8,128)(2,1)S(1)} collective-permute-done((bf16[512,128]{1,0:T(8,128)(2,1)S(1)}, bf16[512,128]{1,0:T(8,128)(2,1)S(1)}, u32[]{:S(2)}, u32[]{:S(2)}) %collective-permute-start.3) | collective-permute-done | bytes 131104 | tf_op jit(solution)/shard_map/ppermute | solution.py:406
  127.9 6.0 %collective-permute-done.5.three_ref = bf16[512,128]{1,0:T(8,128)(2,1)S(1)} collective-permute-done((bf16[512,128]{1,0:T(8,128)(2,1)S(1)}, bf16[512,128]{1,0:T(8,128)(2,1)S(1)}, u32[]{:S(2)}, u32[]{:S(2)}) %collective-permute-start.5) | collective-permute-done | bytes 131104 | tf_op jit(solution)/shard_map/ppermute | solution.py:406
  133.9 0.0 collective-permute-done.4.two_ref
  134.0 0.0 all-to-all-done.5.cross_ref
  134.0 1.2 shard_map.128
  (7 shorter events, 0.1 us)
Async XLA Ops:
  22.4 12.1 %copy-start.6 = (f32[64,7,4]{0,2,1:T(4,128)S(1)}, f32[64,7,4]{0,2,1:T(4,128)}, u32[]{:S(2)}) copy-start(f32[64,7,4]{0,2,1:T(4,128)} %param.10) | copy-start | bytes 21508
  22.4 18.4 %all-to-all-start.1 = ((bf16[32,48,128]{2,1,0:T(8,128)(2,1)}), bf16[32,48,128]{2,1,0:T(8,128)(2,1)S(1)}, u32[]{:S(2)}, u32[]{:S(2)}) async-start(bf16[32,48,128]{2,1,0:T(8,128)(2,1)} %shard_map.121), calls=%async_computation.1 | async-start | bytes 786432 | tf_op jit(solution)/shard_map/all_to_all | solution.py:399
  26.4 8.1 %copy-start.4 = (s32[256,7]{0,1:T(8,128)S(1)}, s32[256,7]{0,1:T(8,128)}, u32[]{:S(2)}) copy-start(s32[256,7]{0,1:T(8,128)} %param.11) | copy-start | bytes 21508
  26.4 12.0 %collective-permute-start.2 = (bf16[512,128]{1,0:T(8,128)(2,1)S(1)}, bf16[512,128]{1,0:T(8,128)(2,1)S(1)}, u32[]{:S(2)}, u32[]{:S(2)}) collective-permute-start(bf16[512,128]{1,0:T(8,128)(2,1)S(1)} %bitcast.9), channel_id=1, source_target_pairs={{0,48},{64,112},{128,176},{192,240},{256,304},{320,368},{384,432},... | collective-permute-start | bytes 393224 | tf_op jit(solution)/shard_map/ppermute | solution.py:406
  30.7 7.7 %collective-permute-start.1 = (bf16[512,128]{1,0:T(8,128)(2,1)S(1)}, bf16[512,128]{1,0:T(8,128)(2,1)S(1)}, u32[]{:S(2)}, u32[]{:S(2)}) collective-permute-start(bf16[512,128]{1,0:T(8,128)(2,1)S(1)} %bitcast.10), channel_id=1, source_target_pairs={{0,32},{16,48},{64,96},{80,112},{128,160},{144,176},{192,224},{208... | collective-permute-start | bytes 393224 | tf_op jit(solution)/shard_map/ppermute | solution.py:406
  32.0 6.5 %collective-permute-start = (bf16[512,128]{1,0:T(8,128)(2,1)S(1)}, bf16[512,128]{1,0:T(8,128)(2,1)S(1)}, u32[]{:S(2)}, u32[]{:S(2)}) collective-permute-start(bf16[512,128]{1,0:T(8,128)(2,1)S(1)} %bitcast.11), channel_id=1, source_target_pairs={{0,16},{16,32},{32,48},{64,80},{80,96},{96,112},{128,144},{144,160... | collective-permute-start | bytes 393224 | tf_op jit(solution)/shard_map/ppermute | solution.py:406
  34.5 4.1 %copy-start.2 = (bf16[256,512]{1,0:T(8,128)(2,1)S(1)}, bf16[256,512]{1,0:T(8,128)(2,1)}, u32[]{:S(2)}) copy-start(bf16[256,512]{1,0:T(8,128)(2,1)} %query_ref.7) | copy-start | bytes 786436
  38.5 0.9 copy-start
  38.5 1.0 copy-start.1
  41.3 24.2 %copy-start.3 = (bf16[16,8192]{1,0:T(8,128)(2,1)S(1)}, bf16[16,8192]{1,0:T(8,128)(2,1)}, u32[]{:S(2)}) copy-start(bf16[16,8192]{1,0:T(8,128)(2,1)} %cot_ref.1) | copy-start | bytes 786436
  41.3 24.2 %copy-start.5 = (f32[8192]{0:T(1024)S(1)}, f32[8192]{0:T(1024)}, u32[]{:S(2)}) copy-start(f32[8192]{0:T(1024)} %param.12) | copy-start | bytes 98308
  88.5 0.7 copy-start.7
  88.5 0.7 copy-start.9
  89.2 25.1 %all-to-all-start.4 = ((bf16[32,56,128]{2,1,0:T(8,128)(2,1)}), bf16[32,56,128]{2,1,0:T(8,128)(2,1)S(1)}, u32[]{:S(2)}, u32[]{:S(2)}) async-start(bf16[32,56,128]{2,1,0:T(8,128)(2,1)} %get-tuple-element.29), calls=%async_computation.4 | async-start | bytes 917504 | tf_op jit(solution)/shard_map/all_to_all | solution.py:399
  115.1 4.7 %copy-start.10 = (bf16[512,128]{1,0:T(8,128)(2,1)S(1)}, bf16[512,128]{1,0:T(8,128)(2,1)}, u32[]{:S(2)}) copy-start(bf16[512,128]{1,0:T(8,128)(2,1)} %copy-done.9) | copy-start | bytes 393220
  115.1 6.0 %copy-start.8 = (bf16[512,128]{1,0:T(8,128)(2,1)S(1)}, bf16[512,128]{1,0:T(8,128)(2,1)}, u32[]{:S(2)}) copy-start(bf16[512,128]{1,0:T(8,128)(2,1)} %copy-done.7) | copy-start | bytes 393220
  115.1 18.9 %all-to-all-start.5 = ((bf16[32,32,128]{2,1,0:T(8,128)(2,1)}), bf16[32,32,128]{2,1,0:T(8,128)(2,1)S(1)}, u32[]{:S(2)}, u32[]{:S(2)}) async-start(bf16[32,32,128]{2,1,0:T(8,128)(2,1)} %shard_map.126), calls=%async_computation.5 | async-start | bytes 524288 | tf_op jit(solution)/shard_map/all_to_all | solution.py:399
  119.8 8.2 %collective-permute-start.3 = (bf16[512,128]{1,0:T(8,128)(2,1)S(1)}, bf16[512,128]{1,0:T(8,128)(2,1)S(1)}, u32[]{:S(2)}, u32[]{:S(2)}) collective-permute-start(bf16[512,128]{1,0:T(8,128)(2,1)S(1)} %copy-done.10), channel_id=1, source_target_pairs={{16,0},{32,16},{48,32},{80,64},{96,80},{112,96},{144,128},{160,144... | collective-permute-start | bytes 393224 | tf_op jit(solution)/shard_map/ppermute | solution.py:406
  121.1 12.8 %collective-permute-start.5 = (bf16[512,128]{1,0:T(8,128)(2,1)S(1)}, bf16[512,128]{1,0:T(8,128)(2,1)S(1)}, u32[]{:S(2)}, u32[]{:S(2)}) collective-permute-start(bf16[512,128]{1,0:T(8,128)(2,1)S(1)} %copy-done.8), channel_id=1, source_target_pairs={{48,0},{112,64},{176,128},{240,192},{304,256},{368,320},{432,384},... | collective-permute-start | bytes 393224 | tf_op jit(solution)/shard_map/ppermute | solution.py:406
  122.4 11.5 %collective-permute-start.4 = (bf16[512,128]{1,0:T(8,128)(2,1)S(1)}, bf16[512,128]{1,0:T(8,128)(2,1)S(1)}, u32[]{:S(2)}, u32[]{:S(2)}) collective-permute-start(bf16[512,128]{1,0:T(8,128)(2,1)S(1)} %copy-done.8), channel_id=1, source_target_pairs={{32,0},{48,16},{96,64},{112,80},{160,128},{176,144},{224,192},{240... | collective-permute-start | bytes 393224 | tf_op jit(solution)/shard_map/ppermute | solution.py:406

commit v6 on v5

--- a/solution.py
+++ b/solution.py
@@ -121,17 +121,17 @@
 
 
 def low_state_kernel(place_ref, one_ref, two_ref, three_ref, state_ref):
-    row = place_ref[0] & ((1 << ROW_BITS) - 1)
-    one = one_ref[...].astype(F32)
-    two = two_ref[...].astype(F32)
-    three = three_ref[...].astype(F32)
-    state_ref[0] = jnp.where((row & 1) == 1, one, 0.0).astype(BF16)
-    pair = jnp.where(row == 2, two + one, jnp.where(row == 3, three + two, 0.0))
-    state_ref[1] = pair.astype(BF16)
-
-
-def low_grad_kernel(one_ref, two_ref, three_ref, sum_ref):
-    sum_ref[...] = one_ref[...].astype(F32) + two_ref[...].astype(F32) + three_ref[...].astype(F32)
+    row = place_ref[0]
+    pair = two_ref[...].astype(F32) + three_ref[...].astype(F32)
+    state_ref[0] = jnp.where((row & 1) == 1, one_ref[...].astype(F32), 0.0).astype(BF16)
+    state_ref[1] = jnp.where((row & 2) == 2, pair, 0.0).astype(BF16)
+
+
+def low_grad_kernel(place_ref, one_ref, two_ref, three_ref, sum_ref):
+    row = place_ref[0]
+    pair = two_ref[...].astype(F32) + three_ref[...].astype(F32)
+    total = jnp.where((row & 1) == 0, one_ref[...].astype(F32), 0.0)
+    sum_ref[...] = total + jnp.where((row & 2) == 0, pair, 0.0)
 
 
 def prefix_kernel(in_ref, out_ref):
@@ -258,7 +258,7 @@
         grad_ref[d, own:, :] = block
 
 
-def grad_kernel(place_ref, head_ref, query_ref, weight_ref, grad_hbm, group_ref, one_ref, two_ref, grad_ref, sem):
+def grad_kernel(head_ref, query_ref, weight_ref, grad_hbm, group_ref, one_ref, two_ref, grad_ref, sem):
     columns = head_ref.shape[0]
     own = head_ref.shape[1] - columns
     heads = query_ref.shape[1] // CH
@@ -282,7 +282,7 @@
                 low.append(product)
             else:
                 put_slices(group_ref, product, h, height, level - ROW_BITS)
-        one_ref[cols, :] = jnp.where((place_ref[0] & 1) == 1, low[0], low[1]).astype(BF16)
+        one_ref[cols, :] = low[0].astype(BF16)
         two_ref[cols, :] = low[1].astype(BF16)
     gain = head_ref[0, own:, :].astype(F32)
     for d in range(1, columns):
@@ -399,10 +399,8 @@
     return lax.all_to_all(value, axis, split_axis=0, concat_axis=0, tiled=True)
 
 
-def row_shift(value, step):
-    row = 1 << ROW_BITS
-    shards = lax.axis_size("seq")
-    pairs = [(s, s + step) for s in range(shards) if 0 <= s % row + step < row]
+def row_swap(value, mask):
+    pairs = [(s, s ^ mask) for s in range(lax.axis_size("seq"))]
     return lax.ppermute(value, "seq", pairs)
 
 
@@ -423,8 +421,8 @@
     total, first = span_states(key_rows, value_rows, shards)
     slices = exchange(total, "seq")
     flat = total.reshape(width, CH)
-    shifts = [row_shift(flat, step) for step in (1, 2, 3)]
-    low = call(low_state_kernel, shaped((ROW_BITS, width, CH), BF16), spot, *shifts)
+    swaps = [row_swap(flat, mask) for mask in (1, 2, 3)]
+    low = call(low_state_kernel, shaped((ROW_BITS, width, CH), BF16), spot, *swaps)
     gain = norm_gain.reshape(1, columns * width)
     table = jnp.transpose(level_table, (1, 2, 0))
     index = jnp.transpose(level_index)
@@ -450,7 +448,6 @@
             shaped((width, CH), BF16),
             shaped((width, CH), BF16),
         ),
-        spot,
         head_grad,
         queries,
         weights,
@@ -458,8 +455,8 @@
         scratch=(pltpu.VMEM((tokens, width), BF16), pltpu.SemaphoreType.DMA),
     )
     group_slices = exchange(groups, "seq")
-    shifts = [row_shift(low_one if step == 1 else low_two, -step) for step in (1, 2, 3)]
-    low_sum = call(low_grad_kernel, shaped((width, CH), F32), *shifts)
+    swaps = [row_swap(low_one if mask == 1 else low_two, mask) for mask in (1, 2, 3)]
+    low_sum = call(low_grad_kernel, shaped((width, CH), F32), spot, *swaps)
     grad_query, near_dk, near_dv, inner, table_part = call(
         back_kernel,
         (

time: 136 us -> 139 us (1.022)
  the two profiles are of different devices: /device:TPU:1 before, /device:TPU:8 now
where the time goes in v6:
time: 139 us; the launch traced here: 138 us
  blocking collectives  60.3 us (43%)
  starting transfers between devices  39.7 us (29%)
  waiting for transfers between devices  20.4 us (15%)
  Pallas kernels  15 us (11%)
  local copies, waits for them, and re-layouts  1.67 us (1%)
    all_to_all x3, blocking collectives, exchange(): return lax.all_to_all(value, axis, split_axis=0, concat_axis=0, tiled=True)  60.3 us
    all_to_all x3, starting transfers between devices, exchange(): return lax.all_to_all(value, axis, split_axis=0, concat_axis=0, tiled=True)  20 us
    ppermute x6, starting transfers between devices, row_swap(): return lax.ppermute(value, 'seq', pairs)  19.7 us
    pallas_call x11, Pallas kernels, call(): pl.pallas_call(kernel, out_shape=out_shape, in_specs=[apart if i in hbm e...  13.7 us
    all_to_all x3, waiting for transfers between devices, exchange(): return lax.all_to_all(value, axis, split_axis=0, concat_axis=0, tiled=True)  10.3 us
    ppermute x6, waiting for transfers between devices, row_swap(): return lax.ppermute(value, 'seq', pairs)  10.1 us
  transfers between devices with their start and end apart: 9, of which 5 were waited for; matrix products, arithmetic and copies ran while one was open for 0% of the time, Pallas kernels for 5%

profile of v6, /device:TPU:8, one launch (start us, length us, event | category | flops | bytes accessed | tf_op | source)
XLA Modules:
  0.0 138.0 jit_solution(7950955390819931083)
XLA Ops:
  0.6 1.3 span_states.1
  2.0 19.6 %all_to_all.30.in_ref = bf16[32,16,128]{2,1,0:T(8,128)(2,1)S(1)} all-to-all(bf16[32,16,128]{2,1,0:T(8,128)(2,1)S(1)} %get-tuple-element.24), channel_id=1, replica_groups=mesh['seq'=32,'head'=16] {'seq'}, dimensions={0} | all-to-all | bytes 262144 | tf_op jit(solution)/shard_map/all_to_all | solution.py:399
  21.6 0.8 shard_map.121
  22.4 4.7 %all-to-all-start.1 = ((bf16[32,48,128]{2,1,0:T(8,128)(2,1)}), bf16[32,48,128]{2,1,0:T(8,128)(2,1)S(1)}, u32[]{:S(2)}, u32[]{:S(2)}) async-start(bf16[32,48,128]{2,1,0:T(8,128)(2,1)} %shard_map.121), calls=%async_computation.1 | async-start | bytes 786432 | tf_op jit(solution)/shard_map/all_to_all | solution.py:399
  27.1 0.0 copy-start.4
  27.1 4.6 %collective-permute-start.2 = (bf16[512,128]{1,0:T(8,128)(2,1)S(1)}, bf16[512,128]{1,0:T(8,128)(2,1)S(1)}, u32[]{:S(2)}, u32[]{:S(2)}) collective-permute-start(bf16[512,128]{1,0:T(8,128)(2,1)S(1)} %bitcast.9), channel_id=1, source_target_pairs={{0,48},{16,32},{32,16},{48,0},{64,112},{80,96},{96,80},{112,64},{1... | collective-permute-start | bytes 393224 | tf_op jit(solution)/shard_map/ppermute | solution.py:404
  31.7 2.8 %collective-permute-start.1 = (bf16[512,128]{1,0:T(8,128)(2,1)S(1)}, bf16[512,128]{1,0:T(8,128)(2,1)S(1)}, u32[]{:S(2)}, u32[]{:S(2)}) collective-permute-start(bf16[512,128]{1,0:T(8,128)(2,1)S(1)} %bitcast.10), channel_id=1, source_target_pairs={{0,32},{16,48},{32,0},{48,16},{64,96},{80,112},{96,64},{112,80},{1... | collective-permute-start | bytes 393224 | tf_op jit(solution)/shard_map/ppermute | solution.py:404
  34.5 2.5 %collective-permute-start = (bf16[512,128]{1,0:T(8,128)(2,1)S(1)}, bf16[512,128]{1,0:T(8,128)(2,1)S(1)}, u32[]{:S(2)}, u32[]{:S(2)}) collective-permute-start(bf16[512,128]{1,0:T(8,128)(2,1)S(1)} %bitcast.11), channel_id=1, source_target_pairs={{0,16},{16,0},{32,48},{48,32},{64,80},{80,64},{96,112},{112,96},{1... | collective-permute-start | bytes 393224 | tf_op jit(solution)/shard_map/ppermute | solution.py:404
  36.9 0.0 copy-done.6
  37.0 0.0 copy-done.4
  37.0 0.0 copy-start.2
  37.0 0.4 shard_map.119.weight_ref
  37.4 1.1 collective-permute-done.2.three_ref
  38.5 3.2 %collective-permute-done.1.two_ref = bf16[512,128]{1,0:T(8,128)(2,1)S(1)} collective-permute-done((bf16[512,128]{1,0:T(8,128)(2,1)S(1)}, bf16[512,128]{1,0:T(8,128)(2,1)S(1)}, u32[]{:S(2)}, u32[]{:S(2)}) %collective-permute-start.1) | collective-permute-done | bytes 131104 | tf_op jit(solution)/shard_map/ppermute | solution.py:404
  41.7 0.0 collective-permute-done.one_ref
  41.7 0.1 shard_map.118.low_ref
  41.8 0.0 copy-done.2
  41.8 0.9 copy-done
  42.6 0.1 copy-done.1
  42.7 1.2 shard_map.120.near_ref
  43.9 0.0 all-to-all-done.1.state_ref
  43.9 0.6 shard_map.122
  44.5 0.0 copy-start.3
  44.5 0.0 copy-start.5
  44.5 21.5 %all_to_all.31.attn_ref = bf16[16,16,512]{2,1,0:T(8,128)(2,1)S(1)} all-to-all(bf16[16,16,512]{2,1,0:T(8,128)(2,1)S(1)} %bitcast.8), channel_id=1, replica_groups=mesh['seq'=32,'head'=16] {'head'}, dimensions={0} | all-to-all | bytes 524288 | tf_op jit(solution)/shard_map/all_to_all | solution.py:399
  66.0 0.0 copy-done.3
  66.0 0.0 copy-done.5
  66.0 1.1 shard_map.123
  67.1 19.1 %all_to_all.32.head_ref = bf16[16,32,512]{2,1,0:T(8,128)(2,1)S(1)} all-to-all(bf16[16,32,512]{2,1,0:T(8,128)(2,1)S(1)} %get-tuple-element.26), channel_id=1, replica_groups=mesh['seq'=32,'head'=16] {'head'}, dimensions={0} | all-to-all | bytes 1048576 | tf_op jit(solution)/shard_map/all_to_all | solution.py:399
  86.3 1.9 %shard_map.124 = (bf16[256,512]{1,0:T(8,128)(2,1)}, bf16[32,56,128]{2,1,0:T(8,128)(2,1)}, bf16[512,128]{1,0:T(8,128)(2,1)S(1)}, bf16[512,128]{1,0:T(8,128)(2,1)S(1)}) custom-call(bf16[16,32,512]{2,1,0:T(8,128)(2,1)S(1)} %all_to_all.32.head_ref, bf16[256,512]{1,0:T(8,128)(2,1)S(1)} %copy-done.2, f32[256,128]{1,0:T(8,128)S(1)} %shard_map.119.weight_ref), custom_call_target="tpu_custom_call" | custom-call | tf_op jit(solution)/shard_map/pallas_call | solution.py:30
  88.2 0.0 copy-start.7
  88.2 0.0 copy-start.9
  88.2 0.6 copy-done.7
  88.9 0.0 copy-done.9
  88.9 9.2 %all-to-all-start.4 = ((bf16[32,56,128]{2,1,0:T(8,128)(2,1)}), bf16[32,56,128]{2,1,0:T(8,128)(2,1)S(1)}, u32[]{:S(2)}, u32[]{:S(2)}) async-start(bf16[32,56,128]{2,1,0:T(8,128)(2,1)} %get-tuple-element.29), calls=%async_computation.4 | async-start | bytes 917504 | tf_op jit(solution)/shard_map/all_to_all | solution.py:399
  98.1 5.7 %shard_map.125 = (bf16[256,512]{1,0:T(8,128)(2,1)}, f32[256,512]{1,0:T(8,128)S(1)}, f32[256,512]{1,0:T(8,128)S(1)}, f32[512,128]{1,0:T(8,128)S(1)}, bf16[14,128]{1,0:T(8,128)(2,1)S(1)}) custom-call(bf16[256,512]{1,0:T(8,128)(2,1)S(1)} %copy-done.2, bf16[256,512]{1,0:T(8,128)(2,1)S(1)} %copy-done, bf16[256,512]{1,0:T(8,128)(2,1)S(1)} %copy-done.1, ...), custom_call_target="tpu_custom_call" | custom-call | tf_op jit(solution)/shard_map/pallas_call | solution.py:30
  103.8 10.3 %all-to-all-done.4.in_ref = bf16[32,56,128]{2,1,0:T(8,128)(2,1)S(1)} async-done(((bf16[32,56,128]{2,1,0:T(8,128)(2,1)}), bf16[32,56,128]{2,1,0:T(8,128)(2,1)S(1)}, u32[]{:S(2)}, u32[]{:S(2)}) %all-to-all-start.4) | async-done | bytes 458784 | tf_op jit(solution)/shard_map/all_to_all | solution.py:399
  114.1 0.8 shard_map.126
  114.9 6.1 %all-to-all-start.5 = ((bf16[32,32,128]{2,1,0:T(8,128)(2,1)}), bf16[32,32,128]{2,1,0:T(8,128)(2,1)S(1)}, u32[]{:S(2)}, u32[]{:S(2)}) async-start(bf16[32,32,128]{2,1,0:T(8,128)(2,1)} %shard_map.126), calls=%async_computation.5 | async-start | bytes 524288 | tf_op jit(solution)/shard_map/all_to_all | solution.py:399
  121.0 3.4 %collective-permute-start.3 = (bf16[512,128]{1,0:T(8,128)(2,1)S(1)}, bf16[512,128]{1,0:T(8,128)(2,1)S(1)}, u32[]{:S(2)}, u32[]{:S(2)}) collective-permute-start(bf16[512,128]{1,0:T(8,128)(2,1)S(1)} %copy-done.10), channel_id=1, source_target_pairs={{0,16},{16,0},{32,48},{48,32},{64,80},{80,64},{96,112},{112,96},{1... | collective-permute-start | bytes 393224 | tf_op jit(solution)/shard_map/ppermute | solution.py:404
  124.4 4.0 %collective-permute-start.5 = (bf16[512,128]{1,0:T(8,128)(2,1)S(1)}, bf16[512,128]{1,0:T(8,128)(2,1)S(1)}, u32[]{:S(2)}, u32[]{:S(2)}) collective-permute-start(bf16[512,128]{1,0:T(8,128)(2,1)S(1)} %copy-done.8), channel_id=1, source_target_pairs={{0,48},{16,32},{32,16},{48,0},{64,112},{80,96},{96,80},{112,64},{1... | collective-permute-start | bytes 393224 | tf_op jit(solution)/shard_map/ppermute | solution.py:404
  128.4 2.5 %collective-permute-start.4 = (bf16[512,128]{1,0:T(8,128)(2,1)S(1)}, bf16[512,128]{1,0:T(8,128)(2,1)S(1)}, u32[]{:S(2)}, u32[]{:S(2)}) collective-permute-start(bf16[512,128]{1,0:T(8,128)(2,1)S(1)} %copy-done.8), channel_id=1, source_target_pairs={{0,32},{16,48},{32,0},{48,16},{64,96},{80,112},{96,64},{112,80},{1... | collective-permute-start | bytes 393224 | tf_op jit(solution)/shard_map/ppermute | solution.py:404
  130.9 0.0 collective-permute-done.3.one_ref
  130.9 2.2 %collective-permute-done.5.three_ref = bf16[512,128]{1,0:T(8,128)(2,1)S(1)} collective-permute-done((bf16[512,128]{1,0:T(8,128)(2,1)S(1)}, bf16[512,128]{1,0:T(8,128)(2,1)S(1)}, u32[]{:S(2)}, u32[]{:S(2)}) %collective-permute-start.5) | collective-permute-done | bytes 131104 | tf_op jit(solution)/shard_map/ppermute | solution.py:404
  133.1 3.6 %collective-permute-done.4.two_ref = bf16[512,128]{1,0:T(8,128)(2,1)S(1)} collective-permute-done((bf16[512,128]{1,0:T(8,128)(2,1)S(1)}, bf16[512,128]{1,0:T(8,128)(2,1)S(1)}, u32[]{:S(2)}, u32[]{:S(2)}) %collective-permute-start.4) | collective-permute-done | bytes 131104 | tf_op jit(solution)/shard_map/ppermute | solution.py:404
  136.7 0.1 shard_map.127.low_ref
  136.8 0.0 all-to-all-done.5.cross_ref
  136.8 1.2 shard_map.128
  (7 shorter events, 0.0 us)
Async XLA Ops:
  22.4 14.6 %copy-start.6 = (f32[64,7,4]{0,2,1:T(4,128)S(1)}, f32[64,7,4]{0,2,1:T(4,128)}, u32[]{:S(2)}) copy-start(f32[64,7,4]{0,2,1:T(4,128)} %param.10) | copy-start | bytes 21508
  22.4 21.5 %all-to-all-start.1 = ((bf16[32,48,128]{2,1,0:T(8,128)(2,1)}), bf16[32,48,128]{2,1,0:T(8,128)(2,1)S(1)}, u32[]{:S(2)}, u32[]{:S(2)}) async-start(bf16[32,48,128]{2,1,0:T(8,128)(2,1)} %shard_map.121), calls=%async_computation.1 | async-start | bytes 786432 | tf_op jit(solution)/shard_map/all_to_all | solution.py:399
  27.1 9.9 %copy-start.4 = (s32[256,7]{0,1:T(8,128)S(1)}, s32[256,7]{0,1:T(8,128)}, u32[]{:S(2)}) copy-start(s32[256,7]{0,1:T(8,128)} %param.11) | copy-start | bytes 21508
  27.1 11.4 %collective-permute-start.2 = (bf16[512,128]{1,0:T(8,128)(2,1)S(1)}, bf16[512,128]{1,0:T(8,128)(2,1)S(1)}, u32[]{:S(2)}, u32[]{:S(2)}) collective-permute-start(bf16[512,128]{1,0:T(8,128)(2,1)S(1)} %bitcast.9), channel_id=1, source_target_pairs={{0,48},{16,32},{32,16},{48,0},{64,112},{80,96},{96,80},{112,64},{1... | collective-permute-start | bytes 393224 | tf_op jit(solution)/shard_map/ppermute | solution.py:404
  31.7 10.0 %collective-permute-start.1 = (bf16[512,128]{1,0:T(8,128)(2,1)S(1)}, bf16[512,128]{1,0:T(8,128)(2,1)S(1)}, u32[]{:S(2)}, u32[]{:S(2)}) collective-permute-start(bf16[512,128]{1,0:T(8,128)(2,1)S(1)} %bitcast.10), channel_id=1, source_target_pairs={{0,32},{16,48},{32,0},{48,16},{64,96},{80,112},{96,64},{112,80},{1... | collective-permute-start | bytes 393224 | tf_op jit(solution)/shard_map/ppermute | solution.py:404
  34.5 7.2 %collective-permute-start = (bf16[512,128]{1,0:T(8,128)(2,1)S(1)}, bf16[512,128]{1,0:T(8,128)(2,1)S(1)}, u32[]{:S(2)}, u32[]{:S(2)}) collective-permute-start(bf16[512,128]{1,0:T(8,128)(2,1)S(1)} %bitcast.11), channel_id=1, source_target_pairs={{0,16},{16,0},{32,48},{48,32},{64,80},{80,64},{96,112},{112,96},{1... | collective-permute-start | bytes 393224 | tf_op jit(solution)/shard_map/ppermute | solution.py:404
  37.0 4.8 %copy-start.2 = (bf16[256,512]{1,0:T(8,128)(2,1)S(1)}, bf16[256,512]{1,0:T(8,128)(2,1)}, u32[]{:S(2)}) copy-start(bf16[256,512]{1,0:T(8,128)(2,1)} %query_ref.7) | copy-start | bytes 786436
  41.7 1.0 copy-start
  41.7 1.0 copy-start.1
  44.5 21.5 %copy-start.3 = (bf16[16,8192]{1,0:T(8,128)(2,1)S(1)}, bf16[16,8192]{1,0:T(8,128)(2,1)}, u32[]{:S(2)}) copy-start(bf16[16,8192]{1,0:T(8,128)(2,1)} %cot_ref.1) | copy-start | bytes 786436
  44.5 21.5 %copy-start.5 = (f32[8192]{0:T(1024)S(1)}, f32[8192]{0:T(1024)}, u32[]{:S(2)}) copy-start(f32[8192]{0:T(1024)} %param.12) | copy-start | bytes 98308
  88.2 0.7 copy-start.7
  88.2 0.7 copy-start.9
  88.9 25.2 %all-to-all-start.4 = ((bf16[32,56,128]{2,1,0:T(8,128)(2,1)}), bf16[32,56,128]{2,1,0:T(8,128)(2,1)S(1)}, u32[]{:S(2)}, u32[]{:S(2)}) async-start(bf16[32,56,128]{2,1,0:T(8,128)(2,1)} %get-tuple-element.29), calls=%async_computation.4 | async-start | bytes 917504 | tf_op jit(solution)/shard_map/all_to_all | solution.py:399
  114.9 6.1 %copy-start.10 = (bf16[512,128]{1,0:T(8,128)(2,1)S(1)}, bf16[512,128]{1,0:T(8,128)(2,1)}, u32[]{:S(2)}) copy-start(bf16[512,128]{1,0:T(8,128)(2,1)} %copy-done.9) | copy-start | bytes 393220
  114.9 9.5 %copy-start.8 = (bf16[512,128]{1,0:T(8,128)(2,1)S(1)}, bf16[512,128]{1,0:T(8,128)(2,1)}, u32[]{:S(2)}) copy-start(bf16[512,128]{1,0:T(8,128)(2,1)} %copy-done.7) | copy-start | bytes 393220
  114.9 21.9 %all-to-all-start.5 = ((bf16[32,32,128]{2,1,0:T(8,128)(2,1)}), bf16[32,32,128]{2,1,0:T(8,128)(2,1)S(1)}, u32[]{:S(2)}, u32[]{:S(2)}) async-start(bf16[32,32,128]{2,1,0:T(8,128)(2,1)} %shard_map.126), calls=%async_computation.5 | async-start | bytes 524288 | tf_op jit(solution)/shard_map/all_to_all | solution.py:399
  121.0 9.9 %collective-permute-start.3 = (bf16[512,128]{1,0:T(8,128)(2,1)S(1)}, bf16[512,128]{1,0:T(8,128)(2,1)S(1)}, u32[]{:S(2)}, u32[]{:S(2)}) collective-permute-start(bf16[512,128]{1,0:T(8,128)(2,1)S(1)} %copy-done.10), channel_id=1, source_target_pairs={{0,16},{16,0},{32,48},{48,32},{64,80},{80,64},{96,112},{112,96},{1... | collective-permute-start | bytes 393224 | tf_op jit(solution)/shard_map/ppermute | solution.py:404
  124.4 8.7 %collective-permute-start.5 = (bf16[512,128]{1,0:T(8,128)(2,1)S(1)}, bf16[512,128]{1,0:T(8,128)(2,1)S(1)}, u32[]{:S(2)}, u32[]{:S(2)}) collective-permute-start(bf16[512,128]{1,0:T(8,128)(2,1)S(1)} %copy-done.8), channel_id=1, source_target_pairs={{0,48},{16,32},{32,16},{48,0},{64,112},{80,96},{96,80},{112,64},{1... | collective-permute-start | bytes 393224 | tf_op jit(solution)/shard_map/ppermute | solution.py:404
  128.4 8.4 %collective-permute-start.4 = (bf16[512,128]{1,0:T(8,128)(2,1)S(1)}, bf16[512,128]{1,0:T(8,128)(2,1)S(1)}, u32[]{:S(2)}, u32[]{:S(2)}) collective-permute-start(bf16[512,128]{1,0:T(8,128)(2,1)S(1)} %copy-done.8), channel_id=1, source_target_pairs={{0,32},{16,48},{32,0},{48,16},{64,96},{80,112},{96,64},{112,80},{1... | collective-permute-start | bytes 393224 | tf_op jit(solution)/shard_map/ppermute | solution.py:404

commit v7 on v5

--- a/solution.py
+++ b/solution.py
@@ -197,7 +197,7 @@
     weight_ref[...] = jnp.concatenate(rows, axis=0).T
 
 
-def near_kernel(query_ref, key_ref, value_ref, first_ref, low_ref, weight_ref, out_ref):
+def near_kernel(query_ref, key_ref, value_ref, first_ref, weight_ref, out_ref):
     heads = query_ref.shape[1] // CH
     spans = query_ref.shape[0] // CH
     causal = causal_mask()
@@ -210,13 +210,10 @@
             near = weight_ref[rows, h : h + 1] * dot_nn(scores, value_ref[rows, cols])
             if c == 1:
                 near = near + weight_ref[rows, heads + h : heads + h + 1] * dot_nn(query, first_ref[cols, :])
-            for level in range(ROW_BITS):
-                spot = (level + 2) * heads + h
-                near = near + weight_ref[rows, spot : spot + 1] * dot_nn(query, low_ref[level, cols, :])
             out_ref[rows, cols] = near
 
 
-def far_kernel(near_ref, query_ref, state_ref, weight_ref, attn_ref):
+def far_kernel(near_ref, query_ref, state_ref, low_ref, weight_ref, attn_ref):
     heads = query_ref.shape[1] // CH
     spans = query_ref.shape[0] // CH
     height = height_of(heads, state_ref)
@@ -227,9 +224,13 @@
             cols = span_rows(h)
             query = query_ref[rows, cols]
             total = near_ref[rows, cols]
-            for level in range(levels):
-                spot = (level + 2 + ROW_BITS) * heads + h
-                total = total + weight_ref[rows, spot : spot + 1] * dot_nn(query, get_slices(state_ref, h, height, level))
+            for level in range(levels + ROW_BITS):
+                spot = (level + 2) * heads + h
+                if level < ROW_BITS:
+                    state = low_ref[level, cols, :]
+                else:
+                    state = get_slices(state_ref, h, height, level - ROW_BITS)
+                total = total + weight_ref[rows, spot : spot + 1] * dot_nn(query, state)
             attn_ref[rows, cols] = total.astype(BF16)
 
 
@@ -429,10 +430,10 @@
     table = jnp.transpose(level_table, (1, 2, 0))
     index = jnp.transpose(level_index)
     weights = call(weight_kernel, shaped((tokens, CH), F32), index, table)
-    near = call(near_kernel, shaped((tokens, width), F32), queries, key_rows, value_rows, first, low, weights)
+    near = call(near_kernel, shaped((tokens, width), F32), queries, key_rows, value_rows, first, weights)
     group_states = call(prefix_kernel, shaped((shards, levels * height, CH), BF16), slices)
     states = exchange(group_states, "seq")
-    attn = call(far_kernel, shaped((tokens, width), BF16), near, queries, states, weights)
+    attn = call(far_kernel, shaped((tokens, width), BF16), near, queries, states, low, weights)
     token_attn = exchange(attn.reshape(columns, own, width), "head")
     normed, token_grad = call(
         norm_kernel,

time: 136 us -> 134 us (0.985)
  starting transfers between devices: 29.6 us -> 27.5 us
  blocking collectives: 63.7 us -> 65.6 us
    all_to_all x3, starting transfers between devices: 17.7 us -> 15.6 us  [exchange(): return lax.all_to_all(value, axis, split_axis=0, concat_axis=0, tiled=True)]
    all_to_all x3, blocking collectives: 63.7 us -> 65.6 us  [exchange(): return lax.all_to_all(value, axis, split_axis=0, concat_axis=0, tiled=True)]
  transfers between devices with their start and end apart: 9 -> 9, of which waited for: 5 -> 6; matrix products, arithmetic and copies ran while one was open for 0% -> 0% of each run, Pallas kernels for 5% -> 5%
where the time goes in v7:
time: 134 us; the launch traced here: 133 us
  blocking collectives  65.6 us (49%)
  starting transfers between devices  27.5 us (21%)
  waiting for transfers between devices  23.5 us (18%)
  Pallas kernels  15.2 us (11%)
    all_to_all x3, blocking collectives, exchange(): return lax.all_to_all(value, axis, split_axis=0, concat_axis=0, tiled=True)  65.6 us
    all_to_all x3, starting transfers between devices, exchange(): return lax.all_to_all(value, axis, split_axis=0, concat_axis=0, tiled=True)  15.6 us
    pallas_call x11, Pallas kernels, call(): pl.pallas_call(kernel, out_shape=out_shape, in_specs=[apart if i in hbm e...  13.9 us
    ppermute x6, waiting for transfers between devices, row_shift(): return lax.ppermute(value, 'seq', pairs)  12.7 us
    ppermute x6, starting transfers between devices, row_shift(): return lax.ppermute(value, 'seq', pairs)  11.9 us
    all_to_all x3, waiting for transfers between devices, exchange(): return lax.all_to_all(value, axis, split_axis=0, concat_axis=0, tiled=True)  10.7 us
  transfers between devices with their start and end apart: 9, of which 6 were waited for; matrix products, arithmetic and copies ran while one was open for 0% of the time, Pallas kernels for 5%

profile of v7, /device:TPU:1, one launch (start us, length us, event | category | flops | bytes accessed | tf_op | source)
XLA Modules:
  0.0 133.3 jit_solution(9854783688899502077)
XLA Ops:
  0.6 1.3 span_states.1
  1.9 19.6 %all_to_all.30.in_ref = bf16[32,16,128]{2,1,0:T(8,128)(2,1)S(1)} all-to-all(bf16[32,16,128]{2,1,0:T(8,128)(2,1)S(1)} %get-tuple-element.24), channel_id=1, replica_groups=mesh['seq'=32,'head'=16] {'seq'}, dimensions={0} | all-to-all | bytes 262144 | tf_op jit(solution)/shard_map/all_to_all | solution.py:400
  21.6 0.8 shard_map.120
  22.4 4.0 %all-to-all-start.1 = ((bf16[32,48,128]{2,1,0:T(8,128)(2,1)}), bf16[32,48,128]{2,1,0:T(8,128)(2,1)S(1)}, u32[]{:S(2)}, u32[]{:S(2)}) async-start(bf16[32,48,128]{2,1,0:T(8,128)(2,1)} %shard_map.120), calls=%async_computation.1 | async-start | bytes 786432 | tf_op jit(solution)/shard_map/all_to_all | solution.py:400
  26.4 0.0 copy-start.4
  26.4 4.3 %collective-permute-start.2 = (bf16[512,128]{1,0:T(8,128)(2,1)S(1)}, bf16[512,128]{1,0:T(8,128)(2,1)S(1)}, u32[]{:S(2)}, u32[]{:S(2)}) collective-permute-start(bf16[512,128]{1,0:T(8,128)(2,1)S(1)} %bitcast.9), channel_id=1, source_target_pairs={{0,48},{64,112},{128,176},{192,240},{256,304},{320,368},{384,432},... | collective-permute-start | bytes 393224 | tf_op jit(solution)/shard_map/ppermute | solution.py:407
  30.7 1.3 collective-permute-start.1
  32.0 2.5 %collective-permute-start = (bf16[512,128]{1,0:T(8,128)(2,1)S(1)}, bf16[512,128]{1,0:T(8,128)(2,1)S(1)}, u32[]{:S(2)}, u32[]{:S(2)}) collective-permute-start(bf16[512,128]{1,0:T(8,128)(2,1)S(1)} %bitcast.11), channel_id=1, source_target_pairs={{0,16},{16,32},{32,48},{64,80},{80,96},{96,112},{128,144},{144,160... | collective-permute-start | bytes 393224 | tf_op jit(solution)/shard_map/ppermute | solution.py:407
  34.5 0.0 copy-done.6
  34.5 0.0 copy-done.4
  34.5 0.4 shard_map.118.weight_ref
  34.9 0.0 copy-done
  34.9 0.0 copy-done.1
  34.9 0.0 copy-done.2
  35.0 1.0 shard_map.119.near_ref
  36.0 2.4 %collective-permute-done.2.three_ref = bf16[512,128]{1,0:T(8,128)(2,1)S(1)} collective-permute-done((bf16[512,128]{1,0:T(8,128)(2,1)S(1)}, bf16[512,128]{1,0:T(8,128)(2,1)S(1)}, u32[]{:S(2)}, u32[]{:S(2)}) %collective-permute-start.2) | collective-permute-done | bytes 131104 | tf_op jit(solution)/shard_map/ppermute | solution.py:407
  38.4 0.0 collective-permute-done.1.two_ref
  38.4 0.1 collective-permute-done.one_ref
  38.5 0.1 shard_map.121.low_ref
  38.6 0.3 all-to-all-done.1.state_ref
  38.9 0.9 shard_map.122
  39.8 0.0 copy-start.3
  39.8 0.0 copy-start.5
  39.8 26.0 %all_to_all.31.attn_ref = bf16[16,16,512]{2,1,0:T(8,128)(2,1)S(1)} all-to-all(bf16[16,16,512]{2,1,0:T(8,128)(2,1)S(1)} %bitcast.8), channel_id=1, replica_groups=mesh['seq'=32,'head'=16] {'head'}, dimensions={0} | all-to-all | bytes 524288 | tf_op jit(solution)/shard_map/all_to_all | solution.py:400
  65.8 0.0 copy-done.3
  65.8 0.0 copy-done.5
  65.8 1.1 shard_map.123
  66.9 20.0 %all_to_all.32.head_ref = bf16[16,32,512]{2,1,0:T(8,128)(2,1)S(1)} all-to-all(bf16[16,32,512]{2,1,0:T(8,128)(2,1)S(1)} %get-tuple-element.26), channel_id=1, replica_groups=mesh['seq'=32,'head'=16] {'head'}, dimensions={0} | all-to-all | bytes 1048576 | tf_op jit(solution)/shard_map/all_to_all | solution.py:400
  86.9 2.0 %shard_map.124 = (bf16[256,512]{1,0:T(8,128)(2,1)}, bf16[32,56,128]{2,1,0:T(8,128)(2,1)}, bf16[512,128]{1,0:T(8,128)(2,1)S(1)}, bf16[512,128]{1,0:T(8,128)(2,1)S(1)}) custom-call(s32[1]{0:T(128)} %bitcast.2.place_ref, bf16[16,32,512]{2,1,0:T(8,128)(2,1)S(1)} %all_to_all.32.head_ref, bf16[256,512]{1,0:T(8,128)(2,1)S(1)} %copy-done, ...), custom_call_target="tpu_custom_call" | custom-call | tf_op jit(solution)/shard_map/pallas_call | solution.py:30
  88.9 0.0 copy-start.7
  88.9 0.0 copy-start.9
  88.9 0.6 copy-done.7
  89.5 0.0 copy-done.9
  89.5 6.9 %all-to-all-start.4 = ((bf16[32,56,128]{2,1,0:T(8,128)(2,1)}), bf16[32,56,128]{2,1,0:T(8,128)(2,1)S(1)}, u32[]{:S(2)}, u32[]{:S(2)}) async-start(bf16[32,56,128]{2,1,0:T(8,128)(2,1)} %get-tuple-element.29), calls=%async_computation.4 | async-start | bytes 917504 | tf_op jit(solution)/shard_map/all_to_all | solution.py:400
  96.5 5.7 %shard_map.125 = (bf16[256,512]{1,0:T(8,128)(2,1)}, f32[256,512]{1,0:T(8,128)S(1)}, f32[256,512]{1,0:T(8,128)S(1)}, f32[512,128]{1,0:T(8,128)S(1)}, bf16[14,128]{1,0:T(8,128)(2,1)S(1)}) custom-call(bf16[256,512]{1,0:T(8,128)(2,1)S(1)} %copy-done, bf16[256,512]{1,0:T(8,128)(2,1)S(1)} %copy-done.1, bf16[256,512]{1,0:T(8,128)(2,1)S(1)} %copy-done.2, ...), custom_call_target="tpu_custom_call" | custom-call | tf_op jit(solution)/shard_map/pallas_call | solution.py:30
  102.2 10.4 %all-to-all-done.4.in_ref = bf16[32,56,128]{2,1,0:T(8,128)(2,1)S(1)} async-done(((bf16[32,56,128]{2,1,0:T(8,128)(2,1)}), bf16[32,56,128]{2,1,0:T(8,128)(2,1)S(1)}, u32[]{:S(2)}, u32[]{:S(2)}) %all-to-all-start.4) | async-done | bytes 458784 | tf_op jit(solution)/shard_map/all_to_all | solution.py:400
  112.5 0.8 shard_map.126
  113.3 4.6 %all-to-all-start.5 = ((bf16[32,32,128]{2,1,0:T(8,128)(2,1)}), bf16[32,32,128]{2,1,0:T(8,128)(2,1)S(1)}, u32[]{:S(2)}, u32[]{:S(2)}) async-start(bf16[32,32,128]{2,1,0:T(8,128)(2,1)} %shard_map.126), calls=%async_computation.5 | async-start | bytes 524288 | tf_op jit(solution)/shard_map/all_to_all | solution.py:400
  118.0 0.0 copy-done.10
  118.0 1.3 collective-permute-start.3
  119.3 0.0 copy-done.8
  119.3 1.3 collective-permute-start.5
  120.6 1.3 collective-permute-start.4
  121.9 4.3 %collective-permute-done.3.one_ref = bf16[512,128]{1,0:T(8,128)(2,1)S(1)} collective-permute-done((bf16[512,128]{1,0:T(8,128)(2,1)S(1)}, bf16[512,128]{1,0:T(8,128)(2,1)S(1)}, u32[]{:S(2)}, u32[]{:S(2)}) %collective-permute-start.3) | collective-permute-done | bytes 131104 | tf_op jit(solution)/shard_map/ppermute | solution.py:407
  126.1 6.0 %collective-permute-done.5.three_ref = bf16[512,128]{1,0:T(8,128)(2,1)S(1)} collective-permute-done((bf16[512,128]{1,0:T(8,128)(2,1)S(1)}, bf16[512,128]{1,0:T(8,128)(2,1)S(1)}, u32[]{:S(2)}, u32[]{:S(2)}) %collective-permute-start.5) | collective-permute-done | bytes 131104 | tf_op jit(solution)/shard_map/ppermute | solution.py:407
  132.1 0.0 collective-permute-done.4.two_ref
  132.2 0.0 all-to-all-done.5.cross_ref
  132.2 1.2 shard_map.128
  (7 shorter events, 0.1 us)
Async XLA Ops:
  21.6 12.9 %copy-start.6 = (f32[64,7,4]{0,2,1:T(4,128)S(1)}, f32[64,7,4]{0,2,1:T(4,128)}, u32[]{:S(2)}) copy-start(f32[64,7,4]{0,2,1:T(4,128)} %param.10) | copy-start | bytes 21508
  22.4 12.6 %copy-start = (bf16[256,512]{1,0:T(8,128)(2,1)S(1)}, bf16[256,512]{1,0:T(8,128)(2,1)}, u32[]{:S(2)}) copy-start(bf16[256,512]{1,0:T(8,128)(2,1)} %query_ref.7) | copy-start | bytes 786436
  22.4 12.6 %copy-start.1 = (bf16[256,512]{1,0:T(8,128)(2,1)S(1)}, bf16[256,512]{1,0:T(8,128)(2,1)}, u32[]{:S(2)}) copy-start(bf16[256,512]{1,0:T(8,128)(2,1)} %key_ref.5) | copy-start | bytes 786436
  22.4 12.6 %copy-start.2 = (bf16[256,512]{1,0:T(8,128)(2,1)S(1)}, bf16[256,512]{1,0:T(8,128)(2,1)}, u32[]{:S(2)}) copy-start(bf16[256,512]{1,0:T(8,128)(2,1)} %value_ref.5) | copy-start | bytes 786436
  22.4 16.5 %all-to-all-start.1 = ((bf16[32,48,128]{2,1,0:T(8,128)(2,1)}), bf16[32,48,128]{2,1,0:T(8,128)(2,1)S(1)}, u32[]{:S(2)}, u32[]{:S(2)}) async-start(bf16[32,48,128]{2,1,0:T(8,128)(2,1)} %shard_map.120), calls=%async_computation.1 | async-start | bytes 786432 | tf_op jit(solution)/shard_map/all_to_all | solution.py:400
  26.4 8.1 %copy-start.4 = (s32[256,7]{0,1:T(8,128)S(1)}, s32[256,7]{0,1:T(8,128)}, u32[]{:S(2)}) copy-start(s32[256,7]{0,1:T(8,128)} %param.11) | copy-start | bytes 21508
  26.4 12.0 %collective-permute-start.2 = (bf16[512,128]{1,0:T(8,128)(2,1)S(1)}, bf16[512,128]{1,0:T(8,128)(2,1)S(1)}, u32[]{:S(2)}, u32[]{:S(2)}) collective-permute-start(bf16[512,128]{1,0:T(8,128)(2,1)S(1)} %bitcast.9), channel_id=1, source_target_pairs={{0,48},{64,112},{128,176},{192,240},{256,304},{320,368},{384,432},... | collective-permute-start | bytes 393224 | tf_op jit(solution)/shard_map/ppermute | solution.py:407
  30.7 7.7 %collective-permute-start.1 = (bf16[512,128]{1,0:T(8,128)(2,1)S(1)}, bf16[512,128]{1,0:T(8,128)(2,1)S(1)}, u32[]{:S(2)}, u32[]{:S(2)}) collective-permute-start(bf16[512,128]{1,0:T(8,128)(2,1)S(1)} %bitcast.10), channel_id=1, source_target_pairs={{0,32},{16,48},{64,96},{80,112},{128,160},{144,176},{192,224},{208... | collective-permute-start | bytes 393224 | tf_op jit(solution)/shard_map/ppermute | solution.py:407
  32.0 6.5 %collective-permute-start = (bf16[512,128]{1,0:T(8,128)(2,1)S(1)}, bf16[512,128]{1,0:T(8,128)(2,1)S(1)}, u32[]{:S(2)}, u32[]{:S(2)}) collective-permute-start(bf16[512,128]{1,0:T(8,128)(2,1)S(1)} %bitcast.11), channel_id=1, source_target_pairs={{0,16},{16,32},{32,48},{64,80},{80,96},{96,112},{128,144},{144,160... | collective-permute-start | bytes 393224 | tf_op jit(solution)/shard_map/ppermute | solution.py:407
  39.8 26.0 %copy-start.3 = (bf16[16,8192]{1,0:T(8,128)(2,1)S(1)}, bf16[16,8192]{1,0:T(8,128)(2,1)}, u32[]{:S(2)}) copy-start(bf16[16,8192]{1,0:T(8,128)(2,1)} %cot_ref.1) | copy-start | bytes 786436
  39.8 26.0 %copy-start.5 = (f32[8192]{0:T(1024)S(1)}, f32[8192]{0:T(1024)}, u32[]{:S(2)}) copy-start(f32[8192]{0:T(1024)} %param.12) | copy-start | bytes 98308
  88.9 0.7 copy-start.7
  88.9 0.7 copy-start.9
  89.5 23.0 %all-to-all-start.4 = ((bf16[32,56,128]{2,1,0:T(8,128)(2,1)}), bf16[32,56,128]{2,1,0:T(8,128)(2,1)S(1)}, u32[]{:S(2)}, u32[]{:S(2)}) async-start(bf16[32,56,128]{2,1,0:T(8,128)(2,1)} %get-tuple-element.29), calls=%async_computation.4 | async-start | bytes 917504 | tf_op jit(solution)/shard_map/all_to_all | solution.py:400
  113.3 4.7 %copy-start.10 = (bf16[512,128]{1,0:T(8,128)(2,1)S(1)}, bf16[512,128]{1,0:T(8,128)(2,1)}, u32[]{:S(2)}) copy-start(bf16[512,128]{1,0:T(8,128)(2,1)} %copy-done.9) | copy-start | bytes 393220
  113.3 6.0 %copy-start.8 = (bf16[512,128]{1,0:T(8,128)(2,1)S(1)}, bf16[512,128]{1,0:T(8,128)(2,1)}, u32[]{:S(2)}) copy-start(bf16[512,128]{1,0:T(8,128)(2,1)} %copy-done.7) | copy-start | bytes 393220
  113.3 18.9 %all-to-all-start.5 = ((bf16[32,32,128]{2,1,0:T(8,128)(2,1)}), bf16[32,32,128]{2,1,0:T(8,128)(2,1)S(1)}, u32[]{:S(2)}, u32[]{:S(2)}) async-start(bf16[32,32,128]{2,1,0:T(8,128)(2,1)} %shard_map.126), calls=%async_computation.5 | async-start | bytes 524288 | tf_op jit(solution)/shard_map/all_to_all | solution.py:400
  118.0 8.2 %collective-permute-start.3 = (bf16[512,128]{1,0:T(8,128)(2,1)S(1)}, bf16[512,128]{1,0:T(8,128)(2,1)S(1)}, u32[]{:S(2)}, u32[]{:S(2)}) collective-permute-start(bf16[512,128]{1,0:T(8,128)(2,1)S(1)} %copy-done.10), channel_id=1, source_target_pairs={{16,0},{32,16},{48,32},{80,64},{96,80},{112,96},{144,128},{160,144... | collective-permute-start | bytes 393224 | tf_op jit(solution)/shard_map/ppermute | solution.py:407
  119.3 12.8 %collective-permute-start.5 = (bf16[512,128]{1,0:T(8,128)(2,1)S(1)}, bf16[512,128]{1,0:T(8,128)(2,1)S(1)}, u32[]{:S(2)}, u32[]{:S(2)}) collective-permute-start(bf16[512,128]{1,0:T(8,128)(2,1)S(1)} %copy-done.8), channel_id=1, source_target_pairs={{48,0},{112,64},{176,128},{240,192},{304,256},{368,320},{432,384},... | collective-permute-start | bytes 393224 | tf_op jit(solution)/shard_map/ppermute | solution.py:407
  120.6 11.5 %collective-permute-start.4 = (bf16[512,128]{1,0:T(8,128)(2,1)S(1)}, bf16[512,128]{1,0:T(8,128)(2,1)S(1)}, u32[]{:S(2)}, u32[]{:S(2)}) collective-permute-start(bf16[512,128]{1,0:T(8,128)(2,1)S(1)} %copy-done.8), channel_id=1, source_target_pairs={{32,0},{48,16},{96,64},{112,80},{160,128},{176,144},{224,192},{240... | collective-permute-start | bytes 393224 | tf_op jit(solution)/shard_map/ppermute | solution.py:407

commit v8 on v4

--- a/solution.py
+++ b/solution.py
@@ -15,13 +15,20 @@
 ROW_BITS = 2
 
 
-def call(kernel, out_shape, *operands):
+def in_hbm(value):
+    return pltpu.with_memory_space_constraint(value, pltpu.MemorySpace.HBM)
+
+
+def call(kernel, out_shape, *operands, scratch=()):
     whole = pl.BlockSpec(memory_space=pltpu.VMEM)
     scalar = pl.BlockSpec(memory_space=pltpu.SMEM)
     return pl.pallas_call(
         kernel,
         out_shape=out_shape,
-        in_specs=[scalar if operand.ndim == 1 else whole for operand in operands],
+        in_specs=[
+            scalar if operand.ndim == 1 else whole for operand in operands
+        ],
+        scratch_shapes=scratch,
         interpret=INTERPRET,
         compiler_params=pltpu.CompilerParams(vmem_limit_bytes=16 * 1024 * 1024),
     )(*operands)
@@ -104,17 +111,7 @@
         name="span_states",
         interpret=INTERPRET,
         compiler_params=pltpu.CompilerParams(vmem_limit_bytes=16 * 1024 * 1024),
-    )(key_rows, value_rows)
-
-
-def low_state_kernel(place_ref, one_ref, two_ref, three_ref, state_ref):
-    row = place_ref[0] & ((1 << ROW_BITS) - 1)
-    one = one_ref[...].astype(F32)
-    two = two_ref[...].astype(F32)
-    three = three_ref[...].astype(F32)
-    state_ref[0] = jnp.where((row & 1) == 1, one, 0.0).astype(BF16)
-    pair = jnp.where(row == 2, two + one, jnp.where(row == 3, three + two, 0.0))
-    state_ref[1] = pair.astype(BF16)
+    )(in_hbm(key_rows), in_hbm(value_rows))
 
 
 def low_grad_kernel(one_ref, two_ref, three_ref, sum_ref):
@@ -125,13 +122,11 @@
     shards, height = in_ref.shape[0], in_ref.shape[1]
     levels = out_ref.shape[1] // height
     sums = [in_ref[s].astype(F32) for s in range(shards)]
-    for _ in range(ROW_BITS):
-        sums = [sums[2 * i] + sums[2 * i + 1] for i in range(len(sums) // 2)]
     zero = jnp.zeros(in_ref.shape[1:], BF16)
     for level in range(levels):
         rounded = [s.astype(BF16) for s in sums]
         for t in range(shards):
-            group = t >> (level + ROW_BITS)
+            group = t >> level
             out_ref[t, level * height : (level + 1) * height, :] = rounded[group - 1] if group & 1 else zero
         sums = [sums[2 * i] + sums[2 * i + 1] for i in range(len(sums) // 2)]
 
@@ -184,7 +179,7 @@
     weight_ref[...] = jnp.concatenate(rows, axis=0).T
 
 
-def near_kernel(query_ref, key_ref, value_ref, first_ref, low_ref, weight_ref, out_ref):
+def near_kernel(query_ref, key_ref, value_ref, first_ref, weight_ref, out_ref):
     heads = query_ref.shape[1] // CH
     spans = query_ref.shape[0] // CH
     causal = causal_mask()
@@ -197,9 +192,6 @@
             near = weight_ref[rows, h : h + 1] * dot_nn(scores, value_ref[rows, cols])
             if c == 1:
                 near = near + weight_ref[rows, heads + h : heads + h + 1] * dot_nn(query, first_ref[cols, :])
-            for level in range(ROW_BITS):
-                spot = (level + 2) * heads + h
-                near = near + weight_ref[rows, spot : spot + 1] * dot_nn(query, low_ref[level, cols, :])
             out_ref[rows, cols] = near
 
 
@@ -215,8 +207,9 @@
             query = query_ref[rows, cols]
             total = near_ref[rows, cols]
             for level in range(levels):
-                spot = (level + 2 + ROW_BITS) * heads + h
-                total = total + weight_ref[rows, spot : spot + 1] * dot_nn(query, get_slices(state_ref, h, height, level))
+                spot = (level + 2) * heads + h
+                state = get_slices(state_ref, h, height, level)
+                total = total + weight_ref[rows, spot : spot + 1] * dot_nn(query, state)
             attn_ref[rows, cols] = total.astype(BF16)
 
 
@@ -245,7 +238,7 @@
         grad_ref[d, own:, :] = block
 
 
-def grad_kernel(place_ref, head_ref, query_ref, weight_ref, grad_ref, group_ref, one_ref, two_ref):
+def grad_kernel(place_ref, head_ref, query_ref, weight_ref, group_ref, one_ref, two_ref, grad_ref):
     columns = head_ref.shape[0]
     own = head_ref.shape[1] - columns
     heads = query_ref.shape[1] // CH
@@ -283,13 +276,16 @@
 
 
 def back_kernel(
-    query_ref, key_ref, value_ref, grad_ref, weight_ref, state_ref, low_ref, first_ref, index_ref,
-    dq_ref, dk_ref, dv_ref, inner_ref, table_ref, gw_ref,
+    query_ref, key_ref, value_ref, head_ref, weight_ref, state_ref, first_ref, index_ref,
+    dq_ref, dk_ref, dv_ref, inner_ref, table_ref, gw_ref, grad_ref,
 ):
+    own = head_ref.shape[1] - head_ref.shape[0]
+    for d in range(head_ref.shape[0]):
+        grad_ref[d * own : (d + 1) * own, :] = head_ref[d, 0:own, :]
     heads = query_ref.shape[1] // CH
     spans = query_ref.shape[0] // CH
     height = height_of(heads, state_ref)
-    levels = state_ref.shape[1] // height + ROW_BITS
+    levels = state_ref.shape[1] // height
     all_levels = levels + 2
     causal = causal_mask()
     gw_ref[...] = jnp.zeros(gw_ref.shape, F32)
@@ -319,11 +315,7 @@
                 inner_ref[cols, :] = dot_tn(query, (weight * grad.astype(F32)).astype(BF16))
             for level in range(levels):
                 spot = (level + 2) * heads + h
-                if level < ROW_BITS:
-                    state = low_ref[level, cols, :]
-                else:
-                    state = get_slices(state_ref, h, height, level - ROW_BITS)
-                far = dot_nt(grad, state)
+                far = dot_nt(grad, get_slices(state_ref, h, height, level))
                 gw_ref[rows, spot : spot + 1] = jnp.sum(query_f * far, axis=1, keepdims=True)
                 dq = dq + weight_ref[rows, spot : spot + 1] * far
             dq_ref[rows, cols] = dq.astype(BF16)
@@ -393,7 +385,8 @@
     all_levels = level_table.shape[1]
     shards = lax.axis_size("seq")
     columns = lax.axis_size("head")
-    levels = shards.bit_length() - 1 - ROW_BITS
+    all_bits = shards.bit_length() - 1
+    levels = all_bits - ROW_BITS
     height = heads * CH // shards
     own = tokens // columns
     table_rows = all_levels * heads * TABLE // CH
@@ -403,15 +396,12 @@
 
     total, first = span_states(key_rows, value_rows, shards)
     slices = exchange(total, "seq")
-    flat = total.reshape(width, CH)
-    shifts = [row_shift(flat, step) for step in (1, 2, 3)]
-    low = call(low_state_kernel, shaped((ROW_BITS, width, CH), BF16), spot, *shifts)
     gain = norm_gain.reshape(1, columns * width)
     table = jnp.transpose(level_table, (1, 2, 0))
     index = jnp.transpose(level_index)
     weights = call(weight_kernel, shaped((tokens, CH), F32), index, table)
-    near = call(near_kernel, shaped((tokens, width), F32), queries, key_rows, value_rows, first, low, weights)
-    group_states = call(prefix_kernel, shaped((shards, levels * height, CH), BF16), slices)
+    near = call(near_kernel, shaped((tokens, width), F32), queries, key_rows, value_rows, first, weights)
+    group_states = call(prefix_kernel, shaped((shards, all_bits * height, CH), BF16), slices)
     states = exchange(group_states, "seq")
     attn = call(far_kernel, shaped((tokens, width), BF16), near, queries, states, weights)
     token_attn = exchange(attn.reshape(columns, own, width), "head")
@@ -423,10 +413,9 @@
         gain,
     )
     head_grad = exchange(token_grad, "head")
-    grad, groups, low_one, low_two = call(
+    groups, low_one, low_two = call(
         grad_kernel,
         (
-            shaped((tokens, width), BF16),
             shaped((shards, levels * height + 8, CH), BF16),
             shaped((width, CH), BF16),
             shaped((width, CH), BF16),
@@ -435,11 +424,12 @@
         head_grad,
         queries,
         weights,
+        scratch=(pltpu.VMEM((tokens, width), BF16),),
     )
     group_slices = exchange(groups, "seq")
     shifts = [row_shift(low_one if step == 1 else low_two, -step) for step in (1, 2, 3)]
     low_sum = call(low_grad_kernel, shaped((width, CH), F32), *shifts)
-    grad_query, near_dk, near_dv, inner, table_part, _ = call(
+    grad_query, near_dk, near_dv, inner, table_part = call(
         back_kernel,
         (
             shaped((tokens, width), BF16),
@@ -447,17 +437,16 @@
             shaped((tokens, width), F32),
             shaped((heads * CH, CH), F32),
             shaped((table_rows, CH), BF16),
-            shaped((tokens, CH), F32),
         ),
         queries,
         key_rows,
         value_rows,
-        grad,
+        head_grad,
         weights,
         states,
-        low,
         first,
         index,
+        scratch=(pltpu.VMEM((tokens, CH), F32), pltpu.VMEM((tokens, width), BF16)),
     )
     key_slices = call(
         suffix_kernel, shaped((shards, height + table_rows + gain_rows, CH), BF16), group_slices, table_part

time: 137 us -> 138 us (level)
  waiting for transfers between devices: 24.2 us -> 54.3 us
  blocking collectives: 63.8 us -> 45 us
  starting transfers between devices: 29.6 us -> 20.9 us
  local copies, waits for them, and re-layouts: 5.2 us -> 2.17 us
  Pallas kernels: 13 us -> 14.4 us
    all_to_all x3 -> x4, waiting for transfers between devices: 10.4 us -> 43.4 us  [exchange(): return lax.all_to_all(value, axis, split_axis=0, concat_axis=0, tiled=True)]
    all_to_all x3 -> x2, blocking collectives: 63.8 us -> 45 us  [exchange(): return lax.all_to_all(value, axis, split_axis=0, concat_axis=0, tiled=True)]
    ppermute x6 -> x3, starting transfers between devices: 11.9 us -> 3.88 us  [row_shift(): return lax.ppermute(value, 'seq', pairs)]
    unnamed x30 -> x26, local copies, waits for them, and re-layouts: 5.2 us -> 2.17 us
    ppermute x6 -> x3, waiting for transfers between devices: 13.8 us -> 10.9 us  [row_shift(): return lax.ppermute(value, 'seq', pairs)]
    all_to_all x3 -> x4, starting transfers between devices: 17.7 us -> 17 us  [exchange(): return lax.all_to_all(value, axis, split_axis=0, concat_axis=0, tiled=True)]
    pallas_call x11 -> x10, Pallas kernels: 12.7 us -> 13.1 us  [call(): pl.pallas_call(kernel, out_shape=out_shape, in_specs=[scalar if operand.n...]
  transfers between devices with their start and end apart: 9 -> 7, of which waited for: 5 -> 6; matrix products, arithmetic and copies ran while one was open for 0% -> 0% of each run, Pallas kernels for 5% -> 5%
where the time goes in v8:
time: 138 us
  waiting for transfers between devices  54.3 us (39%)
  blocking collectives  45 us (33%)
  starting transfers between devices  20.9 us (15%)
  Pallas kernels  14.4 us (10%)
  local copies, waits for them, and re-layouts  2.17 us (2%)
    all_to_all x2, blocking collectives, exchange(): return lax.all_to_all(value, axis, split_axis=0, concat_axis=0, tiled=True)  45 us
    all_to_all x4, waiting for transfers between devices, exchange(): return lax.all_to_all(value, axis, split_axis=0, concat_axis=0, tiled=True)  43.4 us
    all_to_all x4, starting transfers between devices, exchange(): return lax.all_to_all(value, axis, split_axis=0, concat_axis=0, tiled=True)  17 us
    pallas_call x10, Pallas kernels, call(): pl.pallas_call(kernel, out_shape=out_shape, in_specs=[scalar if operand.n...  13.1 us
    ppermute x3, waiting for transfers between devices, row_shift(): return lax.ppermute(value, 'seq', pairs)  10.9 us
    ppermute x3, starting transfers between devices, row_shift(): return lax.ppermute(value, 'seq', pairs)  3.88 us
  transfers between devices with their start and end apart: 7, of which 6 were waited for; matrix products, arithmetic and copies ran while one was open for 0% of the time, Pallas kernels for 5%

profile of v8, /device:TPU:1, one launch (start us, length us, event | category | flops | bytes accessed | tf_op | source)
XLA Modules:
  0.0 137.6 jit_solution(10784874778167861042)
XLA Ops:
  0.6 1.3 span_states.1
  1.9 19.6 %all_to_all.30.in_ref = bf16[32,16,128]{2,1,0:T(8,128)(2,1)S(1)} all-to-all(bf16[32,16,128]{2,1,0:T(8,128)(2,1)S(1)} %get-tuple-element.23), channel_id=1, replica_groups=mesh['seq'=32,'head'=16] {'seq'}, dimensions={0} | all-to-all | bytes 262144 | tf_op jit(solution)/shard_map/all_to_all | solution.py:372
  21.6 0.9 shard_map.120
  22.5 0.0 copy-start.6
  22.5 0.0 copy-start.8
  22.5 0.0 copy-start
  22.5 0.0 copy-start.1
  22.5 0.0 copy-start.2
  22.5 4.0 %all-to-all-start.1 = ((bf16[32,80,128]{2,1,0:T(8,128)(2,1)}), bf16[32,80,128]{2,1,0:T(8,128)(2,1)S(1)}, u32[]{:S(2)}, u32[]{:S(2)}) async-start(bf16[32,80,128]{2,1,0:T(8,128)(2,1)} %shard_map.120), calls=%async_computation.1 | async-start | bytes 1310720 | tf_op jit(solution)/shard_map/all_to_all | solution.py:372
  26.6 0.0 copy-done.6
  26.6 0.0 copy-done.8
  26.6 0.4 shard_map.118.weight_ref
  27.0 0.0 copy-done
  27.0 0.0 copy-done.1
  27.0 0.0 copy-done.2
  27.1 1.0 shard_map.119.near_ref
  28.1 16.2 %all-to-all-done.1.state_ref = bf16[32,80,128]{2,1,0:T(8,128)(2,1)S(1)} async-done(((bf16[32,80,128]{2,1,0:T(8,128)(2,1)}), bf16[32,80,128]{2,1,0:T(8,128)(2,1)S(1)}, u32[]{:S(2)}, u32[]{:S(2)}) %all-to-all-start.1) | async-done | bytes 655392 | tf_op jit(solution)/shard_map/all_to_all | solution.py:372
  44.3 0.9 shard_map.121
  45.2 0.0 copy-start.5
  45.2 0.0 copy-start.7
  45.2 25.3 %all_to_all.31.attn_ref = bf16[16,16,512]{2,1,0:T(8,128)(2,1)S(1)} all-to-all(bf16[16,16,512]{2,1,0:T(8,128)(2,1)S(1)} %bitcast.7), channel_id=1, replica_groups=mesh['seq'=32,'head'=16] {'head'}, dimensions={0} | all-to-all | bytes 524288 | tf_op jit(solution)/shard_map/all_to_all | solution.py:372
  70.5 0.0 copy-done.5
  70.5 0.0 copy-done.7
  70.5 1.3 shard_map.122
  71.9 3.5 %all-to-all-start.3 = ((bf16[16,32,512]{2,1,0:T(8,128)(2,1)}), bf16[16,32,512]{2,1,0:T(8,128)(2,1)S(1)}, u32[]{:S(2)}, u32[]{:S(2)}) async-start(bf16[16,32,512]{2,1,0:T(8,128)(2,1)} %get-tuple-element.25), calls=%async_computation.3 | async-start | bytes 1048576 | tf_op jit(solution)/shard_map/all_to_all | solution.py:372
  75.3 16.8 %all-to-all-done.3.head_ref = bf16[16,32,512]{2,1,0:T(8,128)(2,1)S(1)} async-done(((bf16[16,32,512]{2,1,0:T(8,128)(2,1)}), bf16[16,32,512]{2,1,0:T(8,128)(2,1)S(1)}, u32[]{:S(2)}, u32[]{:S(2)}) %all-to-all-start.3) | async-done | bytes 524320 | tf_op jit(solution)/shard_map/all_to_all | solution.py:372
  92.1 1.9 %shard_map.124 = (bf16[32,56,128]{2,1,0:T(8,128)(2,1)}, bf16[512,128]{1,0:T(8,128)(2,1)S(1)}, bf16[512,128]{1,0:T(8,128)(2,1)S(1)}) custom-call(s32[1]{0:T(128)} %bitcast.4.place_ref, bf16[16,32,512]{2,1,0:T(8,128)(2,1)S(1)} %all-to-all-done.3.head_ref, bf16[256,512]{1,0:T(8,128)(2,1)S(1)} %copy-done, f32[256,128]{1,0:T(8,128)S(1)} %shard_map.118.weight_ref), custom_call_target="tpu_custom_call" | custom-call | tf_op jit(solution)/shard_map/pallas_call | solution.py:25
  93.9 0.0 copy-start.9
  94.0 0.7 copy-done.9
  94.6 0.0 copy-start.11
  94.6 0.7 copy-done.11
  95.3 4.6 %all-to-all-start.4 = ((bf16[32,56,128]{2,1,0:T(8,128)(2,1)}), bf16[32,56,128]{2,1,0:T(8,128)(2,1)S(1)}, u32[]{:S(2)}, u32[]{:S(2)}) async-start(bf16[32,56,128]{2,1,0:T(8,128)(2,1)} %get-tuple-element.27), calls=%async_computation.4 | async-start | bytes 917504 | tf_op jit(solution)/shard_map/all_to_all | solution.py:372
  99.9 4.7 %shard_map.123 = (bf16[256,512]{1,0:T(8,128)(2,1)}, f32[256,512]{1,0:T(8,128)S(1)}, f32[256,512]{1,0:T(8,128)S(1)}, f32[512,128]{1,0:T(8,128)S(1)}, bf16[14,128]{1,0:T(8,128)(2,1)S(1)}) custom-call(bf16[256,512]{1,0:T(8,128)(2,1)S(1)} %copy-done, bf16[256,512]{1,0:T(8,128)(2,1)S(1)} %copy-done.1, bf16[256,512]{1,0:T(8,128)(2,1)S(1)} %copy-done.2, ...), custom_call_target="tpu_custom_call" | custom-call | tf_op jit(solution)/shard_map/pallas_call | solution.py:25
  104.6 0.8 copy-done.3
  105.5 10.4 %all-to-all-done.4.in_ref = bf16[32,56,128]{2,1,0:T(8,128)(2,1)S(1)} async-done(((bf16[32,56,128]{2,1,0:T(8,128)(2,1)}), bf16[32,56,128]{2,1,0:T(8,128)(2,1)S(1)}, u32[]{:S(2)}, u32[]{:S(2)}) %all-to-all-start.4) | async-done | bytes 458784 | tf_op jit(solution)/shard_map/all_to_all | solution.py:372
  115.9 0.8 shard_map.125
  116.7 4.9 %all-to-all-start.5 = ((bf16[32,32,128]{2,1,0:T(8,128)(2,1)}), bf16[32,32,128]{2,1,0:T(8,128)(2,1)S(1)}, u32[]{:S(2)}, u32[]{:S(2)}) async-start(bf16[32,32,128]{2,1,0:T(8,128)(2,1)} %shard_map.125), calls=%async_computation.5 | async-start | bytes 524288 | tf_op jit(solution)/shard_map/all_to_all | solution.py:372
  121.6 0.0 copy-done.12
  121.6 1.3 collective-permute-start
  122.9 0.0 copy-done.10
  122.9 1.3 collective-permute-start.1
  124.2 1.3 collective-permute-start.2
  125.5 4.3 %collective-permute-done.one_ref = bf16[512,128]{1,0:T(8,128)(2,1)S(1)} collective-permute-done((bf16[512,128]{1,0:T(8,128)(2,1)S(1)}, bf16[512,128]{1,0:T(8,128)(2,1)S(1)}, u32[]{:S(2)}, u32[]{:S(2)}) %collective-permute-start) | collective-permute-done | bytes 131104 | tf_op jit(solution)/shard_map/ppermute | solution.py:379
  129.7 2.7 %collective-permute-done.1.two_ref = bf16[512,128]{1,0:T(8,128)(2,1)S(1)} collective-permute-done((bf16[512,128]{1,0:T(8,128)(2,1)S(1)}, bf16[512,128]{1,0:T(8,128)(2,1)S(1)}, u32[]{:S(2)}, u32[]{:S(2)}) %collective-permute-start.1) | collective-permute-done | bytes 131104 | tf_op jit(solution)/shard_map/ppermute | solution.py:379
  132.5 3.9 %collective-permute-done.2.three_ref = bf16[512,128]{1,0:T(8,128)(2,1)S(1)} collective-permute-done((bf16[512,128]{1,0:T(8,128)(2,1)S(1)}, bf16[512,128]{1,0:T(8,128)(2,1)S(1)}, u32[]{:S(2)}, u32[]{:S(2)}) %collective-permute-start.2) | collective-permute-done | bytes 131104 | tf_op jit(solution)/shard_map/ppermute | solution.py:379
  136.4 0.0 all-to-all-done.5.cross_ref
  136.5 0.0 copy-done.4
  136.5 1.2 shard_map.127
  (5 shorter events, 0.1 us)
Async XLA Ops:
  22.5 4.1 %copy-start.6 = (s32[256,7]{0,1:T(8,128)S(1)}, s32[256,7]{0,1:T(8,128)}, u32[]{:S(2)}) copy-start(s32[256,7]{0,1:T(8,128)} %param.11) | copy-start | bytes 21508
  22.5 4.1 %copy-start.8 = (f32[64,7,4]{0,2,1:T(4,128)S(1)}, f32[64,7,4]{0,2,1:T(4,128)}, u32[]{:S(2)}) copy-start(f32[64,7,4]{0,2,1:T(4,128)} %param.10) | copy-start | bytes 21508
  22.5 4.5 %copy-start = (bf16[256,512]{1,0:T(8,128)(2,1)S(1)}, bf16[256,512]{1,0:T(8,128)(2,1)}, u32[]{:S(2)}) copy-start(bf16[256,512]{1,0:T(8,128)(2,1)} %query_ref.7) | copy-start | bytes 786436
  22.5 4.5 %copy-start.1 = (bf16[256,512]{1,0:T(8,128)(2,1)S(1)}, bf16[256,512]{1,0:T(8,128)(2,1)}, u32[]{:S(2)}) copy-start(bf16[256,512]{1,0:T(8,128)(2,1)} %key_ref.5) | copy-start | bytes 786436
  22.5 4.5 %copy-start.2 = (bf16[256,512]{1,0:T(8,128)(2,1)S(1)}, bf16[256,512]{1,0:T(8,128)(2,1)}, u32[]{:S(2)}) copy-start(bf16[256,512]{1,0:T(8,128)(2,1)} %value_ref.5) | copy-start | bytes 786436
  22.5 21.8 %all-to-all-start.1 = ((bf16[32,80,128]{2,1,0:T(8,128)(2,1)}), bf16[32,80,128]{2,1,0:T(8,128)(2,1)S(1)}, u32[]{:S(2)}, u32[]{:S(2)}) async-start(bf16[32,80,128]{2,1,0:T(8,128)(2,1)} %shard_map.120), calls=%async_computation.1 | async-start | bytes 1310720 | tf_op jit(solution)/shard_map/all_to_all | solution.py:372
  45.2 25.4 %copy-start.5 = (bf16[16,8192]{1,0:T(8,128)(2,1)S(1)}, bf16[16,8192]{1,0:T(8,128)(2,1)}, u32[]{:S(2)}) copy-start(bf16[16,8192]{1,0:T(8,128)(2,1)} %cot_ref.1) | copy-start | bytes 786436
  45.2 25.4 %copy-start.7 = (f32[8192]{0:T(1024)S(1)}, f32[8192]{0:T(1024)}, u32[]{:S(2)}) copy-start(f32[8192]{0:T(1024)} %param.12) | copy-start | bytes 98308
  71.9 20.2 %all-to-all-start.3 = ((bf16[16,32,512]{2,1,0:T(8,128)(2,1)}), bf16[16,32,512]{2,1,0:T(8,128)(2,1)S(1)}, u32[]{:S(2)}, u32[]{:S(2)}) async-start(bf16[16,32,512]{2,1,0:T(8,128)(2,1)} %get-tuple-element.25), calls=%async_computation.3 | async-start | bytes 1048576 | tf_op jit(solution)/shard_map/all_to_all | solution.py:372
  93.9 0.7 copy-start.9
  94.6 0.7 copy-start.11
  95.3 20.6 %all-to-all-start.4 = ((bf16[32,56,128]{2,1,0:T(8,128)(2,1)}), bf16[32,56,128]{2,1,0:T(8,128)(2,1)S(1)}, u32[]{:S(2)}, u32[]{:S(2)}) async-start(bf16[32,56,128]{2,1,0:T(8,128)(2,1)} %get-tuple-element.27), calls=%async_computation.4 | async-start | bytes 917504 | tf_op jit(solution)/shard_map/all_to_all | solution.py:372
  104.6 0.8 copy-start.3
  115.9 5.7 %copy-start.12 = (bf16[512,128]{1,0:T(8,128)(2,1)S(1)}, bf16[512,128]{1,0:T(8,128)(2,1)}, u32[]{:S(2)}) copy-start(bf16[512,128]{1,0:T(8,128)(2,1)} %copy-done.11) | copy-start | bytes 393220
  115.9 7.0 %copy-start.10 = (bf16[512,128]{1,0:T(8,128)(2,1)S(1)}, bf16[512,128]{1,0:T(8,128)(2,1)}, u32[]{:S(2)}) copy-start(bf16[512,128]{1,0:T(8,128)(2,1)} %copy-done.9) | copy-start | bytes 393220
  116.7 19.8 %copy-start.4 = (f32[256,512]{1,0:T(8,128)S(1)}, f32[256,512]{1,0:T(8,128)}, u32[]{:S(2)}) copy-start(f32[256,512]{1,0:T(8,128)} %copy-done.3) | copy-start | bytes 1572868
  116.7 19.8 %all-to-all-start.5 = ((bf16[32,32,128]{2,1,0:T(8,128)(2,1)}), bf16[32,32,128]{2,1,0:T(8,128)(2,1)S(1)}, u32[]{:S(2)}, u32[]{:S(2)}) async-start(bf16[32,32,128]{2,1,0:T(8,128)(2,1)} %shard_map.125), calls=%async_computation.5 | async-start | bytes 524288 | tf_op jit(solution)/shard_map/all_to_all | solution.py:372
  121.6 8.2 %collective-permute-start = (bf16[512,128]{1,0:T(8,128)(2,1)S(1)}, bf16[512,128]{1,0:T(8,128)(2,1)S(1)}, u32[]{:S(2)}, u32[]{:S(2)}) collective-permute-start(bf16[512,128]{1,0:T(8,128)(2,1)S(1)} %copy-done.12), channel_id=1, source_target_pairs={{16,0},{32,16},{48,32},{80,64},{96,80},{112,96},{144,128},{160,144... | collective-permute-start | bytes 393224 | tf_op jit(solution)/shard_map/ppermute | solution.py:379
  122.9 9.6 %collective-permute-start.1 = (bf16[512,128]{1,0:T(8,128)(2,1)S(1)}, bf16[512,128]{1,0:T(8,128)(2,1)S(1)}, u32[]{:S(2)}, u32[]{:S(2)}) collective-permute-start(bf16[512,128]{1,0:T(8,128)(2,1)S(1)} %copy-done.10), channel_id=1, source_target_pairs={{32,0},{48,16},{96,64},{112,80},{160,128},{176,144},{224,192},{240... | collective-permute-start | bytes 393224 | tf_op jit(solution)/shard_map/ppermute | solution.py:379
  124.2 12.2 %collective-permute-start.2 = (bf16[512,128]{1,0:T(8,128)(2,1)S(1)}, bf16[512,128]{1,0:T(8,128)(2,1)S(1)}, u32[]{:S(2)}, u32[]{:S(2)}) collective-permute-start(bf16[512,128]{1,0:T(8,128)(2,1)S(1)} %copy-done.10), channel_id=1, source_target_pairs={{48,0},{112,64},{176,128},{240,192},{304,256},{368,320},{432,384},... | collective-permute-start | bytes 393224 | tf_op jit(solution)/shard_map/ppermute | solution.py:379

commit v9 on v8

--- a/solution.py
+++ b/solution.py
@@ -112,10 +112,6 @@
         interpret=INTERPRET,
         compiler_params=pltpu.CompilerParams(vmem_limit_bytes=16 * 1024 * 1024),
     )(in_hbm(key_rows), in_hbm(value_rows))
-
-
-def low_grad_kernel(one_ref, two_ref, three_ref, sum_ref):
-    sum_ref[...] = one_ref[...].astype(F32) + two_ref[...].astype(F32) + three_ref[...].astype(F32)
 
 
 def prefix_kernel(in_ref, out_ref):
@@ -333,7 +329,7 @@
 
 
 def final_kernel(
-    cross_ref, low_ref, inner_ref, key_ref, value_ref, dk_ref, dv_ref, grad_key_ref, grad_value_ref, table_ref, gain_ref
+    cross_ref, one_ref, two_ref, three_ref, inner_ref, key_ref, value_ref, dk_ref, dv_ref, grad_key_ref, grad_value_ref, table_ref, gain_ref
 ):
     heads = key_ref.shape[1] // CH
     spans = key_ref.shape[0] // CH
@@ -358,7 +354,8 @@
             table_ref[level] = total[top : top + heads, left : left + TABLE]
     for h in range(heads):
         cols = span_rows(h)
-        cross = get_slices(cross_ref, h, height).astype(F32) + low_ref[cols, :]
+        low = one_ref[cols, :].astype(F32) + two_ref[cols, :].astype(F32) + three_ref[cols, :].astype(F32)
+        cross = get_slices(cross_ref, h, height).astype(F32) + low
         for c in range(spans):
             rows = span_rows(c)
             state = (cross if c == 1 else inner_ref[cols, :] + cross).astype(BF16)
@@ -428,7 +425,6 @@
     )
     group_slices = exchange(groups, "seq")
     shifts = [row_shift(low_one if step == 1 else low_two, -step) for step in (1, 2, 3)]
-    low_sum = call(low_grad_kernel, shaped((width, CH), F32), *shifts)
     grad_query, near_dk, near_dv, inner, table_part = call(
         back_kernel,
         (
@@ -461,7 +457,7 @@
             shaped((columns * heads, CH), F32),
         ),
         cross,
-        low_sum,
+        *shifts,
         inner,
         key_rows,
         value_rows,

time: 138 us -> 138 us (level)
    pallas_call x10 -> x9, Pallas kernels: 13.1 us -> 13.1 us  [call(): pl.pallas_call(kernel, out_shape=out_shape, in_specs=[scalar if operand.n...]
where the time goes in v9:
time: 138 us; the launch traced here: 137 us
  waiting for transfers between devices  54.3 us (39%)
  blocking collectives  45 us (33%)
  starting transfers between devices  20.9 us (15%)
  Pallas kernels  14.4 us (10%)
  local copies, waits for them, and re-layouts  1.55 us (1%)
    all_to_all x2, blocking collectives, exchange(): return lax.all_to_all(value, axis, split_axis=0, concat_axis=0, tiled=True)  45 us
    all_to_all x4, waiting for transfers between devices, exchange(): return lax.all_to_all(value, axis, split_axis=0, concat_axis=0, tiled=True)  43.4 us
    all_to_all x4, starting transfers between devices, exchange(): return lax.all_to_all(value, axis, split_axis=0, concat_axis=0, tiled=True)  17 us
    pallas_call x9, Pallas kernels, call(): pl.pallas_call(kernel, out_shape=out_shape, in_specs=[scalar if operand.n...  13.1 us
    ppermute x3, waiting for transfers between devices, row_shift(): return lax.ppermute(value, 'seq', pairs)  10.9 us
    ppermute x3, starting transfers between devices, row_shift(): return lax.ppermute(value, 'seq', pairs)  3.88 us
  transfers between devices with their start and end apart: 7, of which 6 were waited for; matrix products, arithmetic and copies ran while one was open for 0% of the time, Pallas kernels for 5%

profile of v9, /device:TPU:1, one launch (start us, length us, event | category | flops | bytes accessed | tf_op | source)
XLA Modules:
  0.0 136.9 jit_solution(2139252656091766846)
XLA Ops:
  0.6 1.3 span_states.1
  1.9 19.6 %all_to_all.30.in_ref = bf16[32,16,128]{2,1,0:T(8,128)(2,1)S(1)} all-to-all(bf16[32,16,128]{2,1,0:T(8,128)(2,1)S(1)} %get-tuple-element.23), channel_id=1, replica_groups=mesh['seq'=32,'head'=16] {'seq'}, dimensions={0} | all-to-all | bytes 262144 | tf_op jit(solution)/shard_map/all_to_all | solution.py:369
  21.6 0.9 shard_map.120
  22.5 0.0 copy-start.6
  22.5 0.0 copy-start.8
  22.5 0.0 copy-start
  22.5 0.0 copy-start.1
  22.5 0.0 copy-start.2
  22.5 4.0 %all-to-all-start.1 = ((bf16[32,80,128]{2,1,0:T(8,128)(2,1)}), bf16[32,80,128]{2,1,0:T(8,128)(2,1)S(1)}, u32[]{:S(2)}, u32[]{:S(2)}) async-start(bf16[32,80,128]{2,1,0:T(8,128)(2,1)} %shard_map.120), calls=%async_computation.1 | async-start | bytes 1310720 | tf_op jit(solution)/shard_map/all_to_all | solution.py:369
  26.6 0.0 copy-done.6
  26.6 0.0 copy-done.8
  26.6 0.4 shard_map.118.weight_ref
  27.0 0.0 copy-done
  27.0 0.0 copy-done.1
  27.0 0.0 copy-done.2
  27.1 1.0 shard_map.119.near_ref
  28.1 16.2 %all-to-all-done.1.state_ref = bf16[32,80,128]{2,1,0:T(8,128)(2,1)S(1)} async-done(((bf16[32,80,128]{2,1,0:T(8,128)(2,1)}), bf16[32,80,128]{2,1,0:T(8,128)(2,1)S(1)}, u32[]{:S(2)}, u32[]{:S(2)}) %all-to-all-start.1) | async-done | bytes 655392 | tf_op jit(solution)/shard_map/all_to_all | solution.py:369
  44.3 0.9 shard_map.121
  45.2 0.0 copy-start.5
  45.2 0.0 copy-start.7
  45.2 25.3 %all_to_all.31.attn_ref = bf16[16,16,512]{2,1,0:T(8,128)(2,1)S(1)} all-to-all(bf16[16,16,512]{2,1,0:T(8,128)(2,1)S(1)} %bitcast.7), channel_id=1, replica_groups=mesh['seq'=32,'head'=16] {'head'}, dimensions={0} | all-to-all | bytes 524288 | tf_op jit(solution)/shard_map/all_to_all | solution.py:369
  70.5 0.0 copy-done.5
  70.5 0.0 copy-done.7
  70.5 1.3 shard_map.122
  71.9 3.5 %all-to-all-start.3 = ((bf16[16,32,512]{2,1,0:T(8,128)(2,1)}), bf16[16,32,512]{2,1,0:T(8,128)(2,1)S(1)}, u32[]{:S(2)}, u32[]{:S(2)}) async-start(bf16[16,32,512]{2,1,0:T(8,128)(2,1)} %get-tuple-element.25), calls=%async_computation.3 | async-start | bytes 1048576 | tf_op jit(solution)/shard_map/all_to_all | solution.py:369
  75.3 16.8 %all-to-all-done.3.head_ref = bf16[16,32,512]{2,1,0:T(8,128)(2,1)S(1)} async-done(((bf16[16,32,512]{2,1,0:T(8,128)(2,1)}), bf16[16,32,512]{2,1,0:T(8,128)(2,1)S(1)}, u32[]{:S(2)}, u32[]{:S(2)}) %all-to-all-start.3) | async-done | bytes 524320 | tf_op jit(solution)/shard_map/all_to_all | solution.py:369
  92.1 1.9 %shard_map.124 = (bf16[32,56,128]{2,1,0:T(8,128)(2,1)}, bf16[512,128]{1,0:T(8,128)(2,1)S(1)}, bf16[512,128]{1,0:T(8,128)(2,1)S(1)}) custom-call(s32[1]{0:T(128)} %bitcast.4.place_ref, bf16[16,32,512]{2,1,0:T(8,128)(2,1)S(1)} %all-to-all-done.3.head_ref, bf16[256,512]{1,0:T(8,128)(2,1)S(1)} %copy-done, f32[256,128]{1,0:T(8,128)S(1)} %shard_map.118.weight_ref), custom_call_target="tpu_custom_call" | custom-call | tf_op jit(solution)/shard_map/pallas_call | solution.py:25
  93.9 0.0 copy-start.9
  94.0 0.0 copy-start.11
  94.0 0.7 copy-done.9
  94.6 0.0 copy-done.11
  94.6 4.6 %all-to-all-start.4 = ((bf16[32,56,128]{2,1,0:T(8,128)(2,1)}), bf16[32,56,128]{2,1,0:T(8,128)(2,1)S(1)}, u32[]{:S(2)}, u32[]{:S(2)}) async-start(bf16[32,56,128]{2,1,0:T(8,128)(2,1)} %get-tuple-element.27), calls=%async_computation.4 | async-start | bytes 917504 | tf_op jit(solution)/shard_map/all_to_all | solution.py:369
  99.3 4.7 %shard_map.123 = (bf16[256,512]{1,0:T(8,128)(2,1)}, f32[256,512]{1,0:T(8,128)S(1)}, f32[256,512]{1,0:T(8,128)S(1)}, f32[512,128]{1,0:T(8,128)S(1)}, bf16[14,128]{1,0:T(8,128)(2,1)S(1)}) custom-call(bf16[256,512]{1,0:T(8,128)(2,1)S(1)} %copy-done, bf16[256,512]{1,0:T(8,128)(2,1)S(1)} %copy-done.1, bf16[256,512]{1,0:T(8,128)(2,1)S(1)} %copy-done.2, ...), custom_call_target="tpu_custom_call" | custom-call | tf_op jit(solution)/shard_map/pallas_call | solution.py:25
  104.0 0.8 copy-done.3
  104.8 10.4 %all-to-all-done.4.in_ref = bf16[32,56,128]{2,1,0:T(8,128)(2,1)S(1)} async-done(((bf16[32,56,128]{2,1,0:T(8,128)(2,1)}), bf16[32,56,128]{2,1,0:T(8,128)(2,1)S(1)}, u32[]{:S(2)}, u32[]{:S(2)}) %all-to-all-start.4) | async-done | bytes 458784 | tf_op jit(solution)/shard_map/all_to_all | solution.py:369
  115.3 0.8 shard_map.125
  116.1 4.9 %all-to-all-start.5 = ((bf16[32,32,128]{2,1,0:T(8,128)(2,1)}), bf16[32,32,128]{2,1,0:T(8,128)(2,1)S(1)}, u32[]{:S(2)}, u32[]{:S(2)}) async-start(bf16[32,32,128]{2,1,0:T(8,128)(2,1)} %shard_map.125), calls=%async_computation.5 | async-start | bytes 524288 | tf_op jit(solution)/shard_map/all_to_all | solution.py:369
  120.9 0.0 copy-done.12
  120.9 1.3 collective-permute-start
  122.2 0.0 copy-done.10
  122.2 1.3 collective-permute-start.1
  123.5 1.3 collective-permute-start.2
  124.8 4.3 %collective-permute-done.one_ref = bf16[512,128]{1,0:T(8,128)(2,1)S(1)} collective-permute-done((bf16[512,128]{1,0:T(8,128)(2,1)S(1)}, bf16[512,128]{1,0:T(8,128)(2,1)S(1)}, u32[]{:S(2)}, u32[]{:S(2)}) %collective-permute-start) | collective-permute-done | bytes 131104 | tf_op jit(solution)/shard_map/ppermute | solution.py:376
  129.1 2.7 %collective-permute-done.1.two_ref = bf16[512,128]{1,0:T(8,128)(2,1)S(1)} collective-permute-done((bf16[512,128]{1,0:T(8,128)(2,1)S(1)}, bf16[512,128]{1,0:T(8,128)(2,1)S(1)}, u32[]{:S(2)}, u32[]{:S(2)}) %collective-permute-start.1) | collective-permute-done | bytes 131104 | tf_op jit(solution)/shard_map/ppermute | solution.py:376
  131.8 3.9 %collective-permute-done.2.three_ref = bf16[512,128]{1,0:T(8,128)(2,1)S(1)} collective-permute-done((bf16[512,128]{1,0:T(8,128)(2,1)S(1)}, bf16[512,128]{1,0:T(8,128)(2,1)S(1)}, u32[]{:S(2)}, u32[]{:S(2)}) %collective-permute-start.2) | collective-permute-done | bytes 131104 | tf_op jit(solution)/shard_map/ppermute | solution.py:376
  135.8 0.0 all-to-all-done.5.cross_ref
  135.8 0.0 copy-done.4
  135.8 1.2 shard_map.126
  (4 shorter events, 0.0 us)
Async XLA Ops:
  22.5 4.1 %copy-start.6 = (s32[256,7]{0,1:T(8,128)S(1)}, s32[256,7]{0,1:T(8,128)}, u32[]{:S(2)}) copy-start(s32[256,7]{0,1:T(8,128)} %param.11) | copy-start | bytes 21508
  22.5 4.1 %copy-start.8 = (f32[64,7,4]{0,2,1:T(4,128)S(1)}, f32[64,7,4]{0,2,1:T(4,128)}, u32[]{:S(2)}) copy-start(f32[64,7,4]{0,2,1:T(4,128)} %param.10) | copy-start | bytes 21508
  22.5 4.5 %copy-start = (bf16[256,512]{1,0:T(8,128)(2,1)S(1)}, bf16[256,512]{1,0:T(8,128)(2,1)}, u32[]{:S(2)}) copy-start(bf16[256,512]{1,0:T(8,128)(2,1)} %query_ref.7) | copy-start | bytes 786436
  22.5 4.5 %copy-start.1 = (bf16[256,512]{1,0:T(8,128)(2,1)S(1)}, bf16[256,512]{1,0:T(8,128)(2,1)}, u32[]{:S(2)}) copy-start(bf16[256,512]{1,0:T(8,128)(2,1)} %key_ref.5) | copy-start | bytes 786436
  22.5 4.5 %copy-start.2 = (bf16[256,512]{1,0:T(8,128)(2,1)S(1)}, bf16[256,512]{1,0:T(8,128)(2,1)}, u32[]{:S(2)}) copy-start(bf16[256,512]{1,0:T(8,128)(2,1)} %value_ref.5) | copy-start | bytes 786436
  22.5 21.8 %all-to-all-start.1 = ((bf16[32,80,128]{2,1,0:T(8,128)(2,1)}), bf16[32,80,128]{2,1,0:T(8,128)(2,1)S(1)}, u32[]{:S(2)}, u32[]{:S(2)}) async-start(bf16[32,80,128]{2,1,0:T(8,128)(2,1)} %shard_map.120), calls=%async_computation.1 | async-start | bytes 1310720 | tf_op jit(solution)/shard_map/all_to_all | solution.py:369
  45.2 25.4 %copy-start.5 = (bf16[16,8192]{1,0:T(8,128)(2,1)S(1)}, bf16[16,8192]{1,0:T(8,128)(2,1)}, u32[]{:S(2)}) copy-start(bf16[16,8192]{1,0:T(8,128)(2,1)} %cot_ref.1) | copy-start | bytes 786436
  45.2 25.4 %copy-start.7 = (f32[8192]{0:T(1024)S(1)}, f32[8192]{0:T(1024)}, u32[]{:S(2)}) copy-start(f32[8192]{0:T(1024)} %param.12) | copy-start | bytes 98308
  71.9 20.2 %all-to-all-start.3 = ((bf16[16,32,512]{2,1,0:T(8,128)(2,1)}), bf16[16,32,512]{2,1,0:T(8,128)(2,1)S(1)}, u32[]{:S(2)}, u32[]{:S(2)}) async-start(bf16[16,32,512]{2,1,0:T(8,128)(2,1)} %get-tuple-element.25), calls=%async_computation.3 | async-start | bytes 1048576 | tf_op jit(solution)/shard_map/all_to_all | solution.py:369
  93.9 0.7 copy-start.9
  94.0 0.7 copy-start.11
  94.6 20.6 %all-to-all-start.4 = ((bf16[32,56,128]{2,1,0:T(8,128)(2,1)}), bf16[32,56,128]{2,1,0:T(8,128)(2,1)S(1)}, u32[]{:S(2)}, u32[]{:S(2)}) async-start(bf16[32,56,128]{2,1,0:T(8,128)(2,1)} %get-tuple-element.27), calls=%async_computation.4 | async-start | bytes 917504 | tf_op jit(solution)/shard_map/all_to_all | solution.py:369
  104.0 0.8 copy-start.3
  115.3 20.5 %copy-start.4 = (f32[256,512]{1,0:T(8,128)S(1)}, f32[256,512]{1,0:T(8,128)}, u32[]{:S(2)}) copy-start(f32[256,512]{1,0:T(8,128)} %copy-done.3) | copy-start | bytes 1572868
  116.1 4.9 %copy-start.12 = (bf16[512,128]{1,0:T(8,128)(2,1)S(1)}, bf16[512,128]{1,0:T(8,128)(2,1)}, u32[]{:S(2)}) copy-start(bf16[512,128]{1,0:T(8,128)(2,1)} %copy-done.11) | copy-start | bytes 393220
  116.1 6.2 %copy-start.10 = (bf16[512,128]{1,0:T(8,128)(2,1)S(1)}, bf16[512,128]{1,0:T(8,128)(2,1)}, u32[]{:S(2)}) copy-start(bf16[512,128]{1,0:T(8,128)(2,1)} %copy-done.9) | copy-start | bytes 393220
  116.1 19.7 %all-to-all-start.5 = ((bf16[32,32,128]{2,1,0:T(8,128)(2,1)}), bf16[32,32,128]{2,1,0:T(8,128)(2,1)S(1)}, u32[]{:S(2)}, u32[]{:S(2)}) async-start(bf16[32,32,128]{2,1,0:T(8,128)(2,1)} %shard_map.125), calls=%async_computation.5 | async-start | bytes 524288 | tf_op jit(solution)/shard_map/all_to_all | solution.py:369
  120.9 8.2 %collective-permute-start = (bf16[512,128]{1,0:T(8,128)(2,1)S(1)}, bf16[512,128]{1,0:T(8,128)(2,1)S(1)}, u32[]{:S(2)}, u32[]{:S(2)}) collective-permute-start(bf16[512,128]{1,0:T(8,128)(2,1)S(1)} %copy-done.12), channel_id=1, source_target_pairs={{16,0},{32,16},{48,32},{80,64},{96,80},{112,96},{144,128},{160,144... | collective-permute-start | bytes 393224 | tf_op jit(solution)/shard_map/ppermute | solution.py:376
  122.2 9.6 %collective-permute-start.1 = (bf16[512,128]{1,0:T(8,128)(2,1)S(1)}, bf16[512,128]{1,0:T(8,128)(2,1)S(1)}, u32[]{:S(2)}, u32[]{:S(2)}) collective-permute-start(bf16[512,128]{1,0:T(8,128)(2,1)S(1)} %copy-done.10), channel_id=1, source_target_pairs={{32,0},{48,16},{96,64},{112,80},{160,128},{176,144},{224,192},{240... | collective-permute-start | bytes 393224 | tf_op jit(solution)/shard_map/ppermute | solution.py:376
  123.5 12.2 %collective-permute-start.2 = (bf16[512,128]{1,0:T(8,128)(2,1)S(1)}, bf16[512,128]{1,0:T(8,128)(2,1)S(1)}, u32[]{:S(2)}, u32[]{:S(2)}) collective-permute-start(bf16[512,128]{1,0:T(8,128)(2,1)S(1)} %copy-done.10), channel_id=1, source_target_pairs={{48,0},{112,64},{176,128},{240,192},{304,256},{368,320},{432,384},... | collective-permute-start | bytes 393224 | tf_op jit(solution)/shard_map/ppermute | solution.py:376
